TPU v7x, 32 devices: a whole 2x2x4 slice. The times are simulated.
32 devices in a mesh: dp: 32 (over z, y, x, core).
Axes of the slice: x: 2, y: 2, z: 4, core: 2. Of those that a mesh axis runs over, the one named last changes fastest.
Arguments:
- tokens: bfloat16 [4096, 2048], P('dp'), may hold values from -6 to 6
- cotangent: bfloat16 [4096, 2048], P('dp'), may hold values from -6 to 6
- lengths: int32 [32], replicated, may hold values from 1 to 160, 4096 in all
- wq: bfloat16 [2048, 2048], P('dp'), may hold values from -0.125 to 0.125
- bq: bfloat16 [2048], P('dp'), may hold values from -3 to 3
- wk: bfloat16 [2048, 2048], P('dp'), may hold values from -0.125 to 0.125
- wv: bfloat16 [2048, 2048], P('dp'), may hold values from -0.125 to 0.125
- bv: bfloat16 [2048], P('dp'), may hold values from -3 to 3
- wo: bfloat16 [2048, 2048], P('dp'), may hold values from -0.5 to 0.5
- bo: bfloat16 [2048], P('dp'), may hold values from -3 to 3
- norm1_gain: bfloat16 [2048], P('dp'), may hold values from 0.5 to 1.5
- norm1_bias: bfloat16 [2048], P('dp'), may hold values from -2 to 2
- w1: bfloat16 [2048, 8192], P('dp'), may hold values from -0.125 to 0.125
- b1: bfloat16 [8192], P('dp'), may hold values from -3 to 3
- w2: bfloat16 [8192, 2048], P('dp'), may hold values from -0.0625 to 0.0625
- b2: bfloat16 [2048], P('dp'), may hold values from -3 to 3
- norm2_gain: bfloat16 [2048], P('dp'), may hold values from 0.5 to 1.5
- norm2_bias: bfloat16 [2048], P('dp'), may hold values from -2 to 2
Outputs:
- output: bfloat16 [4096, 2048], P('dp')
- input_grad: bfloat16 [4096, 2048], P('dp')
- grad_wq: float32 [2048, 2048], P('dp')
- grad_bq: float32 [2048], P('dp')
- grad_wk: float32 [2048, 2048], P('dp')
- grad_wv: float32 [2048, 2048], P('dp')
- grad_bv: float32 [2048], P('dp')
- grad_wo: float32 [2048, 2048], P('dp')
- grad_bo: float32 [2048], P('dp')
- grad_norm1_gain: float32 [2048], P('dp')
- grad_norm1_bias: float32 [2048], P('dp')
- grad_w1: float32 [2048, 8192], P('dp')
- grad_b1: float32 [8192], P('dp')
- grad_w2: float32 [8192, 2048], P('dp')
- grad_b2: float32 [2048], P('dp')
- grad_norm2_gain: float32 [2048], P('dp')
- grad_norm2_bias: float32 [2048], P('dp')
Inputs may be any that keep to these rules, and one draw needn't show every extreme that they name: The lengths sum to 4096; the longest is exactly 160.
All inputs are finite; a program needn't handle non-finite values.
Results may differ from a plain program's by a relative error of at most 0.015.
Values may be sent and summed in bfloat16 or wider, within the bound.
A program may use at most 448 MiB of HBM per device.

v0:
```python
import jax
import jax.numpy as jnp
from jax import lax
from jax.sharding import PartitionSpec as P

HEADS = 16
HEAD_DIM = 128
SEQ_MAX = 160
SPAN = 3


norm_eps = 1e-05


def layer_norm(residual, gain_vec, shift_vec):
    mean_val = jnp.mean(residual, axis=-1, keepdims=True)
    centred = residual - mean_val
    var_val = jnp.mean(centred * centred, axis=-1, keepdims=True)
    return centred * lax.rsqrt(var_val + norm_eps) * gain_vec + shift_vec


def gelu_tanh(values):
    return jax.nn.gelu(values, approximate=True)


def plan_layout(lengths, tok_dev):
    starts = jnp.cumsum(lengths) - lengths
    owner_first = starts // tok_dev
    return (starts, starts, lengths, owner_first)


def to_owners(shard, layout, dev_count, piece_rows):
    starts, owner_start, owner_length, owner_first = layout
    tok_dev = shard.shape[0]
    feat_width = shard.shape[1]
    device = lax.axis_index("dp")
    held_rows = lax.all_to_all(
        shard.reshape(dev_count, piece_rows, feat_width),
        "dp",
        split_axis=0,
        concat_axis=0,
        tiled=True,
    )
    held_rows = held_rows.reshape(dev_count * piece_rows, feat_width)
    slot_ids = jnp.arange(SPAN * piece_rows, dtype=jnp.int32)
    shard_step = slot_ids // piece_rows
    within = slot_ids % piece_rows
    source = owner_first[:, None] + shard_step[None, :]
    global_row = source * tok_dev + device * piece_rows + within[None, :]
    inside = (
        (global_row >= owner_start[:, None])
        & (global_row < (owner_start + owner_length)[:, None])
        & (source < dev_count)
    )
    picked = held_rows[jnp.clip(source, 0, dev_count - 1) * piece_rows + within[None, :]]
    outgoing = jnp.where(inside[:, :, None], picked, jnp.zeros((), picked.dtype))
    arrived = lax.all_to_all(outgoing, "dp", split_axis=0, concat_axis=0, tiled=True)
    arrived = arrived.reshape(dev_count * SPAN * piece_rows, feat_width)
    my_start = owner_start[device]
    my_length = owner_length[device]
    my_first = owner_first[device]
    places = jnp.arange(SEQ_MAX, dtype=jnp.int32)
    global_pos = my_start + places
    shard_of = global_pos // tok_dev
    offset_in = global_pos % tok_dev
    slot_index = (
        offset_in // piece_rows * (SPAN * piece_rows)
        + (shard_of - my_first) * piece_rows
        + offset_in % piece_rows
    )
    valid_rows = places < my_length
    slot_index = jnp.where(valid_rows, slot_index, 0)
    owned = jnp.where(valid_rows[:, None], arrived[slot_index], jnp.zeros((), arrived.dtype))
    return (owned, valid_rows)


def to_order(owned, layout, dev_count, piece_rows, tok_dev):
    starts, owner_start, owner_length, owner_first = layout
    feat_width = owned.shape[1]
    device = lax.axis_index("dp")
    my_start = owner_start[device]
    my_length = owner_length[device]
    my_first = owner_first[device]
    slot_ids = jnp.arange(SPAN * piece_rows, dtype=jnp.int32)
    shard_step = slot_ids // piece_rows
    within = slot_ids % piece_rows
    targets = jnp.arange(dev_count, dtype=jnp.int32)
    global_row = (
        (my_first + shard_step)[None, :] * tok_dev + targets[:, None] * piece_rows + within[None, :]
    )
    place_row = global_row - my_start
    inside = (place_row >= 0) & (place_row < my_length)
    picked = owned[jnp.clip(place_row, 0, owned.shape[0] - 1)]
    outgoing = jnp.where(inside[:, :, None], picked, jnp.zeros((), picked.dtype))
    returned = lax.all_to_all(outgoing, "dp", split_axis=0, concat_axis=0, tiled=True)
    returned = returned.reshape(dev_count * SPAN * piece_rows, feat_width)
    sources = jnp.arange(dev_count, dtype=jnp.int32)
    within_piece = jnp.arange(piece_rows, dtype=jnp.int32)
    row_ids = sources[:, None] * tok_dev + device * piece_rows + within_piece[None, :]
    seq_of = jnp.sum((row_ids[:, :, None] >= starts[None, None, :]).astype(jnp.int32), 2) - 1
    slot_index = (
        seq_of * (SPAN * piece_rows)
        + (sources[:, None] - owner_first[seq_of]) * piece_rows
        + within_piece[None, :]
    )
    pieces = returned[slot_index]
    ordered = lax.all_to_all(pieces, "dp", split_axis=0, concat_axis=0, tiled=True)
    return ordered.reshape(tok_dev, feat_width)


def per_device(
    tokens,
    cotangent,
    lengths,
    wq,
    bq,
    wk,
    wv,
    bv,
    wo,
    bo,
    norm1_gain,
    norm1_bias,
    w1,
    b1,
    w2,
    b2,
    norm2_gain,
    norm2_bias,
):
    f32 = jnp.float32
    bf16 = jnp.bfloat16
    dev_count = lax.axis_size("dp")
    tok_dev = tokens.shape[0]
    feat_width = tokens.shape[1]
    piece_rows = tok_dev // dev_count
    layout = plan_layout(lengths, tok_dev)
    joined, valid_rows = to_owners(
        jnp.concatenate([tokens, cotangent], 1), layout, dev_count, piece_rows
    )
    inputs = joined[:, :feat_width]
    upstream = joined[:, feat_width:].astype(f32)
    slot_count = inputs.shape[0]
    score_scale = HEAD_DIM ** (-0.5)
    full_wq, full_wk, full_wv, full_wo, full_bq, full_bv, full_bo, gain_one, shift_one = (
        lax.all_gather(wq, "dp", axis=0, tiled=True),
        lax.all_gather(wk, "dp", axis=0, tiled=True),
        lax.all_gather(wv, "dp", axis=0, tiled=True),
        lax.all_gather(wo, "dp", axis=0, tiled=True),
        lax.all_gather(bq, "dp", axis=0, tiled=True),
        lax.all_gather(bv, "dp", axis=0, tiled=True),
        lax.all_gather(bo, "dp", axis=0, tiled=True),
        lax.all_gather(norm1_gain, "dp", axis=0, tiled=True),
        lax.all_gather(norm1_bias, "dp", axis=0, tiled=True),
    )
    queries = (
        (jnp.dot(inputs, full_wq, preferred_element_type=f32) + full_bq.astype(f32))
        .astype(bf16)
        .reshape(slot_count, HEADS, HEAD_DIM)
    )
    keys_low = (
        jnp.dot(inputs, full_wk, preferred_element_type=f32)
        .astype(bf16)
        .reshape(slot_count, HEADS, HEAD_DIM)
    )
    values_low = (
        (jnp.dot(inputs, full_wv, preferred_element_type=f32) + full_bv.astype(f32))
        .astype(bf16)
        .reshape(slot_count, HEADS, HEAD_DIM)
    )
    scores = jnp.einsum("qhd,khd->hqk", queries, keys_low, preferred_element_type=f32) * score_scale
    scores = jnp.where(valid_rows[None, None, :], scores, -1e30)
    row_max = jnp.max(scores, -1, keepdims=True)
    row_total = jnp.sum(jnp.exp(scores - row_max), -1, keepdims=True)
    log_total = row_max + jnp.log(row_total)
    attn_probs = jnp.exp(scores - log_total).astype(bf16)
    attended = jnp.einsum("hqk,khd->qhd", attn_probs, values_low, preferred_element_type=f32)
    attended = attended.reshape(slot_count, feat_width).astype(bf16)
    branch = jnp.dot(attended, full_wo, preferred_element_type=f32) + full_bo.astype(f32)
    resid_one = inputs.astype(f32) + branch
    hidden, norm_one_back = jax.vjp(
        layer_norm, resid_one, gain_one.astype(f32), shift_one.astype(f32)
    )
    hidden_low = hidden.astype(bf16)
    full_w1, full_w2, full_b1, full_b2, gain_two, shift_two = (
        lax.all_gather(w1, "dp", axis=0, tiled=True),
        lax.all_gather(w2, "dp", axis=0, tiled=True),
        lax.all_gather(b1, "dp", axis=0, tiled=True),
        lax.all_gather(b2, "dp", axis=0, tiled=True),
        lax.all_gather(norm2_gain, "dp", axis=0, tiled=True),
        lax.all_gather(norm2_bias, "dp", axis=0, tiled=True),
    )
    upward = jnp.dot(hidden_low, full_w1, preferred_element_type=f32) + full_b1.astype(f32)
    activ, gelu_back = jax.vjp(gelu_tanh, upward)
    activ_low = activ.astype(bf16)
    mixed = jnp.dot(activ_low, full_w2, preferred_element_type=f32) + full_b2.astype(f32)
    resid_two = hidden + mixed
    normed, norm_two_back = jax.vjp(
        layer_norm, resid_two, gain_two.astype(f32), shift_two.astype(f32)
    )
    result = jnp.where(valid_rows[:, None], normed, 0.0).astype(bf16)
    output = to_order(result, layout, dev_count, piece_rows, tok_dev)
    back_w1, back_w2 = (
        lax.all_gather(w1, "dp", axis=0, tiled=True),
        lax.all_gather(w2, "dp", axis=0, tiled=True),
    )
    grad_resid_two, grad_gain_two, grad_shift_two = norm_two_back(upstream)
    grad_mixed = grad_resid_two.astype(bf16)
    grad_bias_two = jnp.sum(grad_mixed.astype(f32), 0)
    grad_activ = jnp.einsum("td,fd->tf", grad_mixed, back_w2, preferred_element_type=f32)
    grad_upward = gelu_back(grad_activ)[0].astype(bf16)
    grad_bias_one = jnp.sum(grad_upward.astype(f32), 0)
    grad_hidden = grad_resid_two + jnp.einsum(
        "tf,df->td", grad_upward, back_w1, preferred_element_type=f32
    )
    grad_w2 = jnp.einsum("tf,td->fd", activ_low, grad_mixed, preferred_element_type=f32)
    grad_w1 = jnp.einsum("td,tf->df", hidden_low, grad_upward, preferred_element_type=f32)
    mlp_grads = (
        lax.psum_scatter(grad_w1, "dp", scatter_dimension=0, tiled=True),
        lax.psum_scatter(grad_w2, "dp", scatter_dimension=0, tiled=True),
        lax.psum_scatter(grad_bias_one, "dp", scatter_dimension=0, tiled=True),
        lax.psum_scatter(grad_bias_two, "dp", scatter_dimension=0, tiled=True),
        lax.psum_scatter(grad_gain_two, "dp", scatter_dimension=0, tiled=True),
        lax.psum_scatter(grad_shift_two, "dp", scatter_dimension=0, tiled=True),
    )
    back_wq, back_wk, back_wv, back_wo = (
        lax.all_gather(wq, "dp", axis=0, tiled=True),
        lax.all_gather(wk, "dp", axis=0, tiled=True),
        lax.all_gather(wv, "dp", axis=0, tiled=True),
        lax.all_gather(wo, "dp", axis=0, tiled=True),
    )
    grad_resid_one, grad_gain_one, grad_shift_one = norm_one_back(grad_hidden)
    grad_branch = grad_resid_one.astype(bf16)
    grad_bo = jnp.sum(grad_branch.astype(f32), 0)
    grad_wo = jnp.einsum("tc,td->cd", attended, grad_branch, preferred_element_type=f32)
    grad_attended = jnp.einsum(
        "td,cd->tc", grad_branch, back_wo, preferred_element_type=f32
    ).astype(bf16)
    grad_attended = grad_attended.reshape(slot_count, HEADS, HEAD_DIM)
    re_scores = (
        jnp.einsum("qhd,khd->hqk", queries, keys_low, preferred_element_type=f32) * score_scale
    )
    re_scores = jnp.where(valid_rows[None, None, :], re_scores, -1e30)
    re_probs = jnp.exp(re_scores - log_total)
    re_probs_low = re_probs.astype(bf16)
    grad_values = jnp.einsum(
        "hqk,qhd->khd", re_probs_low, grad_attended, preferred_element_type=f32
    ).astype(bf16)
    grad_probs = jnp.einsum("qhd,khd->hqk", grad_attended, values_low, preferred_element_type=f32)
    grad_scores = re_probs * (grad_probs - jnp.sum(re_probs * grad_probs, -1, keepdims=True))
    grad_scores_low = grad_scores.astype(bf16)
    grad_queries = (
        jnp.einsum("hqk,khd->qhd", grad_scores_low, keys_low, preferred_element_type=f32)
        * score_scale
    ).astype(bf16)
    grad_keys = (
        jnp.einsum("hqk,qhd->khd", grad_scores_low, queries, preferred_element_type=f32)
        * score_scale
    ).astype(bf16)
    grad_queries = grad_queries.reshape(slot_count, feat_width)
    grad_keys = grad_keys.reshape(slot_count, feat_width)
    grad_values = grad_values.reshape(slot_count, feat_width)
    grad_bq = jnp.sum(grad_queries.astype(f32), 0)
    grad_bv = jnp.sum(grad_values.astype(f32), 0)
    grad_wq = jnp.einsum("tc,td->cd", inputs, grad_queries, preferred_element_type=f32)
    grad_wk = jnp.einsum("tc,td->cd", inputs, grad_keys, preferred_element_type=f32)
    grad_wv = jnp.einsum("tc,td->cd", inputs, grad_values, preferred_element_type=f32)
    grad_input = grad_resid_one + jnp.einsum(
        "td,cd->tc", grad_queries, back_wq, preferred_element_type=f32
    )
    grad_input = grad_input + jnp.einsum(
        "td,cd->tc", grad_keys, back_wk, preferred_element_type=f32
    )
    grad_input = grad_input + jnp.einsum(
        "td,cd->tc", grad_values, back_wv, preferred_element_type=f32
    )
    grad_input = jnp.where(valid_rows[:, None], grad_input, 0.0).astype(bf16)
    attn_grads = (
        lax.psum_scatter(grad_wq, "dp", scatter_dimension=0, tiled=True),
        lax.psum_scatter(grad_wk, "dp", scatter_dimension=0, tiled=True),
        lax.psum_scatter(grad_wv, "dp", scatter_dimension=0, tiled=True),
        lax.psum_scatter(grad_wo, "dp", scatter_dimension=0, tiled=True),
        lax.psum_scatter(grad_bq, "dp", scatter_dimension=0, tiled=True),
        lax.psum_scatter(grad_bv, "dp", scatter_dimension=0, tiled=True),
        lax.psum_scatter(grad_bo, "dp", scatter_dimension=0, tiled=True),
        lax.psum_scatter(grad_gain_one, "dp", scatter_dimension=0, tiled=True),
        lax.psum_scatter(grad_shift_one, "dp", scatter_dimension=0, tiled=True),
    )
    sum_w1, sum_w2, sum_b1, sum_b2, sum_g2, sum_s2 = mlp_grads
    sum_wq, sum_wk, sum_wv, sum_wo, sum_bq, sum_bv, sum_bo, sum_g1, sum_s1 = attn_grads
    input_grad = to_order(grad_input, layout, dev_count, piece_rows, tok_dev)
    return (
        output,
        input_grad,
        sum_wq,
        sum_bq,
        sum_wk,
        sum_wv,
        sum_bv,
        sum_wo,
        sum_bo,
        sum_g1,
        sum_s1,
        sum_w1,
        sum_b1,
        sum_w2,
        sum_b2,
        sum_g2,
        sum_s2,
    )


def solution(mesh):
    in_specs = (
        P("dp", None),
        P("dp", None),
        P(),
        P("dp", None),
        P("dp"),
        P("dp", None),
        P("dp", None),
        P("dp"),
        P("dp", None),
        P("dp"),
        P("dp"),
        P("dp"),
        P("dp", None),
        P("dp"),
        P("dp", None),
        P("dp"),
        P("dp"),
        P("dp"),
    )
    out_specs = (
        P("dp", None),
        P("dp", None),
        P("dp", None),
        P("dp"),
        P("dp", None),
        P("dp", None),
        P("dp"),
        P("dp", None),
        P("dp"),
        P("dp"),
        P("dp"),
        P("dp", None),
        P("dp"),
        P("dp", None),
        P("dp"),
        P("dp"),
        P("dp"),
    )
    return jax.shard_map(
        per_device, mesh=mesh, in_specs=in_specs, out_specs=out_specs, check_vma=False
    )
```

profile of v0, /device:TPU:7, one launch (start us, length us, event | category | flops | bytes accessed | tf_op | source)
XLA Modules:
  0.0 3216.7 jit_solution(6134563321470671264)
XLA Ops:
  12.5 6.4 all-to-all-start
  21.6 2.0 fusion.80
  23.7 1.3 compare_select_fusion
  25.1 30.5 all-to-all-done
  56.0 4.0 gather_fusion
  60.0 5.5 reshape.775
  65.5 4.9 broadcast_select_fusion
  70.5 5.3 all-to-all-start.1
  77.9 158.8 %all-reduce.18 = (bf16[2048]{0:T(1024)(128)(2,1)S(1)}, bf16[2048]{0:T(1024)(128)(2,1)S(1)}, bf16[2048]{0:T(1024)(128)(2,1)S(1)}, bf16[2048]{0:T(1024)(128)(2,1)S...) all-reduce(bf16[2048]{0:T(1024)(128)(2,1)S(1)} %dynamic-update-slic, ...), channel_id=1, replica_groups=mesh['dp'=32] {'dp'}, use_global_device_ids=true, to_apply=%add.2 | all-reduce | flops 16384 | bytes 65536
  236.8 34.6 %all-gather = bf16[32,1,256]{2,1,0:T(2,128)(2,1)S(1)} all-gather(bf16[1,1,256]{2,1,0:T(2,128)(2,1)S(1)} %reshape.853), channel_id=1, replica_groups=mesh['dp'=32] {'dp'}, dimensions={0}, use_global_device_ids=true | all-gather | bytes 16896 | tf_op jit(solution)/shard_map/all_gather | solution.py:188
  272.1 2.0 compare_select_fusion.2
  274.1 4.6 reshape.762
  278.7 2.4 gather_fusion.1
  281.2 1.5 broadcast_select_fusion.3
  282.7 6.2 fusion.25
  288.9 5.2 fusion.22
  295.5 7.6 all-gather.8.cloned.1.call-done
  303.1 5.1 fusion.23
  310.1 71.8 %all-gather.14.cloned.1.call-done = bf16[2048,2048]{1,0:T(8,128)(2,1)} async-done(((bf16[64,2048]{1,0:T(8,128)(2,1)}), bf16[2048,2048]{1,0:T(8,128)(2,1)}) %all-gather.14.cloned.1.call-update) | async-done | bytes 8388624 | tf_op jit(solution)/shard_map/all_gather | solution.py:149
  381.9 5.1 fusion.95
  387.4 190.6 %all-gather.16.cloned.1.call-done = bf16[2048,8192]{1,0:T(8,128)(2,1)} async-done(((bf16[64,8192]{1,0:T(8,128)(2,1)}), bf16[2048,8192]{1,0:T(8,128)(2,1)}) %all-gather.16.cloned.1.call-update) | async-done | bytes 33554448 | tf_op jit(solution)/shard_map/all_gather | solution.py:186
  578.0 16.7 convolution_add_fusion
  594.7 179.0 %all-gather.18.cloned.1.call-done = bf16[8192,2048]{1,0:T(8,128)(2,1)} async-done(((bf16[256,2048]{1,0:T(8,128)(2,1)}), bf16[8192,2048]{1,0:T(8,128)(2,1)}) %all-gather.18.cloned.1.call-update) | async-done | bytes 33554448 | tf_op jit(solution)/shard_map/all_gather | solution.py:187
  773.7 19.5 fusion.96
  793.2 1.7 multiply_reduce_fusion.3
  796.1 1.6 fusion.94
  799.6 20.6 convert_reduce_fusion
  820.2 20.4 multiply_reduce_fusion.1
  840.6 1.8 fusion.93
  843.5 6.4 fusion.26
  849.9 2.3 convert_reduce_fusion.4
  855.1 2.2 convert_reduce_fusion.5
  857.4 9.2 fusion.28
  866.9 2.0 fusion.21
  869.7 8.1 fusion.31
  877.9 9.2 fusion.34
  888.2 8.1 fusion.37
  897.5 25.8 fusion.91
  923.6 25.0 fusion.88
  950.1 6.3 convolution_add_fusion.5
  956.5 6.4 convolution_add_fusion.4
  962.9 6.3 fusion.12
  969.2 2.5 gather_fusion.5
  971.6 1.6 reshape.815
  973.2 2.4 gather_fusion.2
  975.7 1.5 reshape.791
  977.2 3.9 broadcast_select_fusion.1
  981.2 73.9 %all_to_all.30 = bf16[32,12,2048]{2,1,0:T(8,128)(2,1)} all-to-all(bf16[32,12,2048]{2,1,0:T(8,128)(2,1)S(1)} %get-tuple-element.53), channel_id=1, replica_groups=mesh['dp'=32] {'dp'}, dimensions={0} | all-to-all | bytes 3145728 | tf_op jit(solution)/shard_map/all_to_all | solution.py:95
  1055.1 4.6 all-to-all-start.2
  1061.8 2.5 reshape.772
  1066.3 61.6 %all-to-all-done.2 = bf16[32,12,2048]{2,1,0:T(8,128)(2,1)} async-done(((bf16[32,12,2048]{2,1,0:T(8,128)(2,1)}), bf16[32,12,2048]{2,1,0:T(8,128)(2,1)}, u32[]{:S(2)}, u32[]{:S(2)}) %all-to-all-start.2) | async-done | bytes 1572896 | tf_op jit(solution)/shard_map/all_to_all | solution.py:95
  1127.9 3.3 all-to-all-start.5
  1131.1 2.5 reshape.766
  1135.6 15.8 all-to-all-done.5
  1151.4 4.0 all-to-all-start.3
  1160.4 1.3 dynamic-slice.4
  1165.4 1.3 dynamic-slice.5
  1167.7 7.1 all-to-all-done.3
  1175.6 45.6 %reduce-scatter.11.cloned.1.call-done = f32[64,2048]{1,0:T(8,128)} async-done(((f32[2048,2048]{1,0:T(8,128)}), f32[64,2048]{1,0:T(8,128)}) %reduce-scatter.11.cloned.1.call-update) | async-done | bytes 524304 | tf_op jit(solution)/shard_map/reduce_scatter | solution.py:281
  1221.2 191.1 %reduce-scatter.9.cloned.1.call-done = f32[64,2048]{1,0:T(8,128)} async-done(((f32[2048,2048]{1,0:T(8,128)}), f32[64,2048]{1,0:T(8,128)}) %reduce-scatter.9.cloned.1.call-update) | async-done | bytes 524304 | tf_op jit(solution)/shard_map/reduce_scatter | solution.py:280
  1412.3 187.3 %reduce-scatter.7.cloned.1.call-done = f32[64,2048]{1,0:T(8,128)} async-done(((f32[2048,2048]{1,0:T(8,128)}), f32[64,2048]{1,0:T(8,128)}) %reduce-scatter.7.cloned.1.call-update) | async-done | bytes 524304 | tf_op jit(solution)/shard_map/reduce_scatter | solution.py:279
  1599.6 187.5 %reduce-scatter.13.cloned.1.call-done = f32[64,2048]{1,0:T(8,128)} async-done(((f32[2048,2048]{1,0:T(8,128)}), f32[64,2048]{1,0:T(8,128)}) %reduce-scatter.13.cloned.1.call-update) | async-done | bytes 524304 | tf_op jit(solution)/shard_map/reduce_scatter | solution.py:282
  1787.1 709.3 %reduce-scatter.17.cloned.1.call-done = f32[256,2048]{1,0:T(8,128)} async-done(((f32[8192,2048]{1,0:T(8,128)}), f32[256,2048]{1,0:T(8,128)}) %reduce-scatter.17.cloned.1.call-update) | async-done | bytes 2097168 | tf_op jit(solution)/shard_map/reduce_scatter | solution.py:220
  2496.4 713.3 %reduce-scatter.15.cloned.1.call-done = f32[64,8192]{1,0:T(8,128)} async-done(((f32[2048,8192]{1,0:T(8,128)}), f32[64,8192]{1,0:T(8,128)}) %reduce-scatter.15.cloned.1.call-update) | async-done | bytes 2097168 | tf_op jit(solution)/shard_map/reduce_scatter | solution.py:219
  (203 shorter events, 43.4 us)
Async XLA Ops:
  7.2 4.0 copy-start.22
  7.2 4.0 copy-start.23
  7.2 275.5 %all-gather.12.cloned.1.call-start = ((), (), s32[]{:S(2)}) async-start(), calls=%async_computation.14 | async-start | bytes 8650752 | tf_op jit(solution)/shard_map/all_gather | solution.py:147
  7.9 281.0 %all-gather.10.cloned.1.call-start = ((), (), s32[]{:S(2)}) async-start(), calls=%async_computation.13 | async-start | bytes 8650752 | tf_op jit(solution)/shard_map/all_gather | solution.py:146
  8.7 294.4 %all-gather.8.cloned.1.call-start = ((), (), s32[]{:S(2)}) async-start(), calls=%async_computation.12 | async-start | bytes 8650752 | tf_op jit(solution)/shard_map/all_gather | solution.py:148
  9.4 372.5 %all-gather.14.cloned.1.call-start = ((), (), s32[]{:S(2)}) async-start(), calls=%async_computation.15 | async-start | bytes 8650752 | tf_op jit(solution)/shard_map/all_gather | solution.py:149
  10.0 568.0 %all-gather.16.cloned.1.call-start = ((), (), s32[]{:S(2)}) async-start(), calls=%async_computation.16 | async-start | bytes 34603008 | tf_op jit(solution)/shard_map/all_gather | solution.py:186
  10.6 763.1 %all-gather.18.cloned.1.call-start = ((), (), s32[]{:S(2)}) async-start(), calls=%async_computation.17 | async-start | bytes 34603008 | tf_op jit(solution)/shard_map/all_gather | solution.py:187
  11.3 7.6 copy-start.28
  12.5 43.2 %all-to-all-start = ((bf16[32,4,4096]{2,1,0:T(4,128)(2,1)}), bf16[32,4,4096]{2,1,0:T(4,128)(2,1)S(1)}, u32[]{:S(2)}, u32[]{:S(2)}) async-start(bf16[32,4,4096]{2,1,0:T(4,128)(2,1)} %reshape.760), calls=%async_computation | async-start | bytes 2097152 | tf_op jit(solution)/shard_map/all_to_all | solution.py:37
  19.8 3.8 copy-start.26
  19.8 40.2 %copy-start = (s32[32]{0:T(128)}, s32[32]{0:T(128)S(1)}, u32[]{:S(2)}) copy-start(s32[32]{0:T(128)S(1)} %get-tuple-element.50) | copy-start | bytes 388
  70.4 5.4 copy-start.29
  70.4 5.4 copy-start.30
  70.5 5.7 copy-start.31
  70.5 5.9 copy-start.32
  70.5 6.2 copy-start.33
  70.5 6.4 copy-start.34
  70.5 6.7 copy-start.35
  70.5 6.9 copy-start.36
  70.5 7.2 copy-start.37
  70.5 203.6 %all-to-all-start.1 = ((bf16[32,12,4096]{2,1,0:T(8,128)(2,1)}), bf16[32,12,4096]{2,1,0:T(8,128)(2,1)}, u32[]{:S(2)}, u32[]{:S(2)}) async-start(bf16[32,12,4096]{2,1,0:T(8,128)(2,1)} %broadcast_select_fusion), calls=%async_computation.1 | async-start | bytes 8388608 | tf_op jit(solution)/shard_map/all_to_all | solution.py:57
  75.8 1079.6 %all-reduce.21.cloned.1.call-start = ((), (), s32[]{:S(2)}) async-start(), calls=%async_computation.24 | async-start | bytes 196608
  282.6 6.3 copy-start.5
  288.9 5.2 copy-start.38
  294.2 1.4 copy-start.40
  294.8 13.4 copy-start.3
  308.3 0.9 copy-start.20
  310.1 77.0 %copy-start.18 = (bf16[16,20,8,128]{3,2,1,0:T(8,128)(2,1)}, bf16[16,20,8,128]{3,2,1,0:T(8,128)(2,1)S(1)}, u32[]{:S(2)}) copy-start(bf16[16,20,8,128]{3,2,1,0:T(8,128)(2,1)S(1)} %fusion.24) | copy-start | bytes 1966084
  594.7 200.3 %copy-start.6 = (bf16[160,4096]{1,0:T(8,128)(2,1)S(1)}, bf16[160,4096]{1,0:T(8,128)(2,1)}, u32[]{:S(2)}) copy-start(bf16[160,4096]{1,0:T(8,128)(2,1)} %copy-done.5) | copy-start | bytes 3932164
  793.2 1.7 copy-start.9
  797.7 1.1 copy-start.10
  799.6 20.6 copy-start.11
  842.4 1.1 copy-start.7
  843.5 6.4 copy-start.4
  849.9 2.3 copy-start.21
  853.2 2.0 copy-start.39
  854.1 1.1 copy-start.17
  857.3 363.9 %reduce-scatter.11.cloned.1.call-start = ((), (), s32[]{:S(2)}) async-start(), calls=%async_computation.20 | async-start | bytes 17301504 | tf_op jit(solution)/shard_map/reduce_scatter | solution.py:281
  866.6 545.7 %reduce-scatter.9.cloned.1.call-start = ((), (), s32[]{:S(2)}) async-start(), calls=%async_computation.19 | async-start | bytes 17301504 | tf_op jit(solution)/shard_map/reduce_scatter | solution.py:280
  868.9 0.9 copy-start.15
  877.9 721.7 %reduce-scatter.7.cloned.1.call-start = ((), (), s32[]{:S(2)}) async-start(), calls=%async_computation.18 | async-start | bytes 17301504 | tf_op jit(solution)/shard_map/reduce_scatter | solution.py:279
  887.2 1.1 copy-start.19
  887.2 899.9 %reduce-scatter.13.cloned.1.call-start = ((), (), s32[]{:S(2)}) async-start(), calls=%async_computation.21 | async-start | bytes 17301504 | tf_op jit(solution)/shard_map/reduce_scatter | solution.py:282
  896.4 1.1 copy-start.12
  896.4 1600.0 %reduce-scatter.17.cloned.1.call-start = ((), (), s32[]{:S(2)}) async-start(), calls=%async_computation.23 | async-start | bytes 69206016 | tf_op jit(solution)/shard_map/reduce_scatter | solution.py:220
  923.2 2286.4 %reduce-scatter.15.cloned.1.call-start = ((), (), s32[]{:S(2)}) async-start(), calls=%async_computation.22 | async-start | bytes 69206016 | tf_op jit(solution)/shard_map/reduce_scatter | solution.py:219
  948.6 0.7 copy-start.25
  948.6 0.8 copy-start.24
  948.6 1.3 copy-start.8
  948.6 1.5 copy-start.14
  950.1 6.4 copy-start.16
  956.5 6.4 copy-start.13
  971.6 1.6 copy-start.2
  1055.0 4.7 copy-start.27
  1055.1 5.1 copy-start.1
  1055.1 72.8 %all-to-all-start.2 = ((bf16[32,12,2048]{2,1,0:T(8,128)(2,1)}), bf16[32,12,2048]{2,1,0:T(8,128)(2,1)}, u32[]{:S(2)}, u32[]{:S(2)}) async-start(bf16[32,12,2048]{2,1,0:T(8,128)(2,1)} %get-tuple-element.54), calls=%async_computation.2 | async-start | bytes 4194304 | tf_op jit(solution)/shard_map/all_to_all | solution.py:95
  1127.9 23.5 all-to-all-start.5
  1151.4 23.4 all-to-all-start.3
Sparse Core Ops, SparseCore 0:
  10.9 115.5 all-gather.11
  129.3 95.5 all-gather.9
  227.8 75.2 all-gather.7
  305.8 76.0 all-gather.13
  384.6 193.3 all-gather.15
  580.7 192.9 all-gather.17
  857.5 122.4 all-reduce.20
  983.0 238.2 reduce-scatter.10
  1224.2 188.0 reduce-scatter.8
  1415.1 184.4 reduce-scatter.6
  1602.6 184.4 reduce-scatter.12
  1790.0 706.3 reduce-scatter.16
  2499.4 710.2 reduce-scatter.14
where the time goes:
time: 3230 us; the launch traced here: 3220 us
  waiting for transfers between devices  2600 us (80%)
  blocking collectives  267 us (8%)
  matrix products  219 us (7%)
  local copies, waits for them, and re-layouts  61.5 us (2%)
    reduce_scatter x1, waiting for transfers between devices, per_device(): lax.psum_scatter(grad_w1, 'dp', scatter_dimension=0, tiled=True)  713 us
    reduce_scatter x1, waiting for transfers between devices, per_device(): lax.psum_scatter(grad_w2, 'dp', scatter_dimension=0, tiled=True)  709 us
    reduce_scatter x1, waiting for transfers between devices, per_device(): lax.psum_scatter(grad_wk, 'dp', scatter_dimension=0, tiled=True)  191 us
    all_gather x1, waiting for transfers between devices, per_device(): lax.all_gather(w1, 'dp', axis=0, tiled=True)  191 us
    reduce_scatter x1, waiting for transfers between devices, per_device(): lax.psum_scatter(grad_wo, 'dp', scatter_dimension=0, tiled=True)  187 us
    reduce_scatter x1, waiting for transfers between devices, per_device(): lax.psum_scatter(grad_wq, 'dp', scatter_dimension=0, tiled=True)  187 us
    all_gather x1, waiting for transfers between devices, per_device(): lax.all_gather(w2, 'dp', axis=0, tiled=True)  179 us
    unnamed x1, blocking collectives  159 us
  transfers between devices with their start and end apart: 18, of which 14 were waited for; matrix products, arithmetic and copies ran while one was open for 7% of the time, Pallas kernels for 0%

commit v1 on v0

--- a/solution.py
+++ b/solution.py
@@ -1,12 +1,25 @@
+import functools
+
 import jax
 import jax.numpy as jnp
 from jax import lax
+from jax.experimental import pallas as pl
+from jax.experimental.pallas import tpu as pltpu
 from jax.sharding import PartitionSpec as P
 
 HEADS = 16
 HEAD_DIM = 128
 SEQ_MAX = 160
 SPAN = 3
+
+GROUP = 16
+HALO = 256
+WINDOW = 512
+TILE = 128
+MESH_ID = pl.DeviceIdType.MESH
+VMEM_LIMIT = 60 << 20
+PORTIONS = ((0, 48), (48, 48), (96, 32))
+ORDERS = ((0, 1, 2), (1, 2, 0), (2, 0, 1))
 
 
 norm_eps = 1e-05
@@ -310,6 +323,599 @@
     )
 
 
+def flip(device, bit):
+    step = 1 << bit
+    return device + step - 2 * step * ((device // step) % 2)
+
+
+def chip_bits(device):
+    return [(device // 2) % 2, (device // 4) % 2, (device // 8) % 2]
+
+
+def enter(partners):
+    barrier = pltpu.get_barrier_semaphore()
+    for partner in partners:
+        pl.semaphore_signal(barrier, inc=1, device_id=(partner,), device_id_type=MESH_ID)
+    pl.semaphore_wait(barrier, len(partners))
+
+
+def push(src, dst, send_sem, recv_sem, device):
+    return pltpu.make_async_remote_copy(
+        src_ref=src,
+        dst_ref=dst,
+        send_sem=send_sem,
+        recv_sem=recv_sem,
+        device_id=(device,),
+        device_id_type=MESH_ID,
+    )
+
+
+def gather_kernel(x_ref, o_ref, local_sem, send_sem, recv_sem, pair_send, pair_recv):
+    device = lax.axis_index("dp")
+    core = device % 2
+    bits = chip_bits(device)
+    partners = [flip(device, 1), flip(device, 2), flip(device, 3)]
+    pair = flip(device, 0)
+    enter(partners + [pair])
+
+    def at(values, rows):
+        return o_ref.at[values[2], values[1], values[0], core, rows, slice(None)]
+
+    own = o_ref.at[bits[2], bits[1], bits[0], core]
+    local = pltpu.make_async_copy(x_ref, own, local_sem)
+    local.start()
+    hops, shares = {}, {}
+
+    def hop(part, step):
+        first, count = PORTIONS[part]
+        rows = pl.ds(first, count)
+        values = list(bits)
+        for dim in ORDERS[part][:step]:
+            values[dim] = slice(None)
+        dst = at(values, rows)
+        src = x_ref.at[rows, :] if step == 0 else dst
+        copy = push(
+            src, dst, send_sem.at[part, step], recv_sem.at[part, step], partners[ORDERS[part][step]]
+        )
+        copy.start()
+        hops[part, step] = copy
+
+    def share(part, step):
+        first, count = PORTIONS[part]
+        rows = pl.ds(first, count)
+        values = list(bits)
+        if step:
+            for dim in ORDERS[part][: step - 1]:
+                values[dim] = slice(None)
+            dim = ORDERS[part][step - 1]
+            values[dim] = 1 - bits[dim]
+        dst = at(values, rows)
+        src = dst if step else x_ref.at[rows, :]
+        copy = push(src, dst, pair_send.at[part, step], pair_recv.at[part, step], pair)
+        copy.start()
+        shares[part, step] = copy
+
+    for part in range(3):
+        hop(part, 0)
+    for part in range(3):
+        share(part, 0)
+    local.wait()
+    for step in (1, 2, 3):
+        for part in range(3):
+            hops[part, step - 1].wait_recv()
+            if step < 3:
+                hop(part, step)
+            share(part, step)
+    for copy in shares.values():
+        copy.wait()
+    for copy in hops.values():
+        copy.wait_send()
+
+
+def group_gather(rows, name, collective_id):
+    count, width = rows.shape
+    vmem = pl.BlockSpec(memory_space=pltpu.VMEM)
+    sems = pltpu.SemaphoreType.DMA
+    out = pl.pallas_call(
+        gather_kernel,
+        out_shape=jax.ShapeDtypeStruct((2, 2, 2, 2, count, width), rows.dtype),
+        in_specs=[vmem],
+        out_specs=vmem,
+        scratch_shapes=[sems, sems((3, 3)), sems((3, 3)), sems((3, 4)), sems((3, 4))],
+        compiler_params=pltpu.CompilerParams(
+            collective_id=collective_id, has_side_effects=True, vmem_limit_bytes=VMEM_LIMIT
+        ),
+        name=name,
+    )(rows)
+    return out.reshape(GROUP * count, width)
+
+
+def scatter_kernel(
+    x_ref, o_ref, pair_in, sums, in_one, in_two, in_three, send_sem, recv_sem, pair_send, pair_recv
+):
+    device = lax.axis_index("dp")
+    core = device % 2
+    bits = chip_bits(device)
+    partners = [flip(device, 1), flip(device, 2), flip(device, 3)]
+    pair = flip(device, 0)
+    width = x_ref.shape[-1]
+    f32 = jnp.float32
+    incoming = (in_one, in_two, in_three)
+    enter(partners + [pair])
+
+    def view(ref, values, rows, with_core=None):
+        where = (values[2], values[1], values[0])
+        if with_core is not None:
+            where = where + (with_core,)
+        return ref.at[where + (rows, slice(None))]
+
+    shares, hops = {}, {}
+    for half in range(2):
+        for part in range(3):
+            first, count = PORTIONS[part]
+            rows = pl.ds(first, count)
+            dim = ORDERS[part][0]
+            values = [slice(None)] * 3
+            values[dim] = 1 - bits[dim] if half == 0 else bits[dim]
+            copy = push(
+                view(x_ref, values, rows, 1 - core),
+                view(pair_in, values, rows),
+                pair_send.at[part, half],
+                pair_recv.at[part, half],
+                pair,
+            )
+            copy.start()
+            shares[part, half] = copy
+
+    def add_up(part, values, arrived, store):
+        first, count = PORTIONS[part]
+
+        def body(index, carry):
+            rows = pl.ds(pl.multiple_of(first + index * 16, 16), 16)
+            where = (values[2], values[1], values[0])
+            total = x_ref[where + (core, rows, slice(None))].astype(f32)
+            total = total + pair_in[where + (rows, slice(None))].astype(f32)
+            for ref in incoming[:arrived]:
+                total = total + ref[where + (rows, slice(None))].astype(f32)
+            store(where, rows, total)
+            return carry
+
+        lax.fori_loop(0, count // 16, body, 0)
+
+    def keep_sum(where, rows, total):
+        sums[where + (rows, slice(None))] = total.astype(sums.dtype)
+
+    def finish(where, rows, total):
+        o_ref[rows, :] = total
+
+    def hop(part, step):
+        first, count = PORTIONS[part]
+        order = ORDERS[part]
+        values = list(bits)
+        values[order[step]] = 1 - bits[order[step]]
+        free = order[step + 1 :]
+        for mask in range(1 << len(free)):
+            slot = list(values)
+            for place, dim in enumerate(free):
+                slot[dim] = (mask >> place) & 1
+            add_up(part, slot, step, keep_sum)
+        for dim in free:
+            values[dim] = slice(None)
+        rows = pl.ds(first, count)
+        copy = push(
+            view(sums, values, rows),
+            view(incoming[step], values, rows),
+            send_sem.at[part, step],
+            recv_sem.at[part, step],
+            partners[order[step]],
+        )
+        copy.start()
+        hops[part, step] = copy
+
+    for part in range(3):
+        shares[part, 0].wait_recv()
+        hop(part, 0)
+    for part in range(3):
+        shares[part, 1].wait_recv()
+        hops[part, 0].wait_recv()
+        hop(part, 1)
+    for part in range(3):
+        hops[part, 1].wait_recv()
+        hop(part, 2)
+    for part in range(3):
+        hops[part, 2].wait_recv()
+        add_up(part, bits, 3, finish)
+    for copy in shares.values():
+        copy.wait_send()
+    for copy in hops.values():
+        copy.wait_send()
+
+
+def group_scatter(partial, name, collective_id):
+    width = partial.shape[-1]
+    count = partial.shape[0] // GROUP
+    low = partial.dtype
+    vmem = pl.BlockSpec(memory_space=pltpu.VMEM)
+    sems = pltpu.SemaphoreType.DMA
+    slots = pltpu.VMEM((2, 2, 2, count, width), low)
+    return pl.pallas_call(
+        scatter_kernel,
+        out_shape=jax.ShapeDtypeStruct((count, width), jnp.float32),
+        in_specs=[vmem],
+        out_specs=vmem,
+        scratch_shapes=[
+            slots, slots, slots, slots, slots,
+            sems((3, 3)), sems((3, 3)), sems((3, 2)), sems((3, 2)),
+        ],
+        compiler_params=pltpu.CompilerParams(
+            collective_id=collective_id, has_side_effects=True, vmem_limit_bytes=VMEM_LIMIT
+        ),
+        name=name,
+    )(partial.reshape(2, 2, 2, 2, count, width))
+
+
+def exchange_kernel(arrays, *refs):
+    ins, outs = refs[:arrays], refs[arrays : 2 * arrays]
+    local_sem, send_sem, recv_sem = refs[2 * arrays :]
+    device = lax.axis_index("dp")
+    base = device // GROUP * GROUP
+    mine = device % GROUP
+    others = [base + (mine + step) % GROUP for step in range(1, GROUP)]
+    enter(others)
+    copies, locals_ = [], []
+    for at in range(arrays):
+        for step, other in enumerate(others):
+            copy = push(
+                ins[at].at[other - base],
+                outs[at].at[mine],
+                send_sem.at[at, step],
+                recv_sem.at[at, step],
+                other,
+            )
+            copy.start()
+            copies.append(copy)
+        local = pltpu.make_async_copy(ins[at].at[mine], outs[at].at[mine], local_sem.at[at])
+        local.start()
+        locals_.append(local)
+    for copy in locals_:
+        copy.wait()
+    for copy in copies:
+        copy.wait()
+
+
+def group_exchange(arrays, name, collective_id):
+    count = len(arrays)
+    anywhere = pl.BlockSpec(memory_space=pl.ANY)
+    sems = pltpu.SemaphoreType.DMA
+    return pl.pallas_call(
+        functools.partial(exchange_kernel, count),
+        out_shape=[jax.ShapeDtypeStruct(item.shape, item.dtype) for item in arrays],
+        in_specs=[anywhere] * count,
+        out_specs=[anywhere] * count,
+        scratch_shapes=[sems((count,)), sems((count, GROUP - 1)), sems((count, GROUP - 1))],
+        compiler_params=pltpu.CompilerParams(
+            collective_id=collective_id, has_side_effects=True, vmem_limit_bytes=VMEM_LIMIT
+        ),
+        name=name,
+    )(*arrays)
+
+
+def window_start(row, total):
+    start = jnp.minimum(jnp.maximum(row - (WINDOW - TILE) // 2, 0), total - WINDOW)
+    return pl.multiple_of(start, 64)
+
+
+def tile_probs(qkv_ref, row, start, seg_q, seg_k):
+    f32 = jnp.float32
+    queries = qkv_ref[pl.ds(row, TILE), 0:HEAD_DIM]
+    keys = qkv_ref[pl.ds(start, WINDOW), HEAD_DIM : 2 * HEAD_DIM]
+    scores = lax.dot_general(queries, keys, (((1,), (1,)), ((), ())), preferred_element_type=f32)
+    scores = jnp.where(seg_q == seg_k, scores * HEAD_DIM ** (-0.5), -1e30)
+    weights = jnp.exp(scores - jnp.max(scores, -1, keepdims=True))
+    return queries, keys, weights / jnp.sum(weights, -1, keepdims=True)
+
+
+def attend_kernel(offset_ref, qkv_ref, seg_q_ref, seg_k_ref, o_ref):
+    total = qkv_ref.shape[0]
+    offset = offset_ref[0]
+
+    def body(tile, carry):
+        row = pl.multiple_of(offset + tile * TILE, TILE)
+        start = window_start(row, total)
+        _, _, probs = tile_probs(
+            qkv_ref, row, start, seg_q_ref[pl.ds(row, TILE), :], seg_k_ref[row // TILE]
+        )
+        values = qkv_ref[pl.ds(start, WINDOW), 2 * HEAD_DIM : 3 * HEAD_DIM]
+        out = jnp.dot(probs.astype(values.dtype), values, preferred_element_type=jnp.float32)
+        o_ref[pl.ds(pl.multiple_of(tile * TILE, TILE), TILE), :] = out.astype(o_ref.dtype)
+        return carry
+
+    lax.fori_loop(0, o_ref.shape[0] // TILE, body, 0, unroll=2)
+
+
+def attend_back_kernel(qkv_ref, grad_ref, seg_q_ref, seg_k_ref, o_ref, dq_sum, dk_sum, dv_sum):
+    total = qkv_ref.shape[0]
+    f32 = jnp.float32
+    low = qkv_ref.dtype
+    scale = HEAD_DIM ** (-0.5)
+    dk_sum[...] = jnp.zeros_like(dk_sum)
+    dv_sum[...] = jnp.zeros_like(dv_sum)
+
+    def body(tile, carry):
+        row = pl.multiple_of(tile * TILE, TILE)
+        start = window_start(row, total)
+        queries, keys, probs = tile_probs(
+            qkv_ref, row, start, seg_q_ref[pl.ds(row, TILE), :], seg_k_ref[tile]
+        )
+        window = pl.ds(start, WINDOW)
+        values = qkv_ref[window, 2 * HEAD_DIM : 3 * HEAD_DIM]
+        grads = grad_ref[pl.ds(row, TILE), :]
+        grad_probs = lax.dot_general(
+            grads, values, (((1,), (1,)), ((), ())), preferred_element_type=f32
+        )
+        inner = jnp.sum(probs * grad_probs, -1, keepdims=True)
+        grad_scores = (probs * (grad_probs - inner)).astype(low)
+        dq_sum[pl.ds(row, TILE), :] = jnp.dot(grad_scores, keys, preferred_element_type=f32)
+        dk_sum[window, :] += lax.dot_general(
+            grad_scores, queries, (((0,), (0,)), ((), ())), preferred_element_type=f32
+        )
+        dv_sum[window, :] += lax.dot_general(
+            probs.astype(low), grads, (((0,), (0,)), ((), ())), preferred_element_type=f32
+        )
+        return carry
+
+    lax.fori_loop(0, total // TILE, body, 0, unroll=2)
+    o_ref[:, 0:HEAD_DIM] = (dq_sum[...] * scale).astype(low)
+    o_ref[:, HEAD_DIM : 2 * HEAD_DIM] = (dk_sum[...] * scale).astype(low)
+    o_ref[:, 2 * HEAD_DIM : 3 * HEAD_DIM] = dv_sum[...].astype(low)
+
+
+def attend(offset, qkv, seg_q, seg_k, rows):
+    vmem = pl.BlockSpec(memory_space=pltpu.VMEM)
+    return pl.pallas_call(
+        attend_kernel,
+        out_shape=jax.ShapeDtypeStruct((rows, HEAD_DIM), qkv.dtype),
+        in_specs=[pl.BlockSpec(memory_space=pltpu.SMEM), vmem, vmem, vmem],
+        out_specs=vmem,
+        compiler_params=pltpu.CompilerParams(vmem_limit_bytes=VMEM_LIMIT),
+        name="attend",
+    )(offset, qkv, seg_q, seg_k)
+
+
+def attend_back(qkv, grads, seg_q, seg_k):
+    vmem = pl.BlockSpec(memory_space=pltpu.VMEM)
+    total = qkv.shape[0]
+    acc = pltpu.VMEM((total, HEAD_DIM), jnp.float32)
+    return pl.pallas_call(
+        attend_back_kernel,
+        out_shape=jax.ShapeDtypeStruct(qkv.shape, qkv.dtype),
+        in_specs=[vmem, vmem, vmem, vmem],
+        out_specs=vmem,
+        scratch_shapes=[acc, acc, acc],
+        compiler_params=pltpu.CompilerParams(vmem_limit_bytes=VMEM_LIMIT),
+        name="attend_back",
+    )(qkv, grads, seg_q, seg_k)
+
+
+def grouped_device(
+    tokens,
+    cotangent,
+    lengths,
+    wq,
+    bq,
+    wk,
+    wv,
+    bv,
+    wo,
+    bo,
+    norm1_gain,
+    norm1_bias,
+    w1,
+    b1,
+    w2,
+    b2,
+    norm2_gain,
+    norm2_bias,
+):
+    f32 = jnp.float32
+    bf16 = jnp.bfloat16
+    devices = lax.axis_size("dp")
+    block, width = tokens.shape
+    own_rows = GROUP * block
+    total_tokens = devices * block
+    weight_rows = wq.shape[0]
+    unit_rows, units = w2.shape[0], w1.shape[1]
+    device = lax.axis_index("dp")
+    group, member = device // GROUP, device % GROUP
+    chip, core = member // 2, member % 2
+    head = core * 8 + chip
+    first_group = group == 0
+    across = [(at, (at + GROUP) % devices) for at in range(devices)]
+    beside = [(at, at + 1 - 2 * (at % 2)) for at in range(devices)]
+
+    def swap(own, other):
+        return jnp.where(first_group, own, other), jnp.where(first_group, other, own)
+
+    def in_order(own, other):
+        return jnp.concatenate(swap(own, other), 0)
+
+    def by_head(weight):
+        return weight.reshape(weight_rows, 2, 8, HEAD_DIM).transpose(2, 1, 0, 3).reshape(
+            GROUP, weight_rows, HEAD_DIM
+        )
+
+    pack_qkv = jnp.concatenate([by_head(wq), by_head(wk), by_head(wv)], -1)
+    pack_w1 = w1.reshape(weight_rows, 2, GROUP, unit_rows).transpose(2, 0, 1, 3).reshape(
+        GROUP, weight_rows, 2 * unit_rows
+    )
+    own_qkv, own_w1 = group_exchange([pack_qkv, pack_w1], "weights_out", 1)
+    own_qkv = own_qkv.reshape(GROUP * weight_rows, 3 * HEAD_DIM)
+    own_w1 = own_w1.reshape(GROUP * weight_rows, 2 * unit_rows)
+    full_qkv = in_order(own_qkv, lax.ppermute(own_qkv, "dp", across))
+    wo_beside = lax.ppermute(wo, "dp", beside)
+    chip_wo = jnp.concatenate(
+        [jnp.where(core == 0, wo, wo_beside), jnp.where(core == 0, wo_beside, wo)], 0
+    )
+    wo_pairs = [
+        (GROUP * g + 2 * k + g, GROUP * (1 - g) + 2 * k + g) for g in range(2) for k in range(8)
+    ]
+    full_wo = jnp.where(core == group, chip_wo, lax.ppermute(chip_wo, "dp", wo_pairs))
+    full_w1 = in_order(own_w1, lax.ppermute(own_w1, "dp", across))
+    full_w2 = in_order(w2, lax.ppermute(w2, "dp", across))
+
+    vectors = [bq, bv, bo, norm1_gain, norm1_bias, b2, norm2_gain, norm2_bias, b1]
+    sizes = [item.shape[0] for item in vectors]
+    gathered = lax.all_gather(jnp.concatenate(vectors), "dp", axis=0).astype(f32)
+    whole, at = [], 0
+    for size in sizes:
+        whole.append(gathered[:, at : at + size].reshape(-1))
+        at += size
+    all_bq, all_bv, all_bo, gain_one, shift_one, all_b2, gain_two, shift_two, all_b1 = whole
+    my_b1 = lax.dynamic_index_in_dim(
+        all_b1.reshape(2, GROUP, unit_rows), member, 1, keepdims=False
+    ).reshape(-1)
+    my_bq = lax.dynamic_slice_in_dim(all_bq, head * HEAD_DIM, HEAD_DIM)
+    my_bv = lax.dynamic_slice_in_dim(all_bv, head * HEAD_DIM, HEAD_DIM)
+    my_bqkv = jnp.concatenate([my_bq, jnp.zeros_like(my_bq), my_bv])
+
+    ext_rows = own_rows + HALO
+    ext_first = group * (own_rows - HALO)
+    offset = group * HALO
+    starts = jnp.cumsum(lengths) - lengths
+    ext_ids = ext_first + jnp.arange(ext_rows, dtype=jnp.int32)
+    seg = jnp.sum((ext_ids[:, None] >= starts[None, :]).astype(jnp.int32), 1)
+    tile_rows = jnp.arange(ext_rows // TILE, dtype=jnp.int32) * TILE
+    tile_starts = jnp.clip(tile_rows - (WINDOW - TILE) // 2, 0, ext_rows - WINDOW)
+    key_ids = ext_first + tile_starts[:, None] + jnp.arange(WINDOW, dtype=jnp.int32)[None, :]
+    seg_k = jnp.sum((key_ids[:, :, None] >= starts[None, None, :]).astype(jnp.int32), 2)
+    seg_k = seg_k[:, None, :]
+    seg_q = seg[:, None]
+
+    def with_halo(rows):
+        edge = jnp.where(first_group, rows[own_rows - HALO :], rows[:HALO])
+        halo = lax.ppermute(edge, "dp", across)
+        return jnp.where(
+            first_group, jnp.concatenate([rows, halo], 0), jnp.concatenate([halo, rows], 0)
+        )
+
+    all_tokens = group_gather(tokens, "gather_tokens", 2)
+    qkv = (jnp.dot(all_tokens, full_qkv, preferred_element_type=f32) + my_bqkv).astype(bf16)
+    qkv_ext = with_halo(qkv)
+    attended = attend(offset.reshape(1), qkv_ext, seg_q, seg_k, own_rows)
+    branch_part = jnp.dot(attended, full_wo, preferred_element_type=f32).astype(bf16)
+    branch = group_scatter(branch_part, "scatter_branch", 3) + all_bo
+    resid_one = tokens.astype(f32) + branch
+    hidden, norm_one_back = jax.vjp(layer_norm, resid_one, gain_one, shift_one)
+
+    all_hidden = group_gather(hidden.astype(bf16), "gather_hidden", 4)
+    upward = jnp.dot(all_hidden, full_w1, preferred_element_type=f32) + my_b1
+    activ, gelu_back = jax.vjp(gelu_tanh, upward)
+    activ_low = activ.astype(bf16)
+    mixed_part = jnp.dot(activ_low, full_w2, preferred_element_type=f32).astype(bf16)
+    mixed = group_scatter(mixed_part, "scatter_mixed", 5) + all_b2
+    normed, norm_two_back = jax.vjp(layer_norm, hidden + mixed, gain_two, shift_two)
+    output = normed.astype(bf16)
+
+    grad_resid_two, grad_gain_two, grad_shift_two = norm_two_back(cotangent.astype(f32))
+    grad_mixed = grad_resid_two.astype(bf16)
+    grad_b2 = jnp.sum(grad_mixed.astype(f32), 0)
+    all_grad_mixed = group_gather(grad_mixed, "gather_grad_mixed", 6)
+    grad_activ = jnp.einsum("td,fd->tf", all_grad_mixed, full_w2, preferred_element_type=f32)
+    grad_upward = gelu_back(grad_activ)[0].astype(bf16)
+    grad_b1 = jnp.sum(grad_upward.astype(f32), 0)
+    hidden_part = jnp.einsum(
+        "tf,df->td", grad_upward, full_w1, preferred_element_type=f32
+    ).astype(bf16)
+    grad_w2 = jnp.einsum("tf,td->fd", activ_low, all_grad_mixed, preferred_element_type=f32)
+    grad_w1 = jnp.einsum("td,tf->df", all_hidden, grad_upward, preferred_element_type=f32)
+
+    def across_sum(grad):
+        halves = grad.reshape((2, grad.shape[0] // 2) + grad.shape[1:])
+        mine = jnp.where(first_group, halves[0], halves[1])
+        theirs = jnp.where(first_group, halves[1], halves[0]).astype(bf16)
+        return mine + lax.ppermute(theirs, "dp", across).astype(f32)
+
+    out_w2 = across_sum(grad_w2)
+    sum_w1 = across_sum(grad_w1)
+    grad_hidden = grad_resid_two + group_scatter(hidden_part, "scatter_grad_hidden", 7)
+
+    grad_resid_one, grad_gain_one, grad_shift_one = norm_one_back(grad_hidden)
+    grad_branch = grad_resid_one.astype(bf16)
+    grad_bo = jnp.sum(grad_branch.astype(f32), 0)
+    all_grad_branch = group_gather(grad_branch, "gather_grad_branch", 8)
+    grad_attended = jnp.einsum(
+        "td,cd->tc", all_grad_branch, full_wo, preferred_element_type=f32
+    ).astype(bf16)
+    grad_wo = jnp.einsum("tc,td->cd", attended, all_grad_branch, preferred_element_type=f32)
+    grad_qkv_ext = attend_back(qkv_ext, with_halo(grad_attended), seg_q, seg_k)
+    grad_qkv = lax.dynamic_slice_in_dim(grad_qkv_ext, offset, own_rows, 0)
+    grad_bqkv = jnp.sum(grad_qkv.astype(f32), 0)
+    input_part = jnp.einsum("tf,df->td", grad_qkv, full_qkv, preferred_element_type=f32)
+    grad_wqkv = jnp.einsum("td,tf->df", all_tokens, grad_qkv, preferred_element_type=f32)
+    sum_qkv = across_sum(grad_wqkv)
+    input_sum = group_scatter(input_part.astype(bf16), "scatter_input", 9)
+    input_grad = (grad_resid_one + input_sum).astype(bf16)
+
+    back_pairs = [(dst, src) for src, dst in wo_pairs]
+    sum_wo = grad_wo + lax.ppermute(grad_wo.astype(bf16), "dp", back_pairs).astype(f32)
+    halves = sum_wo.reshape(2, weight_rows, width)
+    mine_wo = jnp.where(core == 0, halves[0], halves[1])
+    theirs_wo = jnp.where(core == 0, halves[1], halves[0])
+    out_wo = jnp.where(core == group, mine_wo, lax.ppermute(theirs_wo, "dp", beside))
+    rows_w1, rows_qkv = group_exchange(
+        [
+            sum_w1.astype(bf16).reshape(GROUP, weight_rows, 2 * unit_rows),
+            sum_qkv.astype(bf16).reshape(GROUP, weight_rows, 3 * HEAD_DIM),
+        ],
+        "weights_back",
+        10,
+    )
+    out_w1 = (
+        rows_w1.reshape(GROUP, weight_rows, 2, unit_rows)
+        .transpose(1, 2, 0, 3)
+        .reshape(weight_rows, units)
+        .astype(f32)
+    )
+    out_q, out_k, out_v = [
+        rows_qkv[:, :, at * HEAD_DIM : (at + 1) * HEAD_DIM]
+        .reshape(8, 2, weight_rows, HEAD_DIM)
+        .transpose(2, 1, 0, 3)
+        .reshape(weight_rows, width)
+        .astype(f32)
+        for at in range(3)
+    ]
+
+    def place_head(vector):
+        return lax.dynamic_update_slice_in_dim(
+            jnp.zeros((width,), f32), vector, head * HEAD_DIM, 0
+        )
+
+    spread_b1 = lax.dynamic_update_slice_in_dim(
+        jnp.zeros((2, GROUP, unit_rows), f32), grad_b1.reshape(2, 1, unit_rows), member, 1
+    )
+
+    def reduce_vectors(items):
+        parts = jnp.concatenate([item.reshape(devices, -1) for item in items], 1)
+        mine = lax.psum_scatter(parts.reshape(-1), "dp", scatter_dimension=0, tiled=True)
+        result, at = [], 0
+        for item in items:
+            size = item.size // devices
+            result.append(mine[at : at + size])
+            at += size
+        return result
+
+    out_b1, out_b2, out_g2, out_s2, out_bo, out_g1, out_s1 = reduce_vectors(
+        [spread_b1, grad_b2, grad_gain_two, grad_shift_two, grad_bo, grad_gain_one, grad_shift_one]
+    )
+    out_bq, out_bv = reduce_vectors(
+        [place_head(grad_bqkv[:HEAD_DIM]), place_head(grad_bqkv[2 * HEAD_DIM :])]
+    )
+    return (
+        output, input_grad, out_q, out_bq, out_k, out_v, out_bv, out_wo, out_bo, out_g1, out_s1,
+        out_w1, out_b1, out_w2, out_b2, out_g2, out_s2,
+    )
+
+
 def solution(mesh):
     in_specs = (
         P("dp", None),
@@ -350,6 +956,7 @@
         P("dp"),
         P("dp"),
     )
+    two_groups = mesh.shape["dp"] == 2 * GROUP
     return jax.shard_map(
-        per_device, mesh=mesh, in_specs=in_specs, out_specs=out_specs, check_vma=False
-    )
+        grouped_device if two_groups else per_device, mesh=mesh, in_specs=in_specs, out_specs=out_specs, check_vma=False
+    )

time: 3230 us -> 972 us (0.30)
  waiting for transfers between devices: 2600 us -> 76 us
  Pallas kernels: 0 us -> 494 us
  matrix products: 219 us -> 91.8 us
  blocking collectives: 267 us -> 187 us
    reduce_scatter x6 -> x0, waiting for transfers between devices: 2030 us -> none  [the longest x1 713 us: per_device(): lax.psum_scatter(grad_w1, 'dp', scatter_dimension=0, tiled=True)]
    pallas_call x0 -> x12, Pallas kernels: none -> 494 us  [the longest x4 238 us: group_scatter(): pl.pallas_call(scatter_kernel, out_shape=jax.ShapeDtypeStruct((count, wid...]
    all_gather x6 -> x0, waiting for transfers between devices: 449 us -> none  [the longest x1 191 us: per_device(): lax.all_gather(w1, 'dp', axis=0, tiled=True)]
    dot_general x24 -> x12, matrix products: 219 us -> 91.8 us  [the longest x1 11.9 us: grouped_device(): jnp.einsum('td,fd->tf', all_grad_mixed, full_w2, preferred_element_type=f32)]
    unnamed x1, blocking collectives: 159 us -> 41.6 us
    all_to_all x5 -> x0, waiting for transfers between devices: 115 us -> none  [the longest x1 61.6 us: to_order(): lax.all_to_all(outgoing, 'dp', split_axis=0, concat_axis=0, tiled=True)]
    all_gather x1, blocking collectives: 34.6 us -> 146 us  [grouped_device(): lax.all_gather(jnp.concatenate(vectors), 'dp', axis=0).astype(f32)]
    all_to_all x1 -> x0, blocking collectives: 73.9 us -> none  [to_order(): lax.all_to_all(outgoing, 'dp', split_axis=0, concat_axis=0, tiled=True)]
  transfers between devices with their start and end apart: 18 -> 13, of which waited for: 14 -> 2; matrix products, arithmetic and copies ran while one was open for 7% -> 12% of each run, Pallas kernels for 0% -> 42%
where the time goes in v1:
time: 972 us; the launch traced here: 962 us
  Pallas kernels  494 us (51%)
  blocking collectives  187 us (19%)
  matrix products  91.8 us (9%)
  waiting for transfers between devices  76 us (8%)
  other arithmetic  49.1 us (5%)
  local copies, waits for them, and re-layouts  29.9 us (3%)
  starting transfers between devices  19.2 us (2%)
  between operations  15.4 us (2%)
    pallas_call x4, Pallas kernels, group_scatter(): pl.pallas_call(scatter_kernel, out_shape=jax.ShapeDtypeStruct((count, wid...  238 us
    pallas_call x4, Pallas kernels, group_gather(): pl.pallas_call(gather_kernel, out_shape=jax.ShapeDtypeStruct((2, 2, 2, 2,...  175 us
    all_gather x1, blocking collectives, grouped_device(): lax.all_gather(jnp.concatenate(vectors), 'dp', axis=0).astype(f32)  146 us
    unnamed x2, waiting for transfers between devices  68.4 us
    pallas_call x2, Pallas kernels, group_exchange(): pl.pallas_call(functools.partial(exchange_kernel, count), out_shape=[jax....  56.1 us
    unnamed x1, blocking collectives  41.6 us
  transfers between devices with their start and end apart: 13, of which 2 were waited for; matrix products, arithmetic and copies ran while one was open for 12% of the time, Pallas kernels for 42%

profile of v1, /device:TPU:7, one launch (start us, length us, event | category | flops | bytes accessed | tf_op | source)
XLA Modules:
  0.0 962.4 jit_solution(5639798641858696187)
XLA Ops:
  11.2 1.5 copy.102
  13.8 1.5 reshape.324.refs_1_
  16.3 27.7 %weights_out.1 = (bf16[16,64,384]{2,1,0:T(8,128)(2,1)}, bf16[16,64,512]{2,1,0:T(8,128)(2,1)}) custom-call(bf16[16,64,384]{2,1,0:T(8,128)(2,1)} %pad_maximum_fusion.11.refs_0_, bf16[16,64,512]{2,1,0:T(8,128)(2,1)} %reshape.324.refs_1_), custom_call_target="tpu_custom_call" | custom-call | tf_op jit(solution)/shard_map/weights_out/pallas_call | solution.py:590
  44.0 1.4 copy.86
  45.4 2.4 collective-permute-start
  47.9 2.3 collective-permute-start.5
  50.4 145.7 %all-gather.1 = bf16[32,1,768]{2,1,0:T(2,128)(2,1)S(1)} all-gather(bf16[1,1,768]{2,1,0:T(2,128)(2,1)S(1)} %reshape.363), channel_id=2, replica_groups=mesh['dp'=32] {'dp'}, dimensions={0}, use_global_device_ids=true | all-gather | bytes 50688 | tf_op jit(solution)/shard_map/all_gather | solution.py:768
  196.9 44.6 %gather_tokens.1 = bf16[2,2,2,2,128,2048]{5,4,3,2,1,0:T(8,128)(2,1)} custom-call(bf16[128,2048]{1,0:T(8,128)(2,1)} %x_ref.1), custom_call_target="tpu_custom_call" | custom-call | tf_op jit(solution)/shard_map/gather_tokens/pallas_call | solution.py:419
  243.7 1.3 collective-permute-start.3
  245.1 8.5 fusion.7
  254.4 3.8 collective-permute-start.1
  259.4 2.1 broadcast_in_dim.43.seg_q_ref
  261.5 7.6 collective-permute-done.1
  269.0 2.8 maximum_select_fusion.qkv_ref
  271.9 9.3 attend.1
  281.2 6.8 convolution_convert_fusion.3
  288.0 43.0 %scatter_branch.1 = f32[128,2048]{1,0:T(8,128)} custom-call(bf16[2,2,2,2,128,2048]{5,4,3,2,1,0:T(8,128)(2,1)} %bitcast.96), custom_call_target="tpu_custom_call" | custom-call | tf_op jit(solution)/shard_map/scatter_branch/pallas_call | solution.py:541
  331.0 1.5 fusion.31
  333.8 43.8 %gather_hidden.1 = bf16[2,2,2,2,128,2048]{5,4,3,2,1,0:T(8,128)(2,1)} custom-call(bf16[128,2048]{1,0:T(8,128)(2,1)} %fusion.16.x_ref), custom_call_target="tpu_custom_call" | custom-call | tf_op jit(solution)/shard_map/gather_hidden/pallas_call | solution.py:419
  377.6 1.7 broadcast_select_fusion.3
  379.4 7.6 fusion.9
  387.0 2.2 broadcast_select_fusion.1
  389.2 7.2 convolution_convert_fusion.2
  396.4 42.7 %scatter_mixed.1 = f32[128,2048]{1,0:T(8,128)} custom-call(bf16[2,2,2,2,128,2048]{5,4,3,2,1,0:T(8,128)(2,1)} %bitcast.99), custom_call_target="tpu_custom_call" | custom-call | tf_op jit(solution)/shard_map/scatter_mixed/pallas_call | solution.py:541
  439.2 1.7 fusion.30
  441.6 1.3 fusion.29
  443.8 43.5 %gather_grad_mixed.1 = bf16[2,2,2,2,128,2048]{5,4,3,2,1,0:T(8,128)(2,1)} custom-call(bf16[128,2048]{1,0:T(8,128)(2,1)} %get-tuple-element.34.x_ref), custom_call_target="tpu_custom_call" | custom-call | tf_op jit(solution)/shard_map/gather_grad_mixed/pallas_call | solution.py:419
  487.3 11.9 %convert_reduce_fusion = (f32[512]{0:T(512)S(1)}, bf16[2048,512]{1,0:T(8,128)(2,1)S(1)}) fusion(f32[2048,512]{1,0:T(8,128)} %copy-done.34, f32[512]{0:T(512)S(1)} %bitcast.137, bf16[2048,2048]{1,0:T(8,128)(2,1)} %bitcast.104, bf16[256,2048]{1,0:T(8,128)(2,1)} %copy-done.18, bf16[256,2048]{1,0:T(8,128)(2,1)S(1)} %copy-done.17), kind=kOutput, calls=%fused_computation.13 | convolution fusion | flops 4323278336 | bytes 16781312 | tf_op jit(solution)/shard_map/td,fd->tf/dot_general | solution.py:823
  499.3 6.5 fusion.27
  505.9 9.9 %fusion.37 = f32[2048,512]{1,0:T(8,128)} fusion(bf16[2048,2048]{1,0:T(8,128)(2,1)} %bitcast.103, bf16[2048,512]{1,0:T(8,128)(2,1)S(1)} %get-tuple-element.75), kind=kOutput, calls=%fused_computation.121 | convolution fusion | flops 4294967296 | bytes 14680064 | tf_op jit(solution)/shard_map/td,tf->df/dot_general | solution.py:830
  515.8 8.0 convolution_convert_fusion.1
  524.0 3.4 select_convert_fusion.1
  527.4 3.4 select_convert_fusion
  530.7 2.3 collective-permute-start.11
  533.1 97.1 %scatter_grad_hidden.1 = f32[128,2048]{1,0:T(8,128)} custom-call(bf16[2,2,2,2,128,2048]{5,4,3,2,1,0:T(8,128)(2,1)} %bitcast.98), custom_call_target="tpu_custom_call" | custom-call | tf_op jit(solution)/shard_map/scatter_grad_hidden/pallas_call | solution.py:541
  630.2 1.8 multiply_reduce_fusion
  634.4 43.0 %gather_grad_branch.1 = bf16[2,2,2,2,128,2048]{5,4,3,2,1,0:T(8,128)(2,1)} custom-call(bf16[128,2048]{1,0:T(8,128)(2,1)} %get-tuple-element.32.x_ref), custom_call_target="tpu_custom_call" | custom-call | tf_op jit(solution)/shard_map/gather_grad_branch/pallas_call | solution.py:419
  677.4 5.6 fusion.36
  683.2 3.5 convolution_convert_fusion.4
  686.7 1.2 collective-permute-start.6
  687.9 4.0 collective-permute-start.9
  691.8 68.4 %all-reduce.4.cloned.1.call-done = f32[20480]{0:T(1024)} async-done(((f32[20480]{0:T(1024)}), f32[20480]{0:T(1024)}) %all-reduce.4.cloned.1.call-update) | async-done | bytes 81936
  763.1 15.1 %attend_back.1 = bf16[2304,384]{1,0:T(8,128)(2,1)} custom-call(bf16[2304,384]{1,0:T(8,128)(2,1)} %maximum_select_fusion.qkv_ref, bf16[2304,128]{1,0:T(8,128)(2,1)} %maximum_select_fusion.1.grad_ref, s32[2304,1]{1,0:T(8,128)} %broadcast_in_dim.43.seg_q_ref, s32[18,1,512]{2,1,0:T(1,128)} %broadcast_in_dim.18.seg_k_ref), custom_call_target="tpu_custom_call" | custom-call | tf_op jit(solution)/shard_map/attend_back/pallas_call | solution.py:689
  778.2 9.2 convolution_bitcast_fusion
  787.7 7.0 convolution_convert_fusion
  795.1 41.6 %all-reduce = f32[4096]{0:T(1024)S(1)} all-reduce(f32[4096]{0:T(1024)S(1)} %maximum_bitcast_fusion), channel_id=3, replica_groups=mesh['dp'=32] {'dp'}, use_global_device_ids=true, to_apply=%region_12.13.clone | all-reduce | flops 4096 | bytes 32768
  836.7 2.9 select_convert_fusion.2
  840.2 1.1 collective-permute-start.8
  841.3 55.5 %scatter_input.1 = f32[128,2048]{1,0:T(8,128)} custom-call(bf16[2,2,2,2,128,2048]{5,4,3,2,1,0:T(8,128)(2,1)} %bitcast.97), custom_call_target="tpu_custom_call" | custom-call | tf_op jit(solution)/shard_map/scatter_input/pallas_call | solution.py:541
  896.9 2.3 add_convert_fusion.3
  899.2 1.1 convert_add_fusion.1
  901.2 1.6 add_convert_fusion.2
  902.8 1.2 copy.92
  904.0 4.1 add_convert_fusion.1
  908.1 28.4 %weights_back.1 = (bf16[16,64,512]{2,1,0:T(8,128)(2,1)}, bf16[16,64,384]{2,1,0:T(8,128)(2,1)}) custom-call(bf16[16,64,512]{2,1,0:T(8,128)(2,1)} %bitcast.108, bf16[16,64,384]{2,1,0:T(8,128)(2,1)} %bitcast.111), custom_call_target="tpu_custom_call" | custom-call | tf_op jit(solution)/shard_map/weights_back/pallas_call | solution.py:590
  936.5 1.2 fusion.32
  937.8 4.5 convert_add_fusion
  942.3 1.1 copy.94
  943.4 1.1 copy.95
  945.8 2.4 reshape.360
  948.2 1.2 copy.96
  949.4 2.5 copy.106
  951.9 1.3 copy_bitcast_fusion.1
  953.2 1.9 select_select_fusion
  (175 shorter events, 23.5 us)
Async XLA Ops:
  7.2 753.0 %all-reduce.4.cloned.1.call-start = ((), (), s32[]{:S(2)}) async-start(), calls=%async_computation | async-start | bytes 163840
  7.2 234.5 %collective-permute-start.2 = (bf16[64,2048]{1,0:T(8,128)(2,1)}, bf16[64,2048]{1,0:T(8,128)(2,1)}, u32[]{:S(2)}, u32[]{:S(2)}) collective-permute-start(bf16[64,2048]{1,0:T(8,128)(2,1)} %param.26), channel_id=1, source_target_pairs={{0,1},{1,0},{2,3},{3,2},{4,5},{5,4},{6,7},{7,6},{8,9},{9,8},{10,11... | collective-permute-start | bytes 786440 | tf_op jit(solution)/shard_map/ppermute | solution.py:755
  12.7 35.2 %copy-start.11 = (bf16[256,2048]{1,0:T(8,128)(2,1)S(1)}, bf16[256,2048]{1,0:T(8,128)(2,1)}, u32[]{:S(2)}) copy-start(bf16[256,2048]{1,0:T(8,128)(2,1)} %param.32) | copy-start | bytes 3145732
  12.7 37.5 %copy-start.25 = (bf16[64]{0:T(256)(128)(2,1)S(1)}, bf16[64]{0:T(256)(128)(2,1)}, u32[]{:S(2)}) copy-start(bf16[64]{0:T(256)(128)(2,1)} %param.22) | copy-start | bytes 388
  12.7 37.5 %copy-start.26 = (bf16[64]{0:T(256)(128)(2,1)S(1)}, bf16[64]{0:T(256)(128)(2,1)}, u32[]{:S(2)}) copy-start(bf16[64]{0:T(256)(128)(2,1)} %param.25) | copy-start | bytes 388
  12.7 37.5 %copy-start.27 = (bf16[64]{0:T(256)(128)(2,1)S(1)}, bf16[64]{0:T(256)(128)(2,1)}, u32[]{:S(2)}) copy-start(bf16[64]{0:T(256)(128)(2,1)} %param.27) | copy-start | bytes 388
  12.7 37.5 %copy-start.28 = (bf16[64]{0:T(256)(128)(2,1)S(1)}, bf16[64]{0:T(256)(128)(2,1)}, u32[]{:S(2)}) copy-start(bf16[64]{0:T(256)(128)(2,1)} %param.28) | copy-start | bytes 388
  12.7 37.5 %copy-start.29 = (bf16[64]{0:T(256)(128)(2,1)S(1)}, bf16[64]{0:T(256)(128)(2,1)}, u32[]{:S(2)}) copy-start(bf16[64]{0:T(256)(128)(2,1)} %param.29) | copy-start | bytes 388
  12.8 37.5 %copy-start.30 = (bf16[64]{0:T(256)(128)(2,1)S(1)}, bf16[64]{0:T(256)(128)(2,1)}, u32[]{:S(2)}) copy-start(bf16[64]{0:T(256)(128)(2,1)} %param.33) | copy-start | bytes 388
  12.8 37.5 %copy-start.31 = (bf16[64]{0:T(256)(128)(2,1)S(1)}, bf16[64]{0:T(256)(128)(2,1)}, u32[]{:S(2)}) copy-start(bf16[64]{0:T(256)(128)(2,1)} %param.34) | copy-start | bytes 388
  12.8 37.5 %copy-start.32 = (bf16[64]{0:T(256)(128)(2,1)S(1)}, bf16[64]{0:T(256)(128)(2,1)}, u32[]{:S(2)}) copy-start(bf16[64]{0:T(256)(128)(2,1)} %param.35) | copy-start | bytes 388
  12.8 37.5 %copy-start.33 = (bf16[256]{0:T(256)(128)(2,1)S(1)}, bf16[256]{0:T(256)(128)(2,1)}, u32[]{:S(2)}) copy-start(bf16[256]{0:T(256)(128)(2,1)} %param.31) | copy-start | bytes 1540
  13.8 182.5 %copy-start.24 = (s32[32]{0:T(128)S(1)}, s32[32]{0:T(128)}, u32[]{:S(2)}) copy-start(s32[32]{0:T(128)} %param.20) | copy-start | bytes 388
  45.4 199.5 %collective-permute-start = (bf16[1024,384]{0,1:T(8,128)(2,1)S(1)}, bf16[1024,384]{0,1:T(8,128)(2,1)S(1)}, u32[]{:S(2)}, u32[]{:S(2)}) collective-permute-start(bf16[1024,384]{0,1:T(8,128)(2,1)S(1)} %copy.86), channel_id=1, source_target_pairs={{0,16},{1,17},{2,18},{3,19},{4,20},{5,21},{6,22},{7,23},{8,24},{9,... | collective-permute-start | bytes 2359304 | tf_op jit(solution)/shard_map/ppermute | solution.py:754
  47.8 329.8 %collective-permute-start.4 = (bf16[1024,512]{1,0:T(8,128)(2,1)}, bf16[1024,512]{1,0:T(8,128)(2,1)}, u32[]{:S(2)}, u32[]{:S(2)}) collective-permute-start(bf16[1024,512]{1,0:T(8,128)(2,1)} %bitcast.116), channel_id=1, source_target_pairs={{0,16},{1,17},{2,18},{3,19},{4,20},{5,21},{6,22},{7,23},{8,24},{9,... | collective-permute-start | bytes 3145736 | tf_op jit(solution)/shard_map/ppermute | solution.py:763
  47.9 339.1 %collective-permute-start.5 = (bf16[256,2048]{1,0:T(8,128)(2,1)S(1)}, bf16[256,2048]{1,0:T(8,128)(2,1)}, u32[]{:S(2)}, u32[]{:S(2)}) collective-permute-start(bf16[256,2048]{1,0:T(8,128)(2,1)S(1)} %copy-done.11), channel_id=1, source_target_pairs={{0,16},{1,17},{2,18},{3,19},{4,20},{5,21},{6,22},{7,23},{8,24},{9,... | collective-permute-start | bytes 3145736 | tf_op jit(solution)/shard_map/ppermute | solution.py:764
  196.9 44.9 %copy-start.23 = (bf16[64,2048]{1,0:T(8,128)(2,1)S(1)}, bf16[64,2048]{1,0:T(8,128)(2,1)}, u32[]{:S(2)}) copy-start(bf16[64,2048]{1,0:T(8,128)(2,1)} %param.26) | copy-start | bytes 786436
  242.8 38.4 %copy-start.5 = (bf16[64,2048]{1,0:T(8,128)(2,1)}, bf16[64,2048]{1,0:T(8,128)(2,1)S(1)}, u32[]{:S(2)}) copy-start(bf16[64,2048]{1,0:T(8,128)(2,1)S(1)} %get-tuple-element.55) | copy-start | bytes 786436
  243.7 37.5 %collective-permute-start.3 = (bf16[128,2048]{1,0:T(8,128)(2,1)}, bf16[128,2048]{1,0:T(8,128)(2,1)}, u32[]{:S(2)}, u32[]{:S(2)}) collective-permute-start(bf16[128,2048]{1,0:T(8,128)(2,1)} %pad_maximum_fusion.12), channel_id=1, source_target_pairs={{0,16},{2,18},{4,20},{6,22},{8,24},{10,26},{12,28},{14,30},{17,1},... | collective-permute-start | bytes 1572872 | tf_op jit(solution)/shard_map/ppermute | solution.py:762
  245.1 8.6 copy-start.19
  245.1 8.6 copy-start.21
  254.4 14.7 %collective-permute-start.1 = (bf16[256,384]{1,0:T(8,128)(2,1)}, bf16[256,384]{1,0:T(8,128)(2,1)}, u32[]{:S(2)}, u32[]{:S(2)}) collective-permute-start(bf16[256,384]{1,0:T(8,128)(2,1)} %slice_select_fusion.1), channel_id=1, source_target_pairs={{0,16},{1,17},{2,18},{3,19},{4,20},{5,21},{6,22},{7,23},{8,24},{9,... | collective-permute-start | bytes 589832 | tf_op jit(solution)/shard_map/ppermute | solution.py:796
  288.0 43.0 %copy-start.7 = (bf16[128,2048]{1,0:T(8,128)(2,1)S(1)}, bf16[128,2048]{1,0:T(8,128)(2,1)}, u32[]{:S(2)}) copy-start(bf16[128,2048]{1,0:T(8,128)(2,1)} %x_ref.1) | copy-start | bytes 1572868
  379.3 7.7 copy-start.12
  379.3 7.7 copy-start.14
  387.0 9.4 copy-start.34
  389.2 7.2 copy-start.16
  389.2 7.2 copy-start.18
  439.2 2.0 copy-start.8
  443.8 43.5 %copy-start.17 = (bf16[256,2048]{1,0:T(8,128)(2,1)S(1)}, bf16[256,2048]{1,0:T(8,128)(2,1)}, u32[]{:S(2)}) copy-start(bf16[256,2048]{1,0:T(8,128)(2,1)} %copy-done.16) | copy-start | bytes 3145732
  487.3 12.0 %copy-start.2 = (bf16[2,2,2,2,128,2048]{5,4,3,2,1,0:T(8,128)(2,1)S(1)}, bf16[2,2,2,2,128,2048]{5,4,3,2,1,0:T(8,128)(2,1)}, u32[]{:S(2)}) copy-start(bf16[2,2,2,2,128,2048]{5,4,3,2,1,0:T(8,128)(2,1)} %gather_grad_mixed.1) | copy-start | bytes 25165828
  487.3 12.0 %copy-start.35 = (f32[2048,512]{1,0:T(8,128)S(1)}, f32[2048,512]{1,0:T(8,128)}, u32[]{:S(2)}) copy-start(f32[2048,512]{1,0:T(8,128)} %copy-done.34) | copy-start | bytes 12582916
  505.9 9.9 %copy-start.13 = (bf16[1024,512]{1,0:T(8,128)(2,1)S(1)}, bf16[1024,512]{1,0:T(8,128)(2,1)}, u32[]{:S(2)}) copy-start(bf16[1024,512]{1,0:T(8,128)(2,1)} %copy-done.12) | copy-start | bytes 3145732
  505.9 9.9 %copy-start.15 = (bf16[1024,512]{1,0:T(8,128)(2,1)S(1)}, bf16[1024,512]{1,0:T(8,128)(2,1)}, u32[]{:S(2)}) copy-start(bf16[1024,512]{1,0:T(8,128)(2,1)} %copy-done.14) | copy-start | bytes 3145732
  530.7 407.1 %collective-permute-start.11 = (bf16[256,2048]{1,0:T(8,128)(2,1)}, bf16[256,2048]{1,0:T(8,128)(2,1)}, u32[]{:S(2)}, u32[]{:S(2)}) collective-permute-start(bf16[256,2048]{1,0:T(8,128)(2,1)} %select_convert_fusion), channel_id=1, source_target_pairs={{0,16},{1,17},{2,18},{3,19},{4,20},{5,21},{6,22},{7,23},{8,24},{9,... | collective-permute-start | bytes 3145736 | tf_op jit(solution)/shard_map/ppermute | solution.py:836
  533.0 371.0 %collective-permute-start.7 = (bf16[1024,512]{1,0:T(8,128)(2,1)}, bf16[1024,512]{1,0:T(8,128)(2,1)}, u32[]{:S(2)}, u32[]{:S(2)}) collective-permute-start(bf16[1024,512]{1,0:T(8,128)(2,1)} %select_convert_fusion.1), channel_id=1, source_target_pairs={{0,16},{1,17},{2,18},{3,19},{4,20},{5,21},{6,22},{7,23},{8,24},{9,... | collective-permute-start | bytes 3145736 | tf_op jit(solution)/shard_map/ppermute | solution.py:836
  634.4 43.0 %copy-start.1 = (bf16[2048,128]{1,0:T(8,128)(2,1)S(1)}, bf16[2048,128]{1,0:T(8,128)(2,1)}, u32[]{:S(2)}) copy-start(bf16[2048,128]{1,0:T(8,128)(2,1)} %attend.1) | copy-start | bytes 1572868
  677.4 5.8 copy-start
  677.4 5.8 copy-start.6
  686.7 75.4 %collective-permute-start.6 = (bf16[256,128]{1,0:T(8,128)(2,1)S(1)}, bf16[256,128]{1,0:T(8,128)(2,1)S(1)}, u32[]{:S(2)}, u32[]{:S(2)}) collective-permute-start(bf16[256,128]{1,0:T(8,128)(2,1)S(1)} %slice_select_fusion.2), channel_id=1, source_target_pairs={{0,16},{1,17},{2,18},{3,19},{4,20},{5,21},{6,22},{7,23},{8,24},{9,... | collective-permute-start | bytes 196616 | tf_op jit(solution)/shard_map/ppermute | solution.py:796
  687.9 211.4 %collective-permute-start.9 = (bf16[128,2048]{1,0:T(8,128)(2,1)}, bf16[128,2048]{1,0:T(8,128)(2,1)}, u32[]{:S(2)}, u32[]{:S(2)}) collective-permute-start(bf16[128,2048]{1,0:T(8,128)(2,1)} %get-tuple-element.72), channel_id=1, source_target_pairs={{16,0},{18,2},{20,4},{22,6},{24,8},{26,10},{28,12},{30,14},{1,17},... | collective-permute-start | bytes 1572872 | tf_op jit(solution)/shard_map/ppermute | solution.py:860
  778.2 9.2 copy-start.4
  778.2 9.5 copy-start.20
  778.2 9.5 copy-start.22
  840.2 61.0 %collective-permute-start.8 = (bf16[1024,384]{0,1:T(8,128)(2,1)}, bf16[1024,384]{0,1:T(8,128)(2,1)}, u32[]{:S(2)}, u32[]{:S(2)}) collective-permute-start(bf16[1024,384]{0,1:T(8,128)(2,1)} %select_convert_fusion.2), channel_id=1, source_target_pairs={{0,16},{1,17},{2,18},{3,19},{4,20},{5,21},{6,22},{7,23},{8,24},{9,... | collective-permute-start | bytes 2359304 | tf_op jit(solution)/shard_map/ppermute | solution.py:836
  896.9 4.3 copy-start.3
  901.2 52.0 %collective-permute-start.10 = (f32[64,2048]{1,0:T(8,128)}, f32[64,2048]{1,0:T(8,128)}, u32[]{:S(2)}, u32[]{:S(2)}) collective-permute-start(f32[64,2048]{1,0:T(8,128)} %slice_select_fusion), channel_id=1, source_target_pairs={{0,1},{1,0},{2,3},{3,2},{4,5},{5,4},{6,7},{7,6},{8,9},{9,8},{10,11... | collective-permute-start | bytes 1572872 | tf_op jit(solution)/shard_map/ppermute | solution.py:864
  948.1 3.8 copy-start.9
  948.2 3.8 copy-start.10
Sparse Core Ops, SparseCore 0:
  634.5 125.6 all-reduce.3

commit v2 on v1

--- a/solution.py
+++ b/solution.py
@@ -554,50 +554,141 @@
     )(partial.reshape(2, 2, 2, 2, count, width))
 
 
-def exchange_kernel(arrays, *refs):
-    ins, outs = refs[:arrays], refs[arrays : 2 * arrays]
-    local_sem, send_sem, recv_sem = refs[2 * arrays :]
-    device = lax.axis_index("dp")
-    base = device // GROUP * GROUP
-    mine = device % GROUP
-    others = [base + (mine + step) % GROUP for step in range(1, GROUP)]
-    enter(others)
-    copies, locals_ = [], []
-    for at in range(arrays):
+def exchange_blocks(pairs, sems, base, mine, others):
+    local_sem, send_sem, recv_sem = sems
+    copies = []
+    for at, (src, dst) in enumerate(pairs):
         for step, other in enumerate(others):
             copy = push(
-                ins[at].at[other - base],
-                outs[at].at[mine],
+                src.at[other - base],
+                dst.at[mine],
                 send_sem.at[at, step],
                 recv_sem.at[at, step],
                 other,
             )
             copy.start()
             copies.append(copy)
-        local = pltpu.make_async_copy(ins[at].at[mine], outs[at].at[mine], local_sem.at[at])
+        local = pltpu.make_async_copy(src.at[mine], dst.at[mine], local_sem.at[at])
         local.start()
-        locals_.append(local)
-    for copy in locals_:
-        copy.wait()
+        copies.append(local)
+    return copies
+
+
+def group_places():
+    device = lax.axis_index("dp")
+    base = device // GROUP * GROUP
+    mine = device % GROUP
+    others = [base + (mine + step) % GROUP for step in range(1, GROUP)]
+    across = (device + GROUP) % (2 * GROUP)
+    return device // GROUP, base, mine, others, across
+
+
+def weights_out_kernel(
+    qkv_ref, w1_ref, vec_ref, qkv_out, w1_out, vec_out,
+    local_sem, send_sem, recv_sem, vec_local, far_send, far_recv, vec_send, vec_recv,
+):
+    group, base, mine, others, across = group_places()
+    enter(others + [across])
+    far = push(vec_ref, vec_out.at[group, mine], far_send, far_recv, across)
+    far.start()
+    local = pltpu.make_async_copy(vec_ref, vec_out.at[group, mine], vec_local)
+    local.start()
+    copies = exchange_blocks(
+        [(qkv_ref, qkv_out), (w1_ref, w1_out)], (local_sem, send_sem, recv_sem), base, mine, others
+    )
+    local.wait()
+    far.wait()
+    both = vec_out.at[:, mine]
+    for step, other in enumerate(others):
+        copy = push(both, both, vec_send.at[step], vec_recv.at[step], other)
+        copy.start()
+        copies.append(copy)
     for copy in copies:
         copy.wait()
 
 
-def group_exchange(arrays, name, collective_id):
-    count = len(arrays)
+def weights_out(pack_qkv, pack_w1, vector):
     anywhere = pl.BlockSpec(memory_space=pl.ANY)
+    vmem = pl.BlockSpec(memory_space=pltpu.VMEM)
     sems = pltpu.SemaphoreType.DMA
+    peers = GROUP - 1
     return pl.pallas_call(
-        functools.partial(exchange_kernel, count),
-        out_shape=[jax.ShapeDtypeStruct(item.shape, item.dtype) for item in arrays],
-        in_specs=[anywhere] * count,
-        out_specs=[anywhere] * count,
-        scratch_shapes=[sems((count,)), sems((count, GROUP - 1)), sems((count, GROUP - 1))],
+        weights_out_kernel,
+        out_shape=[
+            jax.ShapeDtypeStruct(pack_qkv.shape, pack_qkv.dtype),
+            jax.ShapeDtypeStruct(pack_w1.shape, pack_w1.dtype),
+            jax.ShapeDtypeStruct((2, GROUP) + vector.shape, vector.dtype),
+        ],
+        in_specs=[anywhere, anywhere, vmem],
+        out_specs=[anywhere, anywhere, vmem],
+        scratch_shapes=[
+            sems((2,)), sems((2, peers)), sems((2, peers)),
+            sems, sems, sems, sems((peers,)), sems((peers,)),
+        ],
         compiler_params=pltpu.CompilerParams(
-            collective_id=collective_id, has_side_effects=True, vmem_limit_bytes=VMEM_LIMIT
+            collective_id=1, has_side_effects=True, vmem_limit_bytes=VMEM_LIMIT
         ),
-        name=name,
-    )(*arrays)
+        name="weights_out",
+    )(pack_qkv, pack_w1, vector)
+
+
+def weights_back_kernel(
+    w1_ref, qkv_ref, vec_ref, w1_out, qkv_out, vec_out,
+    arrived, theirs, far_in, local_sem, send_sem, recv_sem, vec_sems, vec_send, vec_recv,
+    far_send, far_recv,
+):
+    group, base, mine, others, across = group_places()
+    enter(others + [across])
+    first = exchange_blocks(
+        [(vec_ref, arrived)], (vec_sems, vec_send, vec_recv), base, mine, others
+    )
+    copies = exchange_blocks(
+        [(w1_ref, w1_out), (qkv_ref, qkv_out)], (local_sem, send_sem, recv_sem), base, mine, others
+    )
+    for copy in first:
+        copy.wait()
+    total = arrived[0]
+    for at in range(1, GROUP):
+        total = total + arrived[at]
+    rows = total.shape[0] // 2
+    low, high = total[:rows], total[rows:]
+    theirs[...] = jnp.where(group == 0, high, low)
+    far = push(theirs, far_in, far_send, far_recv, across)
+    far.start()
+    own = jnp.where(group == 0, low, high)
+    far.wait()
+    vec_out[...] = own + far_in[...]
+    for copy in copies:
+        copy.wait()
+
+
+def weights_back(rows_w1, rows_qkv, vectors):
+    anywhere = pl.BlockSpec(memory_space=pl.ANY)
+    vmem = pl.BlockSpec(memory_space=pltpu.VMEM)
+    sems = pltpu.SemaphoreType.DMA
+    peers = GROUP - 1
+    half = (vectors.shape[1] // 2, vectors.shape[2])
+    return pl.pallas_call(
+        weights_back_kernel,
+        out_shape=[
+            jax.ShapeDtypeStruct(rows_w1.shape, rows_w1.dtype),
+            jax.ShapeDtypeStruct(rows_qkv.shape, rows_qkv.dtype),
+            jax.ShapeDtypeStruct(half, vectors.dtype),
+        ],
+        in_specs=[anywhere, anywhere, vmem],
+        out_specs=[anywhere, anywhere, vmem],
+        scratch_shapes=[
+            pltpu.VMEM(vectors.shape, vectors.dtype),
+            pltpu.VMEM(half, vectors.dtype),
+            pltpu.VMEM(half, vectors.dtype),
+            sems((2,)), sems((2, peers)), sems((2, peers)),
+            sems((1,)), sems((1, peers)), sems((1, peers)), sems, sems,
+        ],
+        compiler_params=pltpu.CompilerParams(
+            collective_id=10, has_side_effects=True, vmem_limit_bytes=VMEM_LIMIT
+        ),
+        name="weights_back",
+    )(rows_w1, rows_qkv, vectors)
 
 
 def window_start(row, total):
@@ -748,7 +839,11 @@
     pack_w1 = w1.reshape(weight_rows, 2, GROUP, unit_rows).transpose(2, 0, 1, 3).reshape(
         GROUP, weight_rows, 2 * unit_rows
     )
-    own_qkv, own_w1 = group_exchange([pack_qkv, pack_w1], "weights_out", 1)
+    vectors = [bq, bv, bo, norm1_gain, norm1_bias, b2, norm2_gain, norm2_bias, b1]
+    sizes = [item.shape[0] for item in vectors]
+    vector = jnp.concatenate(vectors).astype(f32)
+    vector = jnp.pad(vector, (0, 1024 - vector.shape[0])).reshape(8, 128)
+    own_qkv, own_w1, gathered = weights_out(pack_qkv, pack_w1, vector)
     own_qkv = own_qkv.reshape(GROUP * weight_rows, 3 * HEAD_DIM)
     own_w1 = own_w1.reshape(GROUP * weight_rows, 2 * unit_rows)
     full_qkv = in_order(own_qkv, lax.ppermute(own_qkv, "dp", across))
@@ -763,9 +858,7 @@
     full_w1 = in_order(own_w1, lax.ppermute(own_w1, "dp", across))
     full_w2 = in_order(w2, lax.ppermute(w2, "dp", across))
 
-    vectors = [bq, bv, bo, norm1_gain, norm1_bias, b2, norm2_gain, norm2_bias, b1]
-    sizes = [item.shape[0] for item in vectors]
-    gathered = lax.all_gather(jnp.concatenate(vectors), "dp", axis=0).astype(f32)
+    gathered = gathered.reshape(devices, -1)
     whole, at = [], 0
     for size in sizes:
         whole.append(gathered[:, at : at + size].reshape(-1))
@@ -862,14 +955,32 @@
     mine_wo = jnp.where(core == 0, halves[0], halves[1])
     theirs_wo = jnp.where(core == 0, halves[1], halves[0])
     out_wo = jnp.where(core == group, mine_wo, lax.ppermute(theirs_wo, "dp", beside))
-    rows_w1, rows_qkv = group_exchange(
-        [
-            sum_w1.astype(bf16).reshape(GROUP, weight_rows, 2 * unit_rows),
-            sum_qkv.astype(bf16).reshape(GROUP, weight_rows, 3 * HEAD_DIM),
-        ],
-        "weights_back",
-        10,
-    )
+    def place_head(vector):
+        return lax.dynamic_update_slice_in_dim(
+            jnp.zeros((width,), f32), vector, head * HEAD_DIM, 0
+        )
+
+    spread_b1 = lax.dynamic_update_slice_in_dim(
+        jnp.zeros((2, GROUP, unit_rows), f32), grad_b1.reshape(2, 1, unit_rows), member, 1
+    )
+    items = [
+        place_head(grad_bqkv[:HEAD_DIM]), place_head(grad_bqkv[2 * HEAD_DIM :]), grad_bo,
+        grad_gain_one, grad_shift_one, grad_b2, grad_gain_two, grad_shift_two, spread_b1,
+    ]
+    parts = jnp.concatenate([item.reshape(2, GROUP, -1) for item in items], 2)
+    parts = jnp.pad(parts, ((0, 0), (0, 0), (0, 1024 - parts.shape[2])))
+    parts = parts.transpose(1, 0, 2).reshape(GROUP, 16, 128)
+    rows_w1, rows_qkv, sums = weights_back(
+        sum_w1.astype(bf16).reshape(GROUP, weight_rows, 2 * unit_rows),
+        sum_qkv.astype(bf16).reshape(GROUP, weight_rows, 3 * HEAD_DIM),
+        parts,
+    )
+    sums, at = sums.reshape(-1), 0
+    small = []
+    for size in sizes:
+        small.append(sums[at : at + size])
+        at += size
+    out_bq, out_bv, out_bo, out_g1, out_s1, out_b2, out_g2, out_s2, out_b1 = small
     out_w1 = (
         rows_w1.reshape(GROUP, weight_rows, 2, unit_rows)
         .transpose(1, 2, 0, 3)
@@ -885,31 +996,6 @@
         for at in range(3)
     ]
 
-    def place_head(vector):
-        return lax.dynamic_update_slice_in_dim(
-            jnp.zeros((width,), f32), vector, head * HEAD_DIM, 0
-        )
-
-    spread_b1 = lax.dynamic_update_slice_in_dim(
-        jnp.zeros((2, GROUP, unit_rows), f32), grad_b1.reshape(2, 1, unit_rows), member, 1
-    )
-
-    def reduce_vectors(items):
-        parts = jnp.concatenate([item.reshape(devices, -1) for item in items], 1)
-        mine = lax.psum_scatter(parts.reshape(-1), "dp", scatter_dimension=0, tiled=True)
-        result, at = [], 0
-        for item in items:
-            size = item.size // devices
-            result.append(mine[at : at + size])
-            at += size
-        return result
-
-    out_b1, out_b2, out_g2, out_s2, out_bo, out_g1, out_s1 = reduce_vectors(
-        [spread_b1, grad_b2, grad_gain_two, grad_shift_two, grad_bo, grad_gain_one, grad_shift_one]
-    )
-    out_bq, out_bv = reduce_vectors(
-        [place_head(grad_bqkv[:HEAD_DIM]), place_head(grad_bqkv[2 * HEAD_DIM :])]
-    )
     return (
         output, input_grad, out_q, out_bq, out_k, out_v, out_bv, out_wo, out_bo, out_g1, out_s1,
         out_w1, out_b1, out_w2, out_b2, out_g2, out_s2,

time: 972 us -> 815 us (0.84)
  blocking collectives: 187 us -> 0 us
  Pallas kernels: 494 us -> 601 us
  waiting for transfers between devices: 76 us -> 7.69 us
  between operations: 15.4 us -> 1.66 us
    all_gather x1 -> x0, blocking collectives: 146 us -> none  [grouped_device(): lax.all_gather(jnp.concatenate(vectors), 'dp', axis=0).astype(f32)]
    pallas_call x4, Pallas kernels: 175 us -> 277 us  [group_gather(): pl.pallas_call(gather_kernel, out_shape=jax.ShapeDtypeStruct((2, 2, 2, 2,...]
    unnamed x2 -> x0, waiting for transfers between devices: 68.4 us -> none
    unnamed x1 -> x0, blocking collectives: 41.6 us -> none
  transfers between devices with their start and end apart: 13 -> 12, of which waited for: 2 -> 2; matrix products, arithmetic and copies ran while one was open for 12% -> 15% of each run, Pallas kernels for 42% -> 64%
where the time goes in v2:
time: 815 us; the launch traced here: 806 us
  Pallas kernels  601 us (74%)
  matrix products  92 us (11%)
  other arithmetic  49.6 us (6%)
  local copies, waits for them, and re-layouts  37.3 us (5%)
  starting transfers between devices  16.4 us (2%)
    pallas_call x4, Pallas kernels, group_gather(): pl.pallas_call(gather_kernel, out_shape=jax.ShapeDtypeStruct((2, 2, 2, 2,...  277 us
    pallas_call x4, Pallas kernels, group_scatter(): pl.pallas_call(scatter_kernel, out_shape=jax.ShapeDtypeStruct((count, wid...  235 us
    pallas_call x1, Pallas kernels, weights_back(): pl.pallas_call(weights_back_kernel, out_shape=[jax.ShapeDtypeStruct(rows_...  32.4 us
    pallas_call x1, Pallas kernels, weights_out(): pl.pallas_call(weights_out_kernel, out_shape=[jax.ShapeDtypeStruct(pack_q...  32.4 us
  transfers between devices with their start and end apart: 12, of which 2 were waited for; matrix products, arithmetic and copies ran while one was open for 15% of the time, Pallas kernels for 64%

profile of v2, /device:TPU:7, one launch (start us, length us, event | category | flops | bytes accessed | tf_op | source)
XLA Modules:
  0.0 806.0 jit_solution(12798590069873844144)
XLA Ops:
  1.4 6.1 concatenate.37
  11.3 1.5 copy.101
  12.8 1.0 copy.112
  13.8 1.5 reshape.330.w1_ref
  16.3 32.4 %weights_out.1 = (bf16[16,64,384]{2,1,0:T(8,128)(2,1)}, bf16[16,64,512]{2,1,0:T(8,128)(2,1)}, f32[2,16,8,128]{3,2,1,0:T(8,128)}) custom-call(bf16[16,64,384]{2,1,0:T(8,128)(2,1)} %pad_maximum_fusion.11.qkv_ref, bf16[16,64,512]{2,1,0:T(8,128)(2,1)} %reshape.330.w1_ref, f32[8,128]{1,0:T(8,128)} %bitcast_convert_fusion.vec_ref), custom_call_target="tpu_custom_call" | custom-call | tf_op jit(solution)/shard_map/weights_out/pallas_call | solution.py:615
  48.7 1.4 copy.78
  50.9 1.6 collective-permute-start.4
  55.0 146.2 %gather_tokens.1 = bf16[2,2,2,2,128,2048]{5,4,3,2,1,0:T(8,128)(2,1)} custom-call(bf16[128,2048]{1,0:T(8,128)(2,1)} %x_ref.1), custom_call_target="tpu_custom_call" | custom-call | tf_op jit(solution)/shard_map/gather_tokens/pallas_call | solution.py:419
  203.4 1.3 collective-permute-start.3
  204.8 8.5 %fusion.7 = bf16[2048,384]{1,0:T(8,128)(2,1)S(1)} fusion(bf16[2048,2048]{1,0:T(8,128)(2,1)} %bitcast.106, f32[384]{0:T(512)S(1)} %pad_maximum_fusion.13, bf16[1024,384]{0,1:T(8,128)(2,1)S(1)} %get-tuple-element.53, bf16[1024,384]{0,1:T(8,128)(2,1)S(1)} %get-tuple-element.52), kind=kOutput, calls=%fused_computation.18 | convolution fusion | flops 3225944064 | bytes 11535872 | tf_op jit(solution)/shard_map/dot_general | solution.py:895
  214.1 3.7 collective-permute-start.1
  219.0 2.1 broadcast_in_dim.43.seg_q_ref
  221.1 6.8 collective-permute-done.1
  227.9 2.8 maximum_select_fusion.qkv_ref
  230.7 9.3 %attend.1 = bf16[2048,128]{1,0:T(8,128)(2,1)} custom-call(s32[1]{0:T(128)} %bitcast.offset_ref, bf16[2304,384]{1,0:T(8,128)(2,1)} %maximum_select_fusion.qkv_ref, s32[2304,1]{1,0:T(8,128)} %broadcast_in_dim.43.seg_q_ref, s32[18,1,512]{2,1,0:T(1,128)} %broadcast_in_dim.18.seg_k_ref), custom_call_target="tpu_custom_call" | custom-call | tf_op jit(solution)/shard_map/attend/pallas_call | solution.py:766
  240.1 6.8 convolution_convert_fusion.3
  246.8 40.4 %scatter_branch.1 = f32[128,2048]{1,0:T(8,128)} custom-call(bf16[2,2,2,2,128,2048]{5,4,3,2,1,0:T(8,128)(2,1)} %bitcast.102), custom_call_target="tpu_custom_call" | custom-call | tf_op jit(solution)/shard_map/scatter_branch/pallas_call | solution.py:541
  287.3 1.4 fusion.31
  289.0 1.1 fusion.16.x_ref
  290.1 43.9 %gather_hidden.1 = bf16[2,2,2,2,128,2048]{5,4,3,2,1,0:T(8,128)(2,1)} custom-call(bf16[128,2048]{1,0:T(8,128)(2,1)} %fusion.16.x_ref), custom_call_target="tpu_custom_call" | custom-call | tf_op jit(solution)/shard_map/gather_hidden/pallas_call | solution.py:419
  334.0 1.7 broadcast_select_fusion.3
  335.7 7.6 fusion.9
  343.4 2.2 broadcast_select_fusion.1
  345.6 7.2 convolution_convert_fusion.2
  352.8 42.6 %scatter_mixed.1 = f32[128,2048]{1,0:T(8,128)} custom-call(bf16[2,2,2,2,128,2048]{5,4,3,2,1,0:T(8,128)(2,1)} %bitcast.105), custom_call_target="tpu_custom_call" | custom-call | tf_op jit(solution)/shard_map/scatter_mixed/pallas_call | solution.py:541
  395.5 1.7 fusion.30
  397.9 1.3 fusion.29
  400.1 44.4 %gather_grad_mixed.1 = bf16[2,2,2,2,128,2048]{5,4,3,2,1,0:T(8,128)(2,1)} custom-call(bf16[128,2048]{1,0:T(8,128)(2,1)} %get-tuple-element.36.x_ref), custom_call_target="tpu_custom_call" | custom-call | tf_op jit(solution)/shard_map/gather_grad_mixed/pallas_call | solution.py:419
  444.6 11.9 %convert_reduce_fusion = (f32[512]{0:T(512)S(1)}, bf16[2048,512]{1,0:T(8,128)(2,1)S(1)}) fusion(f32[2048,512]{1,0:T(8,128)} %copy-done.25, f32[512]{0:T(512)S(1)} %bitcast.144, bf16[2048,2048]{1,0:T(8,128)(2,1)} %bitcast.110, bf16[256,2048]{1,0:T(8,128)(2,1)} %copy-done.18, bf16[256,2048]{1,0:T(8,128)(2,1)S(1)} %copy-done.17), kind=kOutput, calls=%fused_computation.13 | convolution fusion | flops 4323278336 | bytes 16781312 | tf_op jit(solution)/shard_map/td,fd->tf/dot_general | solution.py:916
  456.5 6.5 fusion.27
  463.0 9.9 %fusion.36 = f32[2048,512]{1,0:T(8,128)} fusion(bf16[2048,2048]{1,0:T(8,128)(2,1)} %bitcast.109, bf16[2048,512]{1,0:T(8,128)(2,1)S(1)} %get-tuple-element.77), kind=kOutput, calls=%fused_computation.123 | convolution fusion | flops 4294967296 | bytes 14680064 | tf_op jit(solution)/shard_map/td,tf->df/dot_general | solution.py:923
  473.0 8.2 %convolution_convert_fusion.1 = bf16[2048,2048]{1,0:T(8,128)(2,1)} fusion(bf16[2048,512]{1,0:T(8,128)(2,1)S(1)} %get-tuple-element.77, bf16[1024,512]{1,0:T(8,128)(2,1)S(1)} %copy-done.15, bf16[1024,512]{1,0:T(8,128)(2,1)S(1)} %copy-done.13), kind=kOutput, calls=%fused_computation.1 | convolution fusion | flops 4303355904 | bytes 12582912 | tf_op jit(solution)/shard_map/tf,df->td/dot_general | solution.py:919
  481.4 3.4 select_convert_fusion.1
  484.8 3.4 select_convert_fusion
  488.2 1.4 collective-permute-start.11
  489.6 1.0 collective-permute-start.7
  490.6 97.0 %scatter_grad_hidden.1 = f32[128,2048]{1,0:T(8,128)} custom-call(bf16[2,2,2,2,128,2048]{5,4,3,2,1,0:T(8,128)(2,1)} %bitcast.104), custom_call_target="tpu_custom_call" | custom-call | tf_op jit(solution)/shard_map/scatter_grad_hidden/pallas_call | solution.py:541
  587.6 1.8 multiply_reduce_fusion
  591.1 42.4 %gather_grad_branch.1 = bf16[2,2,2,2,128,2048]{5,4,3,2,1,0:T(8,128)(2,1)} custom-call(bf16[128,2048]{1,0:T(8,128)(2,1)} %get-tuple-element.38.x_ref), custom_call_target="tpu_custom_call" | custom-call | tf_op jit(solution)/shard_map/gather_grad_branch/pallas_call | solution.py:419
  633.5 5.6 fusion.35
  639.3 3.5 convolution_convert_fusion.4
  643.6 4.3 collective-permute-start.9
  649.7 15.1 %attend_back.1 = bf16[2304,384]{1,0:T(8,128)(2,1)} custom-call(bf16[2304,384]{1,0:T(8,128)(2,1)} %maximum_select_fusion.qkv_ref, bf16[2304,128]{1,0:T(8,128)(2,1)} %maximum_select_fusion.1.grad_ref, s32[2304,1]{1,0:T(8,128)} %broadcast_in_dim.43.seg_q_ref, s32[18,1,512]{2,1,0:T(1,128)} %broadcast_in_dim.18.seg_k_ref), custom_call_target="tpu_custom_call" | custom-call | tf_op jit(solution)/shard_map/attend_back/pallas_call | solution.py:780
  664.8 9.2 %convolution_bitcast_fusion = f32[2048,384]{0,1:T(8,128)} fusion(bf16[2048,2048]{1,0:T(8,128)(2,1)} %bitcast.107, bf16[2304,384]{1,0:T(8,128)(2,1)} %attend_back.1, s32[]{:T(128)S(6)} %select_n.194), kind=kOutput, calls=%fused_computation.17 | convolution fusion | flops 3221225472 | bytes 13107204 | tf_op jit(solution)/shard_map/td,tf->df/dot_general | solution.py:947
  674.4 7.0 convolution_convert_fusion
  681.7 2.9 select_convert_fusion.2
  685.6 55.0 %scatter_input.1 = f32[128,2048]{1,0:T(8,128)} custom-call(bf16[2,2,2,2,128,2048]{5,4,3,2,1,0:T(8,128)(2,1)} %bitcast.103), custom_call_target="tpu_custom_call" | custom-call | tf_op jit(solution)/shard_map/scatter_input/pallas_call | solution.py:541
  740.6 2.3 add_convert_fusion.3
  742.9 1.1 convert_add_fusion.1
  745.0 1.6 add_convert_fusion.2
  746.6 1.2 copy.84
  747.7 4.1 add_convert_fusion.1
  751.9 32.4 %weights_back.1 = (bf16[16,64,512]{2,1,0:T(8,128)(2,1)}, bf16[16,64,384]{2,1,0:T(8,128)(2,1)}, f32[8,128]{1,0:T(8,128)}) custom-call(bf16[16,64,512]{2,1,0:T(8,128)(2,1)} %bitcast.114, bf16[16,64,384]{2,1,0:T(8,128)(2,1)} %bitcast.117, f32[16,16,128]{2,1,0:T(8,128)} %reshape.359.vec_ref), custom_call_target="tpu_custom_call" | custom-call | tf_op jit(solution)/shard_map/weights_back/pallas_call | solution.py:671
  784.3 1.6 fusion.34
  785.9 1.2 fusion.32
  787.2 4.5 convert_add_fusion
  791.7 1.2 slice_bitcast_fusion
  792.9 1.1 copy.94
  794.0 1.1 copy.95
  796.4 2.4 reshape.370
  798.8 1.2 copy.96
  800.0 2.5 copy.106
  802.5 1.3 copy_bitcast_fusion.1
  803.9 1.9 select_select_fusion
  (158 shorter events, 23.5 us)
Async XLA Ops:
  0.7 200.8 %collective-permute-start.2 = (bf16[64,2048]{1,0:T(8,128)(2,1)}, bf16[64,2048]{1,0:T(8,128)(2,1)}, u32[]{:S(2)}, u32[]{:S(2)}) collective-permute-start(bf16[64,2048]{1,0:T(8,128)(2,1)} %param.26), channel_id=1, source_target_pairs={{0,1},{1,0},{2,3},{3,2},{4,5},{5,4},{6,7},{7,6},{8,9},{9,8},{10,11... | collective-permute-start | bytes 786440 | tf_op jit(solution)/shard_map/ppermute | solution.py:850
  12.8 39.8 %copy-start.11 = (bf16[256,2048]{1,0:T(8,128)(2,1)S(1)}, bf16[256,2048]{1,0:T(8,128)(2,1)}, u32[]{:S(2)}) copy-start(bf16[256,2048]{1,0:T(8,128)(2,1)} %param.32) | copy-start | bytes 3145732
  13.8 40.6 %copy-start.24 = (s32[32]{0:T(128)S(1)}, s32[32]{0:T(128)}, u32[]{:S(2)}) copy-start(s32[32]{0:T(128)} %param.20) | copy-start | bytes 388
  50.1 154.5 %collective-permute-start = (bf16[1024,384]{0,1:T(8,128)(2,1)S(1)}, bf16[1024,384]{0,1:T(8,128)(2,1)S(1)}, u32[]{:S(2)}, u32[]{:S(2)}) collective-permute-start(bf16[1024,384]{0,1:T(8,128)(2,1)S(1)} %copy.78), channel_id=1, source_target_pairs={{0,16},{1,17},{2,18},{3,19},{4,20},{5,21},{6,22},{7,23},{8,24},{9,... | collective-permute-start | bytes 2359304 | tf_op jit(solution)/shard_map/ppermute | solution.py:849
  50.9 283.1 %collective-permute-start.4 = (bf16[1024,512]{1,0:T(8,128)(2,1)}, bf16[1024,512]{1,0:T(8,128)(2,1)}, u32[]{:S(2)}, u32[]{:S(2)}) collective-permute-start(bf16[1024,512]{1,0:T(8,128)(2,1)} %bitcast.122), channel_id=1, source_target_pairs={{0,16},{1,17},{2,18},{3,19},{4,20},{5,21},{6,22},{7,23},{8,24},{9,... | collective-permute-start | bytes 3145736 | tf_op jit(solution)/shard_map/ppermute | solution.py:858
  52.6 290.8 %collective-permute-start.5 = (bf16[256,2048]{1,0:T(8,128)(2,1)S(1)}, bf16[256,2048]{1,0:T(8,128)(2,1)}, u32[]{:S(2)}, u32[]{:S(2)}) collective-permute-start(bf16[256,2048]{1,0:T(8,128)(2,1)S(1)} %copy-done.11), channel_id=1, source_target_pairs={{0,16},{1,17},{2,18},{3,19},{4,20},{5,21},{6,22},{7,23},{8,24},{9,... | collective-permute-start | bytes 3145736 | tf_op jit(solution)/shard_map/ppermute | solution.py:859
  55.0 146.5 %copy-start.23 = (bf16[64,2048]{1,0:T(8,128)(2,1)S(1)}, bf16[64,2048]{1,0:T(8,128)(2,1)}, u32[]{:S(2)}) copy-start(bf16[64,2048]{1,0:T(8,128)(2,1)} %param.26) | copy-start | bytes 786436
  202.5 37.6 %copy-start.5 = (bf16[64,2048]{1,0:T(8,128)(2,1)}, bf16[64,2048]{1,0:T(8,128)(2,1)S(1)}, u32[]{:S(2)}) copy-start(bf16[64,2048]{1,0:T(8,128)(2,1)S(1)} %get-tuple-element.59) | copy-start | bytes 786436
  203.4 36.7 %collective-permute-start.3 = (bf16[128,2048]{1,0:T(8,128)(2,1)}, bf16[128,2048]{1,0:T(8,128)(2,1)}, u32[]{:S(2)}, u32[]{:S(2)}) collective-permute-start(bf16[128,2048]{1,0:T(8,128)(2,1)} %pad_maximum_fusion.12), channel_id=1, source_target_pairs={{0,16},{2,18},{4,20},{6,22},{8,24},{10,26},{12,28},{14,30},{17,1},... | collective-permute-start | bytes 1572872 | tf_op jit(solution)/shard_map/ppermute | solution.py:857
  204.8 8.6 %copy-start.19 = (bf16[1024,384]{0,1:T(8,128)(2,1)}, bf16[1024,384]{0,1:T(8,128)(2,1)S(1)}, u32[]{:S(2)}) copy-start(bf16[1024,384]{0,1:T(8,128)(2,1)S(1)} %get-tuple-element.52) | copy-start | bytes 2359300
  204.8 8.6 %copy-start.21 = (bf16[1024,384]{0,1:T(8,128)(2,1)}, bf16[1024,384]{0,1:T(8,128)(2,1)S(1)}, u32[]{:S(2)}) copy-start(bf16[1024,384]{0,1:T(8,128)(2,1)S(1)} %get-tuple-element.53) | copy-start | bytes 2359300
  214.1 13.8 %collective-permute-start.1 = (bf16[256,384]{1,0:T(8,128)(2,1)}, bf16[256,384]{1,0:T(8,128)(2,1)}, u32[]{:S(2)}, u32[]{:S(2)}) collective-permute-start(bf16[256,384]{1,0:T(8,128)(2,1)} %slice_select_fusion.1), channel_id=1, source_target_pairs={{0,16},{1,17},{2,18},{3,19},{4,20},{5,21},{6,22},{7,23},{8,24},{9,... | collective-permute-start | bytes 589832 | tf_op jit(solution)/shard_map/ppermute | solution.py:889
  246.8 40.5 %copy-start.7 = (bf16[128,2048]{1,0:T(8,128)(2,1)S(1)}, bf16[128,2048]{1,0:T(8,128)(2,1)}, u32[]{:S(2)}) copy-start(bf16[128,2048]{1,0:T(8,128)(2,1)} %x_ref.1) | copy-start | bytes 1572868
  335.7 7.7 copy-start.12
  335.7 7.7 copy-start.14
  343.4 9.4 %copy-start.25 = (f32[2048,512]{1,0:T(8,128)}, f32[2048,512]{1,0:T(8,128)S(1)}, u32[]{:S(2)}) copy-start(f32[2048,512]{1,0:T(8,128)S(1)} %fusion.9) | copy-start | bytes 12582916
  345.6 7.2 copy-start.16
  345.6 7.2 copy-start.18
  395.4 2.0 copy-start.8
  400.1 44.4 %copy-start.17 = (bf16[256,2048]{1,0:T(8,128)(2,1)S(1)}, bf16[256,2048]{1,0:T(8,128)(2,1)}, u32[]{:S(2)}) copy-start(bf16[256,2048]{1,0:T(8,128)(2,1)} %copy-done.16) | copy-start | bytes 3145732
  444.6 12.0 %copy-start.2 = (bf16[2,2,2,2,128,2048]{5,4,3,2,1,0:T(8,128)(2,1)S(1)}, bf16[2,2,2,2,128,2048]{5,4,3,2,1,0:T(8,128)(2,1)}, u32[]{:S(2)}) copy-start(bf16[2,2,2,2,128,2048]{5,4,3,2,1,0:T(8,128)(2,1)} %gather_grad_mixed.1) | copy-start | bytes 25165828
  444.6 12.0 %copy-start.26 = (f32[2048,512]{1,0:T(8,128)S(1)}, f32[2048,512]{1,0:T(8,128)}, u32[]{:S(2)}) copy-start(f32[2048,512]{1,0:T(8,128)} %copy-done.25) | copy-start | bytes 12582916
  463.0 9.9 %copy-start.13 = (bf16[1024,512]{1,0:T(8,128)(2,1)S(1)}, bf16[1024,512]{1,0:T(8,128)(2,1)}, u32[]{:S(2)}) copy-start(bf16[1024,512]{1,0:T(8,128)(2,1)} %copy-done.12) | copy-start | bytes 3145732
  463.0 9.9 %copy-start.15 = (bf16[1024,512]{1,0:T(8,128)(2,1)S(1)}, bf16[1024,512]{1,0:T(8,128)(2,1)}, u32[]{:S(2)}) copy-start(bf16[1024,512]{1,0:T(8,128)(2,1)} %copy-done.14) | copy-start | bytes 3145732
  488.2 299.0 %collective-permute-start.11 = (bf16[256,2048]{1,0:T(8,128)(2,1)}, bf16[256,2048]{1,0:T(8,128)(2,1)}, u32[]{:S(2)}, u32[]{:S(2)}) collective-permute-start(bf16[256,2048]{1,0:T(8,128)(2,1)} %select_convert_fusion), channel_id=1, source_target_pairs={{0,16},{1,17},{2,18},{3,19},{4,20},{5,21},{6,22},{7,23},{8,24},{9,... | collective-permute-start | bytes 3145736 | tf_op jit(solution)/shard_map/ppermute | solution.py:929
  489.6 258.2 %collective-permute-start.7 = (bf16[1024,512]{1,0:T(8,128)(2,1)}, bf16[1024,512]{1,0:T(8,128)(2,1)}, u32[]{:S(2)}, u32[]{:S(2)}) collective-permute-start(bf16[1024,512]{1,0:T(8,128)(2,1)} %select_convert_fusion.1), channel_id=1, source_target_pairs={{0,16},{1,17},{2,18},{3,19},{4,20},{5,21},{6,22},{7,23},{8,24},{9,... | collective-permute-start | bytes 3145736 | tf_op jit(solution)/shard_map/ppermute | solution.py:929
  591.0 42.4 %copy-start.1 = (bf16[2048,128]{1,0:T(8,128)(2,1)S(1)}, bf16[2048,128]{1,0:T(8,128)(2,1)}, u32[]{:S(2)}) copy-start(bf16[2048,128]{1,0:T(8,128)(2,1)} %attend.1) | copy-start | bytes 1572868
  633.5 5.8 copy-start
  633.5 5.8 copy-start.6
  642.8 6.0 collective-permute-start.6
  643.6 99.3 %collective-permute-start.9 = (bf16[128,2048]{1,0:T(8,128)(2,1)}, bf16[128,2048]{1,0:T(8,128)(2,1)}, u32[]{:S(2)}, u32[]{:S(2)}) collective-permute-start(bf16[128,2048]{1,0:T(8,128)(2,1)} %get-tuple-element.78), channel_id=1, source_target_pairs={{16,0},{18,2},{20,4},{22,6},{24,8},{26,10},{28,12},{30,14},{1,17},... | collective-permute-start | bytes 1572872 | tf_op jit(solution)/shard_map/ppermute | solution.py:953
  664.8 9.2 %copy-start.4 = (bf16[2304,384]{1,0:T(8,128)(2,1)S(1)}, bf16[2304,384]{1,0:T(8,128)(2,1)}, u32[]{:S(2)}) copy-start(bf16[2304,384]{1,0:T(8,128)(2,1)} %attend_back.1) | copy-start | bytes 5308420
  664.8 9.6 %copy-start.20 = (bf16[1024,384]{0,1:T(8,128)(2,1)S(1)}, bf16[1024,384]{0,1:T(8,128)(2,1)}, u32[]{:S(2)}) copy-start(bf16[1024,384]{0,1:T(8,128)(2,1)} %copy-done.19) | copy-start | bytes 2359300
  664.8 9.6 %copy-start.22 = (bf16[1024,384]{0,1:T(8,128)(2,1)S(1)}, bf16[1024,384]{0,1:T(8,128)(2,1)}, u32[]{:S(2)}) copy-start(bf16[1024,384]{0,1:T(8,128)(2,1)} %copy-done.21) | copy-start | bytes 2359300
  685.6 59.4 %collective-permute-start.8 = (bf16[1024,384]{0,1:T(8,128)(2,1)}, bf16[1024,384]{0,1:T(8,128)(2,1)}, u32[]{:S(2)}, u32[]{:S(2)}) collective-permute-start(bf16[1024,384]{0,1:T(8,128)(2,1)} %select_convert_fusion.2), channel_id=1, source_target_pairs={{0,16},{1,17},{2,18},{3,19},{4,20},{5,21},{6,22},{7,23},{8,24},{9,... | collective-permute-start | bytes 2359304 | tf_op jit(solution)/shard_map/ppermute | solution.py:929
  740.6 4.4 copy-start.3
  745.0 58.9 %collective-permute-start.10 = (f32[64,2048]{1,0:T(8,128)}, f32[64,2048]{1,0:T(8,128)}, u32[]{:S(2)}, u32[]{:S(2)}) collective-permute-start(f32[64,2048]{1,0:T(8,128)} %slice_select_fusion), channel_id=1, source_target_pairs={{0,1},{1,0},{2,3},{3,2},{4,5},{5,4},{6,7},{7,6},{8,9},{9,8},{10,11... | collective-permute-start | bytes 1572872 | tf_op jit(solution)/shard_map/ppermute | solution.py:957
  798.8 3.8 copy-start.9
  798.8 3.8 copy-start.10

commit v3 on v2

--- a/solution.py
+++ b/solution.py
@@ -786,6 +786,353 @@
         compiler_params=pltpu.CompilerParams(vmem_limit_bytes=VMEM_LIMIT),
         name="attend_back",
     )(qkv, grads, seg_q, seg_k)
+
+
+CHUNKS = 4
+COLUMNS = ((0, 768), (768, 640), (1408, 640))
+SPLIT = 256
+
+
+def step_through(flows):
+    waiting, alive = list(flows), []
+    while waiting or alive:
+        if waiting:
+            alive.append(waiting.pop(0))
+        alive = [flow for flow in alive if next(flow, "done") != "done"]
+
+
+class Traffic:
+    def __init__(self, sems):
+        self.hop_send, self.hop_recv, self.pair_send, self.pair_recv = sems
+        device = lax.axis_index("dp")
+        self.core = device % 2
+        self.bits = chip_bits(device)
+        self.partners = [flip(device, 1), flip(device, 2), flip(device, 3)]
+        self.pair = flip(device, 0)
+
+    def chips(self, ref, values, columns):
+        return ref.at[values[2], values[1], values[0], :, columns]
+
+    def push(self, src, dst, stage, chunk, part, step):
+        copy = push(
+            src, dst,
+            self.hop_send.at[stage, chunk, part, step],
+            self.hop_recv.at[stage, chunk, part, step],
+            self.partners[ORDERS[part][step]],
+        )
+        copy.start()
+        return copy
+
+    def gather(self, slots, stage, chunk):
+        mine = slots.at[self.core]
+        hops = {}
+        for step in range(3):
+            for part, (first, count) in enumerate(COLUMNS):
+                if step:
+                    hops[part, step - 1].wait_recv()
+                values = list(self.bits)
+                for dim in ORDERS[part][:step]:
+                    values[dim] = slice(None)
+                view = self.chips(mine, values, pl.ds(first, count))
+                hops[part, step] = self.push(view, view, stage, chunk, part, step)
+            yield
+        for part in range(3):
+            hops[part, 2].wait_recv()
+        share = push(
+            mine, mine, self.pair_send.at[stage, chunk], self.pair_recv.at[stage, chunk], self.pair
+        )
+        share.start()
+        for copy in hops.values():
+            copy.wait_send()
+        self.share = share
+
+    def scatter(self, own, pair_in, sums, incoming, share, stage, chunk, finish):
+        rows = own.shape[-2]
+        f32 = jnp.float32
+        hops = {}
+
+        share.wait()
+        for step in range(4):
+            for part, (first, count) in enumerate(COLUMNS):
+                order = ORDERS[part]
+                columns = pl.ds(first, count)
+                if step:
+                    hops[part, step - 1].wait_recv()
+                values = list(self.bits)
+                free = ()
+                if step < 3:
+                    values[order[step]] = 1 - self.bits[order[step]]
+                    free = order[step + 1 :]
+                for mask in range(1 << len(free)):
+                    slot = list(values)
+                    for place, dim in enumerate(free):
+                        slot[dim] = (mask >> place) & 1
+                    where = (slot[2], slot[1], slot[0])
+                    for row in range(0, rows, 16):
+                        at = (slice(row, row + 16), columns)
+                        total = own[where + at].astype(f32) + pair_in[where + at].astype(f32)
+                        for back in range(step):
+                            left = [slot[dim] for dim in (2, 1, 0) if dim not in order[: back + 1]]
+                            total = total + incoming[back][tuple(left) + at].astype(f32)
+                        if step < 3:
+                            sums[where + at] = total.astype(sums.dtype)
+                        else:
+                            finish(row, first, count, total)
+                if step == 3:
+                    continue
+                for dim in free:
+                    values[dim] = slice(None)
+                left = tuple(slice(None) for _ in free)
+                hops[part, step] = self.push(
+                    self.chips(sums, values, columns),
+                    incoming[step].at[left + (slice(None), columns)],
+                    stage, chunk, part, step,
+                )
+            if step < 3:
+                yield
+        for copy in hops.values():
+            copy.wait_send()
+
+
+def ff_kernel(
+    low_ref, hid_ref, cot_ref, w1_ref, w2_ref, b1_ref, par_ref,
+    out_ref, dhid_ref, vec_ref, gb1_ref, gw2_ref, gw1_ref,
+    all_h, all_m, own_part, far_part, pair_in, sums, in_one, in_two, in_three,
+    up_ref, act_ref, act_t, dup_ref, dup_t, res_ref, stage_ref,
+    hop_send, hop_recv, pair_send, pair_recv, out_sems,
+):
+    f32, low = jnp.float32, low_ref.dtype
+    block, width = low_ref.shape
+    rows = block // CHUNKS
+    half_rows = rows * GROUP // 2
+    units = w1_ref.shape[1]
+    net = Traffic((hop_send, hop_recv, pair_send, pair_recv))
+    core, bits = net.core, net.bits
+    own_slot = (core, bits[2], bits[1], bits[0])
+    enter(net.partners + [net.pair])
+    vec_ref[...] = jnp.zeros_like(vec_ref)
+    gb1_ref[...] = jnp.zeros_like(gb1_ref)
+    for chunk in range(CHUNKS):
+        all_h[(chunk,) + own_slot] = low_ref[chunk * rows : (chunk + 1) * rows, :]
+
+    def row_at(chunk, side):
+        return pl.multiple_of((chunk * 2 + side) * half_rows, half_rows)
+
+    def flat(ref, chunk, side, columns=slice(None)):
+        return ref[chunk, side, :, :, :, :, columns].reshape(half_rows, -1)
+
+    def tiles(count, body):
+        def step(at, carry):
+            body(pl.ds(pl.multiple_of(at * SPLIT, SPLIT), SPLIT))
+            return carry
+
+        lax.fori_loop(0, count // SPLIT, step, 0)
+
+    def upward(chunk, side):
+        here = pl.ds(row_at(chunk, side), half_rows)
+
+        def body(columns):
+            up = jnp.dot(flat(all_h, chunk, side), w1_ref[:, columns], preferred_element_type=f32)
+            up = up + b1_ref[0:1, columns]
+            up_ref[here, columns] = up
+            act = gelu_tanh(up)
+            act_ref[:, columns] = act.astype(low)
+            act_t[columns, here] = act.T.astype(low)
+
+        tiles(units, body)
+
+    def downward(dst):
+        def body(columns):
+            part = jnp.dot(act_ref[...], w2_ref[:, columns], preferred_element_type=f32)
+            dst[:, :, :, :, columns] = part.astype(low).reshape(2, 2, 2, rows, SPLIT)
+
+        tiles(width, body)
+
+    def up_back(chunk, side):
+        here = pl.ds(row_at(chunk, side), half_rows)
+
+        def body(columns):
+            grad = lax.dot_general(
+                flat(all_m, chunk, side), w2_ref[columns, :],
+                (((1,), (1,)), ((), ())), preferred_element_type=f32,
+            )
+            up = up_ref[here, columns]
+            inner = 0.7978845608028654 * (up + 0.044715 * (up * up * up))
+            tanh = jnp.tanh(inner)
+            slope = 0.5 * (1.0 + tanh) + 0.5 * up * (1.0 - tanh * tanh) * (
+                0.7978845608028654 * (1.0 + 0.134145 * (up * up))
+            )
+            grad = (grad * slope).astype(low)
+            dup_ref[:, columns] = grad
+            wide = grad.astype(f32)
+            gb1_ref[0:1, columns] += jnp.sum(wide, 0, keepdims=True)
+            dup_t[columns, here] = wide.T.astype(low)
+
+        tiles(units, body)
+
+    def down_back(dst):
+        def body(columns):
+            part = lax.dot_general(
+                dup_ref[...], w1_ref[columns, :],
+                (((1,), (1,)), ((), ())), preferred_element_type=f32,
+            )
+            dst[:, :, :, :, columns] = part.astype(low).reshape(2, 2, 2, rows, SPLIT)
+
+        tiles(width, body)
+
+    def share_part(stage, chunk):
+        copy = push(
+            far_part.at[chunk % 2], pair_in.at[chunk],
+            pair_send.at[stage, chunk], pair_recv.at[stage, chunk], net.pair,
+        )
+        copy.start()
+        return copy
+
+    def keep(chunk):
+        def finish(row, first, count, total):
+            res_ref[chunk * rows + row : chunk * rows + row + 16, first : first + count] = total
+
+        return finish
+
+    def norms(chunk):
+        for row in range(chunk * rows, (chunk + 1) * rows, 16):
+            at = slice(row, row + 16)
+            res = hid_ref[at, :] + res_ref[at, :] + par_ref[0:1, :]
+            mean = jnp.mean(res, -1, keepdims=True)
+            res = res - mean
+            scale = lax.rsqrt(jnp.mean(res * res, -1, keepdims=True) + norm_eps)
+            res = res * scale
+            out_ref[at, :] = (res * par_ref[1:2, :] + par_ref[2:3, :]).astype(low)
+            grad = cot_ref[at, :].astype(f32)
+            vec_ref[2:3, :] += jnp.sum(grad, 0, keepdims=True)
+            vec_ref[1:2, :] += jnp.sum(grad * res, 0, keepdims=True)
+            grad = grad * par_ref[1:2, :]
+            first = jnp.mean(grad, -1, keepdims=True)
+            second = jnp.mean(grad * res, -1, keepdims=True)
+            grad = (grad - first - res * second) * scale
+            dhid_ref[at, :] = grad
+            grad_low = grad.astype(low)
+            vec_ref[0:1, :] += jnp.sum(grad_low.astype(f32), 0, keepdims=True)
+            at_rows = slice(row - chunk * rows, row - chunk * rows + 16)
+            all_m[(chunk,) + own_slot + (at_rows, slice(None))] = grad_low
+
+    def flow(chunk):
+        incoming = (in_one.at[chunk], in_two.at[chunk], in_three.at[chunk])
+        places = (own_part.at[chunk], pair_in.at[chunk], sums.at[chunk], incoming)
+        yield from net.gather(all_h.at[chunk], 0, chunk)
+        share = net.share
+        upward(chunk, core)
+        downward(own_part.at[chunk])
+        yield
+        share.wait()
+        upward(chunk, 1 - core)
+        downward(far_part.at[chunk % 2])
+        share = share_part(1, chunk)
+        yield
+        yield from net.scatter(*places, share, 1, chunk, keep(chunk))
+        norms(chunk)
+        yield from net.gather(all_m.at[chunk], 2, chunk)
+        share = net.share
+        up_back(chunk, core)
+        down_back(own_part.at[chunk])
+        yield
+        share.wait()
+        up_back(chunk, 1 - core)
+        down_back(far_part.at[chunk % 2])
+        share = share_part(3, chunk)
+        yield
+        yield from net.scatter(*places, share, 3, chunk, keep(chunk))
+        here = slice(chunk * rows, (chunk + 1) * rows)
+        dhid_ref[here, :] += res_ref[here, :]
+
+    def weight_grads():
+        def product(left_t, right, out, columns):
+            total = None
+            for chunk in range(CHUNKS):
+                for side in range(2):
+                    here = slice((chunk * 2 + side) * half_rows, (chunk * 2 + side + 1) * half_rows)
+                    term = jnp.dot(
+                        left_t[:, here], flat(right, chunk, side, columns),
+                        preferred_element_type=f32,
+                    )
+                    total = term if total is None else total + term
+            return total
+
+        def run(left_t, right, out):
+            def step(at, carry):
+                columns = pl.ds(pl.multiple_of(at * SPLIT, SPLIT), SPLIT)
+                slot = at % 2
+
+                @pl.when(at >= 2)
+                def _():
+                    pltpu.make_async_copy(
+                        stage_ref.at[slot], out.at[:, columns], out_sems.at[slot]
+                    ).wait()
+
+                stage_ref[slot] = product(left_t, right, out, columns)
+                pltpu.make_async_copy(
+                    stage_ref.at[slot], out.at[:, columns], out_sems.at[slot]
+                ).start()
+                return carry
+
+            lax.fori_loop(0, width // SPLIT, step, 0)
+            for slot in range(2):
+                pltpu.make_async_copy(
+                    stage_ref.at[slot], out.at[:, pl.ds(0, SPLIT)], out_sems.at[slot]
+                ).wait()
+
+        run(act_t, all_m, gw2_ref)
+        run(dup_t, all_h, gw1_ref)
+
+    step_through([flow(chunk) for chunk in range(CHUNKS)])
+    weight_grads()
+
+
+def feed_forward(low, hidden, cotangent, w1, w2, b1, params):
+    f32, bf16 = jnp.float32, jnp.bfloat16
+    block, width = low.shape
+    rows = block // CHUNKS
+    units = w1.shape[1]
+    half_rows = rows * GROUP // 2
+    all_rows = GROUP * block
+    vmem = pl.BlockSpec(memory_space=pltpu.VMEM)
+    anywhere = pl.BlockSpec(memory_space=pl.ANY)
+    sems = pltpu.SemaphoreType.DMA
+
+    def slots(*lead):
+        return pltpu.VMEM(lead + (rows, width), bf16)
+
+    return pl.pallas_call(
+        ff_kernel,
+        out_shape=[
+            jax.ShapeDtypeStruct((block, width), bf16),
+            jax.ShapeDtypeStruct((block, width), f32),
+            jax.ShapeDtypeStruct((8, width), f32),
+            jax.ShapeDtypeStruct((8, units), f32),
+            jax.ShapeDtypeStruct((units, width), f32),
+            jax.ShapeDtypeStruct((units, width), f32),
+        ],
+        in_specs=[vmem] * 7,
+        out_specs=[vmem] * 4 + [anywhere] * 2,
+        scratch_shapes=[
+            slots(CHUNKS, 2, 2, 2, 2), slots(CHUNKS, 2, 2, 2, 2),
+            slots(CHUNKS, 2, 2, 2), slots(2, 2, 2, 2), slots(CHUNKS, 2, 2, 2),
+            slots(CHUNKS, 2, 2, 2), slots(CHUNKS, 2, 2), slots(CHUNKS, 2), slots(CHUNKS),
+            pltpu.VMEM((all_rows, units), f32),
+            pltpu.VMEM((half_rows, units), bf16),
+            pltpu.VMEM((units, all_rows), bf16),
+            pltpu.VMEM((half_rows, units), bf16),
+            pltpu.VMEM((units, all_rows), bf16),
+            pltpu.VMEM((block, width), f32),
+            pltpu.VMEM((2, units, SPLIT), f32),
+            sems((4, CHUNKS, 3, 3)), sems((4, CHUNKS, 3, 3)), sems((4, CHUNKS)), sems((4, CHUNKS)),
+            sems((2,)),
+        ],
+        compiler_params=pltpu.CompilerParams(
+            collective_id=4, has_side_effects=True, vmem_limit_bytes=63 << 20
+        ),
+        name="feed_forward",
+    )(low, hidden, cotangent, w1, w2, b1, params)
 
 
 def grouped_device(
@@ -847,17 +1194,9 @@
     own_qkv = own_qkv.reshape(GROUP * weight_rows, 3 * HEAD_DIM)
     own_w1 = own_w1.reshape(GROUP * weight_rows, 2 * unit_rows)
     full_qkv = in_order(own_qkv, lax.ppermute(own_qkv, "dp", across))
-    wo_beside = lax.ppermute(wo, "dp", beside)
-    chip_wo = jnp.concatenate(
-        [jnp.where(core == 0, wo, wo_beside), jnp.where(core == 0, wo_beside, wo)], 0
-    )
     wo_pairs = [
         (GROUP * g + 2 * k + g, GROUP * (1 - g) + 2 * k + g) for g in range(2) for k in range(8)
     ]
-    full_wo = jnp.where(core == group, chip_wo, lax.ppermute(chip_wo, "dp", wo_pairs))
-    full_w1 = in_order(own_w1, lax.ppermute(own_w1, "dp", across))
-    full_w2 = in_order(w2, lax.ppermute(w2, "dp", across))
-
     gathered = gathered.reshape(devices, -1)
     whole, at = [], 0
     for size in sizes:
@@ -892,35 +1231,30 @@
         )
 
     all_tokens = group_gather(tokens, "gather_tokens", 2)
+    all_tokens, own_w1, own_wo = lax.optimization_barrier((all_tokens, own_w1, wo))
+    wo_beside = lax.ppermute(own_wo, "dp", beside)
+    chip_wo = jnp.concatenate(
+        [jnp.where(core == 0, own_wo, wo_beside), jnp.where(core == 0, wo_beside, own_wo)], 0
+    )
+    full_wo = jnp.where(core == group, chip_wo, lax.ppermute(chip_wo, "dp", wo_pairs))
+    full_w1 = in_order(own_w1, lax.ppermute(own_w1, "dp", across))
     qkv = (jnp.dot(all_tokens, full_qkv, preferred_element_type=f32) + my_bqkv).astype(bf16)
     qkv_ext = with_halo(qkv)
     attended = attend(offset.reshape(1), qkv_ext, seg_q, seg_k, own_rows)
+    attended, own_w2 = lax.optimization_barrier((attended, w2))
+    full_w2 = in_order(own_w2, lax.ppermute(own_w2, "dp", across))
     branch_part = jnp.dot(attended, full_wo, preferred_element_type=f32).astype(bf16)
     branch = group_scatter(branch_part, "scatter_branch", 3) + all_bo
     resid_one = tokens.astype(f32) + branch
     hidden, norm_one_back = jax.vjp(layer_norm, resid_one, gain_one, shift_one)
 
-    all_hidden = group_gather(hidden.astype(bf16), "gather_hidden", 4)
-    upward = jnp.dot(all_hidden, full_w1, preferred_element_type=f32) + my_b1
-    activ, gelu_back = jax.vjp(gelu_tanh, upward)
-    activ_low = activ.astype(bf16)
-    mixed_part = jnp.dot(activ_low, full_w2, preferred_element_type=f32).astype(bf16)
-    mixed = group_scatter(mixed_part, "scatter_mixed", 5) + all_b2
-    normed, norm_two_back = jax.vjp(layer_norm, hidden + mixed, gain_two, shift_two)
-    output = normed.astype(bf16)
-
-    grad_resid_two, grad_gain_two, grad_shift_two = norm_two_back(cotangent.astype(f32))
-    grad_mixed = grad_resid_two.astype(bf16)
-    grad_b2 = jnp.sum(grad_mixed.astype(f32), 0)
-    all_grad_mixed = group_gather(grad_mixed, "gather_grad_mixed", 6)
-    grad_activ = jnp.einsum("td,fd->tf", all_grad_mixed, full_w2, preferred_element_type=f32)
-    grad_upward = gelu_back(grad_activ)[0].astype(bf16)
-    grad_b1 = jnp.sum(grad_upward.astype(f32), 0)
-    hidden_part = jnp.einsum(
-        "tf,df->td", grad_upward, full_w1, preferred_element_type=f32
-    ).astype(bf16)
-    grad_w2 = jnp.einsum("tf,td->fd", activ_low, all_grad_mixed, preferred_element_type=f32)
-    grad_w1 = jnp.einsum("td,tf->df", all_hidden, grad_upward, preferred_element_type=f32)
+    params = jnp.pad(jnp.stack([all_b2, gain_two, shift_two]), ((0, 5), (0, 0)))
+    output, grad_hidden, vec_two, grad_b1, grad_w2, grad_w1_t = feed_forward(
+        hidden.astype(bf16), hidden, cotangent, full_w1, full_w2,
+        jnp.broadcast_to(my_b1, (8, my_b1.shape[0])), params,
+    )
+    grad_b2, grad_gain_two, grad_shift_two = vec_two[0], vec_two[1], vec_two[2]
+    grad_b1 = grad_b1[0]
 
     def across_sum(grad):
         halves = grad.reshape((2, grad.shape[0] // 2) + grad.shape[1:])
@@ -929,13 +1263,17 @@
         return mine + lax.ppermute(theirs, "dp", across).astype(f32)
 
     out_w2 = across_sum(grad_w2)
-    sum_w1 = across_sum(grad_w1)
-    grad_hidden = grad_resid_two + group_scatter(hidden_part, "scatter_grad_hidden", 7)
 
     grad_resid_one, grad_gain_one, grad_shift_one = norm_one_back(grad_hidden)
     grad_branch = grad_resid_one.astype(bf16)
     grad_bo = jnp.sum(grad_branch.astype(f32), 0)
     all_grad_branch = group_gather(grad_branch, "gather_grad_branch", 8)
+    all_grad_branch, grad_w1_t = lax.optimization_barrier((all_grad_branch, grad_w1_t))
+    halves_t = jnp.split(grad_w1_t, 2, 1)
+    theirs_t = jnp.where(first_group, halves_t[1], halves_t[0]).astype(bf16)
+    sum_w1_t = jnp.where(first_group, halves_t[0], halves_t[1])
+    sum_w1_t = sum_w1_t + lax.ppermute(theirs_t, "dp", across).astype(f32)
+    sum_w1 = sum_w1_t.astype(bf16).T
     grad_attended = jnp.einsum(
         "td,cd->tc", all_grad_branch, full_wo, preferred_element_type=f32
     ).astype(bf16)

time: 815 us -> 681 us (0.84)
  Pallas kernels: 601 us -> 487 us
  matrix products: 92 us -> 42.5 us
  waiting for transfers between devices: 7.69 us -> 48.2 us
  other arithmetic: 49.6 us -> 40.2 us
    pallas_call x4 -> x2, Pallas kernels: 277 us -> 131 us  [group_gather(): pl.pallas_call(gather_kernel, out_shape=jax.ShapeDtypeStruct((2, 2, 2, 2,...]
    pallas_call x0 -> x1, Pallas kernels: none -> 142 us  [feed_forward(): pl.pallas_call(ff_kernel, out_shape=[jax.ShapeDtypeStruct((block, width),...]
    pallas_call x4 -> x2, Pallas kernels: 235 us -> 127 us  [group_scatter(): pl.pallas_call(scatter_kernel, out_shape=jax.ShapeDtypeStruct((count, wid...]
    dot_general x6 -> x0, matrix products: 51.4 us -> none  [the longest x1 11.9 us: grouped_device(): jnp.einsum('td,fd->tf', all_grad_mixed, full_w2, preferred_element_type=f32)]
    ppermute x2, waiting for transfers between devices: 7.66 us -> 48.1 us  [with_halo(): halo = lax.ppermute(edge, 'dp', across)]
  transfers between devices with their start and end apart: 12 -> 12, of which waited for: 2 -> 1; matrix products, arithmetic and copies ran while one was open for 15% -> 14% of each run, Pallas kernels for 64% -> 47%
where the time goes in v3:
time: 681 us; the launch traced here: 672 us
  Pallas kernels  487 us (72%)
  waiting for transfers between devices  48.2 us (7%)
  matrix products  42.5 us (6%)
  other arithmetic  40.2 us (6%)
  local copies, waits for them, and re-layouts  37.1 us (5%)
  starting transfers between devices  14.8 us (2%)
    pallas_call x1, Pallas kernels, feed_forward(): pl.pallas_call(ff_kernel, out_shape=[jax.ShapeDtypeStruct((block, width),...  142 us
    pallas_call x2, Pallas kernels, group_gather(): pl.pallas_call(gather_kernel, out_shape=jax.ShapeDtypeStruct((2, 2, 2, 2,...  131 us
    pallas_call x2, Pallas kernels, group_scatter(): pl.pallas_call(scatter_kernel, out_shape=jax.ShapeDtypeStruct((count, wid...  127 us
    ppermute x2, waiting for transfers between devices, with_halo(): halo = lax.ppermute(edge, 'dp', across)  48.1 us
    pallas_call x1, Pallas kernels, weights_out(): pl.pallas_call(weights_out_kernel, out_shape=[jax.ShapeDtypeStruct(pack_q...  32.4 us
    pallas_call x1, Pallas kernels, weights_back(): pl.pallas_call(weights_back_kernel, out_shape=[jax.ShapeDtypeStruct(rows_...  29.8 us
    pallas_call x1, Pallas kernels, attend_back(): pl.pallas_call(attend_back_kernel, out_shape=jax.ShapeDtypeStruct(qkv.sha...  15.1 us
  transfers between devices with their start and end apart: 12, of which 1 were waited for; matrix products, arithmetic and copies ran while one was open for 14% of the time, Pallas kernels for 47%

profile of v3, /device:TPU:7, one launch (start us, length us, event | category | flops | bytes accessed | tf_op | source)
XLA Modules:
  0.0 671.7 jit_solution(792483684649463091)
XLA Ops:
  0.7 6.2 concatenate.37
  7.5 1.0 copy.88
  8.5 1.0 copy.89
  10.0 1.0 copy.102
  11.0 1.5 reshape.269.w1_ref
  12.5 1.0 pad_maximum_fusion.5.qkv_ref
  13.5 32.4 %weights_out.1 = (bf16[16,64,384]{2,1,0:T(8,128)(2,1)}, bf16[16,64,512]{2,1,0:T(8,128)(2,1)}, f32[2,16,8,128]{3,2,1,0:T(8,128)}) custom-call(bf16[16,64,384]{2,1,0:T(8,128)(2,1)} %pad_maximum_fusion.5.qkv_ref, bf16[16,64,512]{2,1,0:T(8,128)(2,1)} %reshape.269.w1_ref, f32[8,128]{1,0:T(8,128)} %bitcast_convert_fusion.vec_ref), custom_call_target="tpu_custom_call" | custom-call | tf_op jit(solution)/shard_map/weights_out/pallas_call | solution.py:615
  45.9 1.4 collective-permute-start
  47.3 60.7 %gather_tokens.1 = bf16[2,2,2,2,128,2048]{5,4,3,2,1,0:T(8,128)(2,1)} custom-call(bf16[128,2048]{1,0:T(8,128)(2,1)} %x_ref.1), custom_call_target="tpu_custom_call" | custom-call | tf_op jit(solution)/shard_map/gather_tokens/pallas_call | solution.py:419
  110.2 0.9 pad_maximum_fusion.6
  111.1 1.3 collective-permute-start.3
  112.7 8.5 %add_convert_fusion = bf16[2048,384]{1,0:T(8,128)(2,1)S(1)} fusion(bf16[2048,2048]{1,0:T(8,128)(2,1)} %bitcast.92, f32[384]{0:T(512)S(1)} %pad_maximum_fusion.7, bf16[1024,384]{1,0:T(8,128)(2,1)S(1)} %get-tuple-element.74, bf16[1024,384]{1,0:T(8,128)(2,1)S(1)} %get-tuple-element.73), kind=kOutput, calls=%fused_computation.3 | convolution fusion | flops 3225944064 | bytes 11535872 | tf_op jit(solution)/shard_map/dot_general | solution.py:1241
  121.2 3.8 collective-permute-start.1
  126.1 2.0 broadcast_in_dim.37.seg_q_ref
  128.1 48.1 %collective-permute-done.1 = bf16[256,384]{1,0:T(8,128)(2,1)S(1)} collective-permute-done((bf16[256,384]{1,0:T(8,128)(2,1)S(1)}, bf16[256,384]{1,0:T(8,128)(2,1)S(1)}, u32[]{:S(2)}, u32[]{:S(2)}) %collective-permute-start.1) | collective-permute-done | bytes 196640 | tf_op jit(solution)/shard_map/ppermute | solution.py:1228
  176.2 1.9 maximum_select_fusion.qkv_ref
  178.2 9.4 %attend.1 = bf16[2048,128]{1,0:T(8,128)(2,1)} custom-call(s32[1]{0:T(128)} %bitcast.offset_ref, bf16[2304,384]{1,0:T(8,128)(2,1)} %maximum_select_fusion.qkv_ref, s32[2304,1]{1,0:T(8,128)} %broadcast_in_dim.37.seg_q_ref, s32[18,1,512]{2,1,0:T(1,128)} %broadcast_in_dim.32.seg_k_ref), custom_call_target="tpu_custom_call" | custom-call | tf_op jit(solution)/shard_map/attend/pallas_call | solution.py:766
  187.6 6.8 %convolution_convert_fusion.1 = bf16[2048,2048]{1,0:T(8,128)(2,1)} fusion(bf16[2048,128]{1,0:T(8,128)(2,1)} %attend.1, bf16[128,2048]{1,0:T(8,128)(2,1)} %collective-permute-done.3, pred[]{:T(512)S(6)} %eq.17, bf16[64,2048]{1,0:T(8,128)(2,1)S(1)} %get-tuple-element.79, bf16[64,2048]{1,0:T(8,128)(2,1)S(1)} %get-tuple-element.78), kind=kOutput, calls=%fused_computation.1 | convolution fusion | flops 1079246848 | bytes 9961473 | tf_op jit(solution)/shard_map/dot_general | solution.py:1246
  194.4 58.9 %scatter_branch.1 = f32[128,2048]{1,0:T(8,128)} custom-call(bf16[2,2,2,2,128,2048]{5,4,3,2,1,0:T(8,128)(2,1)} %bitcast.90), custom_call_target="tpu_custom_call" | custom-call | tf_op jit(solution)/shard_map/scatter_branch/pallas_call | solution.py:541
  253.3 1.5 fusion.11
  255.1 0.8 copy-done.1
  255.9 1.4 fusion.10
  257.3 1.7 broadcast_select_fusion.3
  258.9 1.5 pad_maximum_fusion.w1_ref
  260.5 1.6 pad_maximum_fusion.1.w2_ref
  262.7 142.3 %feed_forward.1 = (bf16[128,2048]{1,0:T(8,128)(2,1)}, f32[128,2048]{1,0:T(8,128)}, f32[8,2048]{1,0:T(8,128)}, f32[8,512]{1,0:T(8,128)}, f32[512,2048]{1,0:T(8,128)}, /*index=5*/f32[512,2048]{1,0:T(8,128)}) custom-call(bf16[128,2048]{1,0:T(8,128)(2,1)} %get-tuple-element.65.low_ref, f32[128,2048]{1,0:T(8,128)} %get-tuple-element.66.hid_ref, ...), custom_call_target="tpu_custom_call" | custom-call | tf_op jit(solution)/shard_map/feed_forward/pallas_call | solution.py:1105
  405.0 0.9 slice_reduce_fusion.3
  405.9 1.9 multiply_reduce_fusion
  408.5 1.0 slice_reduce_fusion
  409.7 0.9 convert_reduce_fusion.2
  410.8 3.5 select_convert_fusion
  414.2 70.3 %gather_grad_branch.1 = bf16[2,2,2,2,128,2048]{5,4,3,2,1,0:T(8,128)(2,1)} custom-call(bf16[128,2048]{1,0:T(8,128)(2,1)} %get-tuple-element.62.x_ref), custom_call_target="tpu_custom_call" | custom-call | tf_op jit(solution)/shard_map/gather_grad_branch/pallas_call | solution.py:419
  484.6 5.6 fusion.15
  490.3 3.6 convolution_convert_fusion.2
  494.1 5.1 collective-permute-start.9
  499.1 1.2 select_convert_fusion.1
  500.3 1.0 maximum_select_fusion.1.grad_ref
  501.3 15.1 %attend_back.1 = bf16[2304,384]{1,0:T(8,128)(2,1)} custom-call(bf16[2304,384]{1,0:T(8,128)(2,1)} %maximum_select_fusion.qkv_ref, bf16[2304,128]{1,0:T(8,128)(2,1)} %maximum_select_fusion.1.grad_ref, s32[2304,1]{1,0:T(8,128)} %broadcast_in_dim.37.seg_q_ref, s32[18,1,512]{2,1,0:T(1,128)} %broadcast_in_dim.32.seg_k_ref), custom_call_target="tpu_custom_call" | custom-call | tf_op jit(solution)/shard_map/attend_back/pallas_call | solution.py:780
  516.4 10.2 %fusion = f32[2048,384]{1,0:T(8,128)} fusion(bf16[2048,2048]{1,0:T(8,128)(2,1)} %bitcast.93, bf16[2304,384]{1,0:T(8,128)(2,1)} %attend_back.1, s32[]{:T(128)S(6)} %select_n.196), kind=kOutput, calls=%fused_computation.16 | convolution fusion | flops 3221225472 | bytes 13107204 | tf_op jit(solution)/shard_map/td,tf->df/dot_general | solution.py:1285
  526.9 7.7 %convolution_convert_fusion = bf16[2048,2048]{1,0:T(8,128)(2,1)} fusion(bf16[2304,384]{1,0:T(8,128)(2,1)S(1)} %copy-done.7, s32[]{:T(128)S(6)} %select_n.196, bf16[1024,384]{1,0:T(8,128)(2,1)S(1)} %copy-done.19, bf16[1024,384]{1,0:T(8,128)(2,1)S(1)} %copy-done.17), kind=kOutput, calls=%fused_computation | convolution fusion | flops 3228565504 | bytes 11534340 | tf_op jit(solution)/shard_map/tf,df->td/dot_general | solution.py:1284
  535.0 2.9 select_convert_fusion.2
  538.2 0.8 reshape.290.vec_ref
  538.9 2.4 collective-permute-start.8
  541.3 68.4 %scatter_input.1 = f32[128,2048]{1,0:T(8,128)} custom-call(bf16[2,2,2,2,128,2048]{5,4,3,2,1,0:T(8,128)(2,1)} %bitcast.91), custom_call_target="tpu_custom_call" | custom-call | tf_op jit(solution)/shard_map/scatter_input/pallas_call | solution.py:541
  609.7 2.2 add_convert_fusion.3
  611.9 1.3 convert_add_fusion.1
  613.2 0.9 slice_select_fusion
  614.0 0.7 collective-permute-start.10
  614.7 2.7 add_convert_fusion.2
  618.1 1.3 copy.75
  619.4 29.8 %weights_back.1 = (bf16[16,64,512]{2,1,0:T(8,128)(2,1)}, bf16[16,64,384]{2,1,0:T(8,128)(2,1)}, f32[8,128]{1,0:T(8,128)}) custom-call(bf16[16,64,512]{2,1,0:T(8,128)(2,1)} %bitcast.98, bf16[16,64,384]{2,1,0:T(8,128)(2,1)} %bitcast.99, f32[16,16,128]{2,1,0:T(8,128)} %reshape.290.vec_ref), custom_call_target="tpu_custom_call" | custom-call | tf_op jit(solution)/shard_map/weights_back/pallas_call | solution.py:671
  649.2 1.6 fusion.14
  650.8 1.2 fusion.12
  652.1 4.5 convert_add_fusion
  656.6 1.2 slice_bitcast_fusion
  657.9 1.1 copy.85
  659.0 1.1 copy.86
  660.4 1.0 copy.103
  661.3 2.4 reshape.301
  663.7 1.2 copy.87
  664.9 2.5 copy.96
  667.5 1.3 copy_bitcast_fusion.1
  668.8 1.9 select_select_fusion
  670.7 0.8 copy.109
  (144 shorter events, 8.8 us)
Async XLA Ops:
  0.7 8.9 %copy-start.22 = (bf16[64,2048]{1,0:T(8,128)(2,1)S(1)}, bf16[64,2048]{1,0:T(8,128)(2,1)}, u32[]{:S(2)}) copy-start(bf16[64,2048]{1,0:T(8,128)(2,1)} %param.24) | copy-start | bytes 786436
  0.7 9.1 %copy-start.15 = (bf16[64,8192]{1,0:T(8,128)(2,1)S(1)}, bf16[64,8192]{1,0:T(8,128)(2,1)}, u32[]{:S(2)}) copy-start(bf16[64,8192]{1,0:T(8,128)(2,1)} %param.30) | copy-start | bytes 3145732
  45.9 62.1 %copy-start.23 = (bf16[64,2048]{1,0:T(8,128)(2,1)S(1)}, bf16[64,2048]{1,0:T(8,128)(2,1)}, u32[]{:S(2)}) copy-start(bf16[64,2048]{1,0:T(8,128)(2,1)} %param.26) | copy-start | bytes 786436
  45.9 62.4 %copy-start.24 = (f32[2,16,8,128]{3,2,1,0:T(8,128)S(1)}, f32[2,16,8,128]{3,2,1,0:T(8,128)}, u32[]{:S(2)}) copy-start(f32[2,16,8,128]{3,2,1,0:T(8,128)} %get-tuple-element.39) | copy-start | bytes 393220
  45.9 63.4 %copy-start.25 = (s32[32]{0:T(128)S(1)}, s32[32]{0:T(128)}, u32[]{:S(2)}) copy-start(s32[32]{0:T(128)} %param.20) | copy-start | bytes 388
  45.9 66.5 %collective-permute-start = (bf16[1024,384]{1,0:T(8,128)(2,1)}, bf16[1024,384]{1,0:T(8,128)(2,1)S(1)}, u32[]{:S(2)}, u32[]{:S(2)}) collective-permute-start(bf16[1024,384]{1,0:T(8,128)(2,1)} %bitcast.114), channel_id=1, source_target_pairs={{0,16},{1,17},{2,18},{3,19},{4,20},{5,21},{6,22},{7,23},{8,24},{9,... | collective-permute-start | bytes 2359304 | tf_op jit(solution)/shard_map/ppermute | solution.py:1196
  108.0 4.4 copy-start.20
  108.0 2.2 collective-permute-start.2
  108.2 149.0 %collective-permute-start.4 = (bf16[1024,512]{1,0:T(8,128)(2,1)}, bf16[1024,512]{1,0:T(8,128)(2,1)}, u32[]{:S(2)}, u32[]{:S(2)}) collective-permute-start(bf16[1024,512]{1,0:T(8,128)(2,1)} %bitcast.10), channel_id=1, source_target_pairs={{0,16},{1,17},{2,18},{3,19},{4,20},{5,21},{6,22},{7,23},{8,24},{9,... | collective-permute-start | bytes 3145736 | tf_op jit(solution)/shard_map/ppermute | solution.py:1240
  110.2 77.4 %copy-start.9 = (bf16[64,2048]{1,0:T(8,128)(2,1)}, bf16[64,2048]{1,0:T(8,128)(2,1)S(1)}, u32[]{:S(2)}) copy-start(bf16[64,2048]{1,0:T(8,128)(2,1)S(1)} %get-tuple-element.79) | copy-start | bytes 786436
  111.1 76.5 %collective-permute-start.3 = (bf16[128,2048]{1,0:T(8,128)(2,1)}, bf16[128,2048]{1,0:T(8,128)(2,1)}, u32[]{:S(2)}, u32[]{:S(2)}) collective-permute-start(bf16[128,2048]{1,0:T(8,128)(2,1)} %pad_maximum_fusion.6), channel_id=1, source_target_pairs={{0,16},{2,18},{4,20},{6,22},{8,24},{10,26},{12,28},{14,30},{17,1},... | collective-permute-start | bytes 1572872 | tf_op jit(solution)/shard_map/ppermute | solution.py:1239
  112.7 8.5 %copy-start.16 = (bf16[1024,384]{1,0:T(8,128)(2,1)}, bf16[1024,384]{1,0:T(8,128)(2,1)S(1)}, u32[]{:S(2)}) copy-start(bf16[1024,384]{1,0:T(8,128)(2,1)S(1)} %get-tuple-element.73) | copy-start | bytes 2359300
  112.7 8.5 %copy-start.18 = (bf16[1024,384]{1,0:T(8,128)(2,1)}, bf16[1024,384]{1,0:T(8,128)(2,1)S(1)}, u32[]{:S(2)}) copy-start(bf16[1024,384]{1,0:T(8,128)(2,1)S(1)} %get-tuple-element.74) | copy-start | bytes 2359300
  121.2 55.0 %collective-permute-start.1 = (bf16[256,384]{1,0:T(8,128)(2,1)S(1)}, bf16[256,384]{1,0:T(8,128)(2,1)S(1)}, u32[]{:S(2)}, u32[]{:S(2)}) collective-permute-start(bf16[256,384]{1,0:T(8,128)(2,1)S(1)} %slice_select_fusion.1), channel_id=1, source_target_pairs={{0,16},{1,17},{2,18},{3,19},{4,20},{5,21},{6,22},{7,23},{8,24},{9,... | collective-permute-start | bytes 589832 | tf_op jit(solution)/shard_map/ppermute | solution.py:1228
  178.2 9.4 %copy-start.14 = (bf16[256,2048]{1,0:T(8,128)(2,1)S(1)}, bf16[256,2048]{1,0:T(8,128)(2,1)}, u32[]{:S(2)}) copy-start(bf16[256,2048]{1,0:T(8,128)(2,1)} %param.32) | copy-start | bytes 3145732
  187.6 72.8 %collective-permute-start.5 = (bf16[256,2048]{1,0:T(8,128)(2,1)S(1)}, bf16[256,2048]{1,0:T(8,128)(2,1)S(1)}, u32[]{:S(2)}, u32[]{:S(2)}) collective-permute-start(bf16[256,2048]{1,0:T(8,128)(2,1)S(1)} %copy-done.14), channel_id=1, source_target_pairs={{0,16},{1,17},{2,18},{3,19},{4,20},{5,21},{6,22},{7,23},{8,24},{9,... | collective-permute-start | bytes 3145736 | tf_op jit(solution)/shard_map/ppermute | solution.py:1245
  194.4 59.0 %copy-start.11 = (bf16[128,2048]{1,0:T(8,128)(2,1)S(1)}, bf16[128,2048]{1,0:T(8,128)(2,1)}, u32[]{:S(2)}) copy-start(bf16[128,2048]{1,0:T(8,128)(2,1)} %x_ref.1) | copy-start | bytes 1572868
  254.8 1.1 copy-start.1
  405.0 2.9 copy-start.2
  405.0 2.9 copy-start.8
  414.2 237.9 %collective-permute-start.11 = (bf16[256,2048]{1,0:T(8,128)(2,1)}, bf16[256,2048]{1,0:T(8,128)(2,1)}, u32[]{:S(2)}, u32[]{:S(2)}) collective-permute-start(bf16[256,2048]{1,0:T(8,128)(2,1)} %select_convert_fusion), channel_id=1, source_target_pairs={{0,16},{1,17},{2,18},{3,19},{4,20},{5,21},{6,22},{7,23},{8,24},{9,... | collective-permute-start | bytes 3145736 | tf_op jit(solution)/shard_map/ppermute | solution.py:1263
  414.2 70.3 %copy-start.3 = (bf16[2048,128]{1,0:T(8,128)(2,1)S(1)}, bf16[2048,128]{1,0:T(8,128)(2,1)}, u32[]{:S(2)}) copy-start(bf16[2048,128]{1,0:T(8,128)(2,1)} %attend.1) | copy-start | bytes 1572868
  484.6 5.8 copy-start
  484.6 5.8 copy-start.10
  490.3 8.8 %copy-start.4 = (f32[512,2048]{1,0:T(8,128)S(1)}, f32[512,2048]{1,0:T(8,128)}, u32[]{:S(2)}) copy-start(f32[512,2048]{1,0:T(8,128)} %get-tuple-element.48) | copy-start | bytes 12582916
  494.0 6.3 collective-permute-start.6
  494.1 117.8 %collective-permute-start.9 = (bf16[128,2048]{1,0:T(8,128)(2,1)}, bf16[128,2048]{1,0:T(8,128)(2,1)}, u32[]{:S(2)}, u32[]{:S(2)}) collective-permute-start(bf16[128,2048]{1,0:T(8,128)(2,1)} %get-tuple-element.96), channel_id=1, source_target_pairs={{16,0},{18,2},{20,4},{22,6},{24,8},{26,10},{28,12},{30,14},{1,17},... | collective-permute-start | bytes 1572872 | tf_op jit(solution)/shard_map/ppermute | solution.py:1291
  500.3 117.1 %collective-permute-start.7 = (bf16[512,1024]{1,0:T(8,128)(2,1)}, bf16[512,1024]{1,0:T(8,128)(2,1)S(1)}, u32[]{:S(2)}, u32[]{:S(2)}) collective-permute-start(bf16[512,1024]{1,0:T(8,128)(2,1)} %select_convert_fusion.1), channel_id=1, source_target_pairs={{0,16},{1,17},{2,18},{3,19},{4,20},{5,21},{6,22},{7,23},{8,24},{9,... | collective-permute-start | bytes 3145736 | tf_op jit(solution)/shard_map/ppermute | solution.py:1275
  516.4 10.3 %copy-start.7 = (bf16[2304,384]{1,0:T(8,128)(2,1)S(1)}, bf16[2304,384]{1,0:T(8,128)(2,1)}, u32[]{:S(2)}) copy-start(bf16[2304,384]{1,0:T(8,128)(2,1)} %attend_back.1) | copy-start | bytes 5308420
  516.4 10.6 %copy-start.17 = (bf16[1024,384]{1,0:T(8,128)(2,1)S(1)}, bf16[1024,384]{1,0:T(8,128)(2,1)}, u32[]{:S(2)}) copy-start(bf16[1024,384]{1,0:T(8,128)(2,1)} %copy-done.16) | copy-start | bytes 2359300
  516.4 10.6 %copy-start.19 = (bf16[1024,384]{1,0:T(8,128)(2,1)S(1)}, bf16[1024,384]{1,0:T(8,128)(2,1)}, u32[]{:S(2)}) copy-start(bf16[1024,384]{1,0:T(8,128)(2,1)} %copy-done.18) | copy-start | bytes 2359300
  538.9 75.8 %collective-permute-start.8 = (bf16[1024,384]{1,0:T(8,128)(2,1)}, bf16[1024,384]{1,0:T(8,128)(2,1)}, u32[]{:S(2)}, u32[]{:S(2)}) collective-permute-start(bf16[1024,384]{1,0:T(8,128)(2,1)} %select_convert_fusion.2), channel_id=1, source_target_pairs={{0,16},{1,17},{2,18},{3,19},{4,20},{5,21},{6,22},{7,23},{8,24},{9,... | collective-permute-start | bytes 2359304 | tf_op jit(solution)/shard_map/ppermute | solution.py:1263
  611.9 2.9 copy-start.6
  614.0 3.4 copy-start.5
  614.0 54.8 %collective-permute-start.10 = (f32[64,2048]{1,0:T(8,128)}, f32[64,2048]{1,0:T(8,128)}, u32[]{:S(2)}, u32[]{:S(2)}) collective-permute-start(f32[64,2048]{1,0:T(8,128)} %slice_select_fusion), channel_id=1, source_target_pairs={{0,1},{1,0},{2,3},{3,2},{4,5},{5,4},{6,7},{7,6},{8,9},{9,8},{10,11... | collective-permute-start | bytes 1572872 | tf_op jit(solution)/shard_map/ppermute | solution.py:1295
  664.9 2.5 copy-start.12
  664.9 2.5 copy-start.13
  667.5 3.2 copy-start.21

commit v4 on v3

--- a/solution.py
+++ b/solution.py
@@ -691,11 +691,6 @@
     )(rows_w1, rows_qkv, vectors)
 
 
-def window_start(row, total):
-    start = jnp.minimum(jnp.maximum(row - (WINDOW - TILE) // 2, 0), total - WINDOW)
-    return pl.multiple_of(start, 64)
-
-
 def tile_probs(qkv_ref, row, start, seg_q, seg_k):
     f32 = jnp.float32
     queries = qkv_ref[pl.ds(row, TILE), 0:HEAD_DIM]
@@ -706,41 +701,25 @@
     return queries, keys, weights / jnp.sum(weights, -1, keepdims=True)
 
 
-def attend_kernel(offset_ref, qkv_ref, seg_q_ref, seg_k_ref, o_ref):
-    total = qkv_ref.shape[0]
-    offset = offset_ref[0]
-
-    def body(tile, carry):
-        row = pl.multiple_of(offset + tile * TILE, TILE)
-        start = window_start(row, total)
-        _, _, probs = tile_probs(
-            qkv_ref, row, start, seg_q_ref[pl.ds(row, TILE), :], seg_k_ref[row // TILE]
-        )
-        values = qkv_ref[pl.ds(start, WINDOW), 2 * HEAD_DIM : 3 * HEAD_DIM]
-        out = jnp.dot(probs.astype(values.dtype), values, preferred_element_type=jnp.float32)
-        o_ref[pl.ds(pl.multiple_of(tile * TILE, TILE), TILE), :] = out.astype(o_ref.dtype)
-        return carry
-
-    lax.fori_loop(0, o_ref.shape[0] // TILE, body, 0, unroll=2)
-
-
 def attend_back_kernel(qkv_ref, grad_ref, seg_q_ref, seg_k_ref, o_ref, dq_sum, dk_sum, dv_sum):
     total = qkv_ref.shape[0]
     f32 = jnp.float32
     low = qkv_ref.dtype
     scale = HEAD_DIM ** (-0.5)
+    dq_sum[...] = jnp.zeros_like(dq_sum)
     dk_sum[...] = jnp.zeros_like(dk_sum)
     dv_sum[...] = jnp.zeros_like(dv_sum)
 
     def body(tile, carry):
-        row = pl.multiple_of(tile * TILE, TILE)
-        start = window_start(row, total)
+        place = pl.multiple_of(tile * TILE, TILE)
+        row = pl.multiple_of(PAD + place, 64)
+        start = place
         queries, keys, probs = tile_probs(
-            qkv_ref, row, start, seg_q_ref[pl.ds(row, TILE), :], seg_k_ref[tile]
+            qkv_ref, row, start, seg_q_ref[pl.ds(place, TILE), :], seg_k_ref[tile]
         )
         window = pl.ds(start, WINDOW)
         values = qkv_ref[window, 2 * HEAD_DIM : 3 * HEAD_DIM]
-        grads = grad_ref[pl.ds(row, TILE), :]
+        grads = grad_ref[pl.ds(place, TILE), :]
         grad_probs = lax.dot_general(
             grads, values, (((1,), (1,)), ((), ())), preferred_element_type=f32
         )
@@ -755,22 +734,10 @@
         )
         return carry
 
-    lax.fori_loop(0, total // TILE, body, 0, unroll=2)
+    lax.fori_loop(0, grad_ref.shape[0] // TILE, body, 0, unroll=2)
     o_ref[:, 0:HEAD_DIM] = (dq_sum[...] * scale).astype(low)
     o_ref[:, HEAD_DIM : 2 * HEAD_DIM] = (dk_sum[...] * scale).astype(low)
     o_ref[:, 2 * HEAD_DIM : 3 * HEAD_DIM] = dv_sum[...].astype(low)
-
-
-def attend(offset, qkv, seg_q, seg_k, rows):
-    vmem = pl.BlockSpec(memory_space=pltpu.VMEM)
-    return pl.pallas_call(
-        attend_kernel,
-        out_shape=jax.ShapeDtypeStruct((rows, HEAD_DIM), qkv.dtype),
-        in_specs=[pl.BlockSpec(memory_space=pltpu.SMEM), vmem, vmem, vmem],
-        out_specs=vmem,
-        compiler_params=pltpu.CompilerParams(vmem_limit_bytes=VMEM_LIMIT),
-        name="attend",
-    )(offset, qkv, seg_q, seg_k)
 
 
 def attend_back(qkv, grads, seg_q, seg_k):
@@ -791,14 +758,21 @@
 CHUNKS = 4
 COLUMNS = ((0, 768), (768, 640), (1408, 640))
 SPLIT = 256
-
-
-def step_through(flows):
+PAD = (WINDOW - TILE) // 2
+STAGES = 7
+
+
+def step_through(flows, fillers=None):
     waiting, alive = list(flows), []
     while waiting or alive:
         if waiting:
             alive.append(waiting.pop(0))
         alive = [flow for flow in alive if next(flow, "done") != "done"]
+        if fillers is not None:
+            next(fillers, None)
+    if fillers is not None:
+        for _ in fillers:
+            pass
 
 
 class Traffic:
@@ -819,6 +793,13 @@
             self.hop_send.at[stage, chunk, part, step],
             self.hop_recv.at[stage, chunk, part, step],
             self.partners[ORDERS[part][step]],
+        )
+        copy.start()
+        return copy
+
+    def share(self, src, dst, stage, chunk):
+        copy = push(
+            src, dst, self.pair_send.at[stage, chunk], self.pair_recv.at[stage, chunk], self.pair
         )
         copy.start()
         return copy
@@ -838,19 +819,15 @@
             yield
         for part in range(3):
             hops[part, 2].wait_recv()
-        share = push(
-            mine, mine, self.pair_send.at[stage, chunk], self.pair_recv.at[stage, chunk], self.pair
-        )
-        share.start()
+        share = self.share(mine, mine, stage, chunk)
         for copy in hops.values():
             copy.wait_send()
-        self.share = share
-
-    def scatter(self, own, pair_in, sums, incoming, share, stage, chunk, finish):
+        return share
+
+    def scatter(self, own, pair_in, incoming, share, stage, chunk, finish):
         rows = own.shape[-2]
         f32 = jnp.float32
         hops = {}
-
         share.wait()
         for step in range(4):
             for part, (first, count) in enumerate(COLUMNS):
@@ -875,7 +852,7 @@
                             left = [slot[dim] for dim in (2, 1, 0) if dim not in order[: back + 1]]
                             total = total + incoming[back][tuple(left) + at].astype(f32)
                         if step < 3:
-                            sums[where + at] = total.astype(sums.dtype)
+                            own[where + at] = total.astype(own.dtype)
                         else:
                             finish(row, first, count, total)
                 if step == 3:
@@ -884,7 +861,7 @@
                     values[dim] = slice(None)
                 left = tuple(slice(None) for _ in free)
                 hops[part, step] = self.push(
-                    self.chips(sums, values, columns),
+                    self.chips(own, values, columns),
                     incoming[step].at[left + (slice(None), columns)],
                     stage, chunk, part, step,
                 )
@@ -894,26 +871,77 @@
             copy.wait_send()
 
 
-def ff_kernel(
-    low_ref, hid_ref, cot_ref, w1_ref, w2_ref, b1_ref, par_ref,
-    out_ref, dhid_ref, vec_ref, gb1_ref, gw2_ref, gw1_ref,
-    all_h, all_m, own_part, far_part, pair_in, sums, in_one, in_two, in_three,
-    up_ref, act_ref, act_t, dup_ref, dup_t, res_ref, stage_ref,
-    hop_send, hop_recv, pair_send, pair_recv, out_sems,
+def gelu_slope(up):
+    inner = 0.7978845608028654 * (up + 0.044715 * (up * up * up))
+    tanh = jnp.tanh(inner)
+    return 0.5 * (1.0 + tanh) + 0.5 * up * (1.0 - tanh * tanh) * (
+        0.7978845608028654 * (1.0 + 0.134145 * (up * up))
+    )
+
+
+NT = (((1,), (1,)), ((), ()))
+
+
+def layer_kernel(
+    tok_ref, cot_ref, pack_qkv, pack_w1, w2_ref, wo_ref, vec_ref, seg_q_ref, seg_k_ref,
+    out_ref, dres_ref, vecg_ref, gb1_ref, gw2_own, gw2_far, gw1_own, gw1_far, gwo_ref,
+    x_all, h_all, qkv_ref, dout_ref, wqkv_ref,
+    all_h, all_m, own_part, far_part, pair_in, in_one, in_two, in_three,
+    up_ref, act_ref, act_t, dup_ref, dup_t, att_ref, att_t, res_ref, hid_ref, norm_ref, scale_ref,
+    w1_all, w2_all, wo_all, vec_all, low_ref, high_ref, b1_ref, stage_ref, stage_low,
+    hop_send, hop_recv, pair_send, pair_recv,
+    block_local, block_send, block_recv, vec_send, vec_recv, far_send, far_recv,
+    local_sems, out_sems, spill_sems,
 ):
-    f32, low = jnp.float32, low_ref.dtype
-    block, width = low_ref.shape
+    f32, low = jnp.float32, tok_ref.dtype
+    block, width = tok_ref.shape
     rows = block // CHUNKS
     half_rows = rows * GROUP // 2
-    units = w1_ref.shape[1]
+    own_rows = GROUP * block
+    units = w1_all.shape[-1]
+    group, base, mine, others, across = group_places()
     net = Traffic((hop_send, hop_recv, pair_send, pair_recv))
     core, bits = net.core, net.bits
+    chip = mine // 2
+    head = core * 8 + chip
     own_slot = (core, bits[2], bits[1], bits[0])
-    enter(net.partners + [net.pair])
-    vec_ref[...] = jnp.zeros_like(vec_ref)
+    ext = PAD + group * HALO
+    enter(others + [across, flip(across, 0)])
+
+    def far(src, dst, at, device=across):
+        copy = push(src, dst, far_send.at[at], far_recv.at[at], device)
+        copy.start()
+        return copy
+
+    def local(src, dst, at):
+        copy = pltpu.make_async_copy(src, dst, local_sems.at[at])
+        copy.start()
+        return copy
+
+    early = w2_ref.shape[0] // 4
+    far_vec = far(vec_ref, vec_all.at[group, mine], 0)
+    near = [
+        local(vec_ref, vec_all.at[group, mine], 0),
+        local(w2_ref, w2_all.at[group], 1),
+        local(wo_ref, wo_all.at[group, core], 2),
+    ]
+    w2_first, w2_last = pl.ds(0, early), pl.ds(early, w2_ref.shape[0] - early)
+    far_w2 = [far(w2_ref.at[w2_first, :], w2_all.at[group, w2_first, :], 1)]
+    qkv_blocks = exchange_blocks(
+        [(pack_qkv, wqkv_ref.at[group])],
+        (block_local.at[0:1], block_send.at[0:1], block_recv.at[0:1]), base, mine, others,
+    )
+    for chunk in range(CHUNKS):
+        all_m[(chunk,) + own_slot] = tok_ref[chunk * rows : (chunk + 1) * rows, :]
+    wo_near = push(
+        wo_ref, wo_all.at[group, core], far_send.at[2], far_recv.at[2], net.pair
+    )
+    wo_near.start()
+
+    qkv_ref[0:PAD, :] = jnp.zeros((PAD, qkv_ref.shape[1]), low)
+    qkv_ref[qkv_ref.shape[0] - PAD :, :] = jnp.zeros((PAD, qkv_ref.shape[1]), low)
+    vecg_ref[...] = jnp.zeros_like(vecg_ref)
     gb1_ref[...] = jnp.zeros_like(gb1_ref)
-    for chunk in range(CHUNKS):
-        all_h[(chunk,) + own_slot] = low_ref[chunk * rows : (chunk + 1) * rows, :]
 
     def row_at(chunk, side):
         return pl.multiple_of((chunk * 2 + side) * half_rows, half_rows)
@@ -923,16 +951,161 @@
 
     def tiles(count, body):
         def step(at, carry):
-            body(pl.ds(pl.multiple_of(at * SPLIT, SPLIT), SPLIT))
+            body(at, pl.ds(pl.multiple_of(at * SPLIT, SPLIT), SPLIT))
             return carry
 
         lax.fori_loop(0, count // SPLIT, step, 0)
+
+    def pieces(chunk, side):
+        return [
+            pl.multiple_of((slot * 2 + side) * block + chunk * rows, rows)
+            for slot in range(GROUP // 2)
+        ]
+
+    def project_half(chunk, side, which):
+        columns = pl.ds(pl.multiple_of(which * (width // 2), width // 2), width // 2)
+        weight = wqkv_ref[which].reshape(width // 2, -1)
+        return jnp.dot(flat(all_m, chunk, side, columns), weight, preferred_element_type=f32)
+
+    def spill(src, dst, chunk, at):
+        copy = pltpu.make_async_copy(src.at[chunk], dst.at[chunk], spill_sems.at[at, chunk])
+        copy.start()
+        return copy
+
+    wide = slice(0, 3 * HEAD_DIM)
+    spills = {}
+
+    def token_flow(chunk):
+        share = yield from net.gather(all_m.at[chunk], 0, chunk)
+        up_ref[pl.ds(row_at(chunk, core), half_rows), wide] = project_half(chunk, core, group)
+        yield
+        share.wait()
+        up_ref[pl.ds(row_at(chunk, 1 - core), half_rows), wide] = project_half(
+            chunk, 1 - core, group
+        )
+        spills[0, chunk] = spill(all_m, x_all, chunk, 0)
+
+    def weight_flow():
+        yield
+        for copy in qkv_blocks:
+            copy.wait()
+        state["far_qkv"] = far(wqkv_ref.at[group], wqkv_ref.at[group], 3)
+        state["w1_blocks"] = exchange_blocks(
+            [(pack_w1, w1_all.at[group])],
+            (block_local.at[1:2], block_send.at[1:2], block_recv.at[1:2]), base, mine, others,
+        )
+        yield
+        for copy in near:
+            copy.wait()
+        far_vec.wait()
+        both = vec_all.at[:, mine]
+        state["vec"] = []
+        for step, other in enumerate(others):
+            copy = push(both, both, vec_send.at[step], vec_recv.at[step], other)
+            copy.start()
+            state["vec"].append(copy)
+        yield
+
+    state = {"backs": 0}
+    flows = [token_flow(chunk) for chunk in range(CHUNKS)]
+    step_through([flows[0], weight_flow()] + flows[1:])
+
+    for copy in state["vec"]:
+        copy.wait()
+    lane = lax.broadcasted_iota(jnp.int32, (8, 128), 1)
+    for at in range(GROUP):
+        first = vec_all[at // 8, at % 8 * 2]
+        second = vec_all[at // 8, at % 8 * 2 + 1]
+        here = slice(at * 128, at * 128 + 128)
+        low_ref[:, here] = jnp.where(lane < 64, first, pltpu.roll(second, 64, 1))
+        high_ref[:, here] = jnp.where(lane < 64, pltpu.roll(first, 64, 1), second)
+    for half in range(2):
+        for part in range(2):
+            b1_ref[0:1, half * 256 + part * 128 : half * 256 + part * 128 + 128] = vec_all[
+                half, mine, 4 + part : 5 + part, :
+            ]
+    head_at = pl.ds(pl.multiple_of(head * HEAD_DIM, HEAD_DIM), HEAD_DIM)
+    bias_q, bias_v = low_ref[0:1, head_at], high_ref[0:1, head_at]
+    bias_qkv = jnp.concatenate([bias_q, jnp.zeros_like(bias_q), bias_v], 1)
+    bo, shift_one, gain_two = low_ref[1:2, :], low_ref[2:3, :], low_ref[3:4, :]
+    gain_one, b2, shift_two = high_ref[1:2, :], high_ref[2:3, :], high_ref[3:4, :]
+
+    state["far_qkv"].wait()
+    far_wo_to = (1 - group) * GROUP + 2 * chip + group
+    far_wo = push(
+        wo_ref, wo_all.at[group, core], far_send.at[4 + core], far_recv.at[4 + core], far_wo_to
+    )
+    far_wo.start()
+    for chunk in range(CHUNKS):
+        for side in range(2):
+            here = pl.ds((chunk * 2 + side) * half_rows, half_rows)
+            total = up_ref[here, wide] + project_half(chunk, side, 1 - group) + bias_qkv
+            total = total.astype(low)
+            for slot, place in enumerate(pieces(chunk, side)):
+                qkv_ref[pl.ds(pl.multiple_of(ext + place, rows), rows), :] = total[
+                    slot * rows : (slot + 1) * rows
+                ]
+    halo_src = pl.ds(pl.multiple_of(PAD + 1792 - group * 1536, 64), HALO)
+    halo_dst = pl.ds(pl.multiple_of(PAD + 2048 * group, 64), HALO)
+    far_halo = far(qkv_ref.at[halo_src, :], qkv_ref.at[halo_dst, :], 6)
+    for copy in state["w1_blocks"]:
+        copy.wait()
+    far_w1 = far(w1_all.at[group], w1_all.at[group], 7)
+
+    def attend_tile(at):
+        tile = at + group * (GROUP - 1 - 2 * at)
+        row = pl.multiple_of(ext + tile * TILE, 64)
+        start = pl.multiple_of(ext - PAD + tile * TILE, 64)
+        place = pl.multiple_of(group * HALO + tile * TILE, TILE)
+        _, _, probs = tile_probs(
+            qkv_ref, row, start, seg_q_ref[pl.ds(place, TILE), :],
+            seg_k_ref[group * (HALO // TILE) + tile],
+        )
+        values = qkv_ref[pl.ds(start, WINDOW), 2 * HEAD_DIM : 3 * HEAD_DIM]
+        out = jnp.dot(probs.astype(low), values, preferred_element_type=f32)
+        att_ref[pl.ds(pl.multiple_of(tile * TILE, TILE), TILE), :] = out.astype(low)
+
+    def attend_two(at, carry):
+        attend_tile(2 * at)
+        attend_tile(2 * at + 1)
+        return carry
+
+    lax.fori_loop(0, own_rows // TILE // 2 - 1, attend_two, 0)
+    far_halo.wait()
+    attend_tile(own_rows // TILE - 2)
+    attend_tile(own_rows // TILE - 1)
+    for chunk in range(CHUNKS):
+        spills[0, chunk].wait()
+    wo_near.wait()
+    far_wo.wait_send()
+
+    @pl.when(core != group)
+    def _():
+        for at in range(2):
+            push(
+                wo_ref, wo_all.at[1 - group, at], far_send.at[4 + at], far_recv.at[4 + at],
+                far_wo_to,
+            ).wait_recv()
+
+    far_w2.append(far(w2_ref.at[w2_last, :], w2_all.at[group, w2_last, :], 8))
+
+    def branch_part(chunk, side, dst):
+        rows_in = jnp.concatenate([att_ref[pl.ds(at, rows), :] for at in pieces(chunk, side)], 0)
+        att_t[:, pl.ds(row_at(chunk, side), half_rows)] = rows_in.astype(f32).T.astype(low)
+
+        def body(at, columns):
+            weight = wo_all[core, :, :, columns].reshape(HEAD_DIM, SPLIT)
+            part = jnp.dot(rows_in, weight, preferred_element_type=f32)
+            dst[:, :, :, :, columns] = part.astype(low).reshape(2, 2, 2, rows, SPLIT)
+
+        tiles(width, body)
 
     def upward(chunk, side):
         here = pl.ds(row_at(chunk, side), half_rows)
 
-        def body(columns):
-            up = jnp.dot(flat(all_h, chunk, side), w1_ref[:, columns], preferred_element_type=f32)
+        def body(at, columns):
+            weight = w1_all[:, :, :, columns].reshape(width, SPLIT)
+            up = jnp.dot(flat(all_h, chunk, side), weight, preferred_element_type=f32)
             up = up + b1_ref[0:1, columns]
             up_ref[here, columns] = up
             act = gelu_tanh(up)
@@ -942,8 +1115,9 @@
         tiles(units, body)
 
     def downward(dst):
-        def body(columns):
-            part = jnp.dot(act_ref[...], w2_ref[:, columns], preferred_element_type=f32)
+        def body(at, columns):
+            weight = w2_all[:, :, columns].reshape(units, SPLIT)
+            part = jnp.dot(act_ref[...], weight, preferred_element_type=f32)
             dst[:, :, :, :, columns] = part.astype(low).reshape(2, 2, 2, rows, SPLIT)
 
         tiles(width, body)
@@ -951,42 +1125,34 @@
     def up_back(chunk, side):
         here = pl.ds(row_at(chunk, side), half_rows)
 
-        def body(columns):
+        def body(at, columns):
             grad = lax.dot_general(
-                flat(all_m, chunk, side), w2_ref[columns, :],
-                (((1,), (1,)), ((), ())), preferred_element_type=f32,
+                flat(all_m, chunk, side), w2_all[at], NT, preferred_element_type=f32
             )
-            up = up_ref[here, columns]
-            inner = 0.7978845608028654 * (up + 0.044715 * (up * up * up))
-            tanh = jnp.tanh(inner)
-            slope = 0.5 * (1.0 + tanh) + 0.5 * up * (1.0 - tanh * tanh) * (
-                0.7978845608028654 * (1.0 + 0.134145 * (up * up))
-            )
-            grad = (grad * slope).astype(low)
+            grad = (grad * gelu_slope(up_ref[here, columns])).astype(low)
             dup_ref[:, columns] = grad
-            wide = grad.astype(f32)
-            gb1_ref[0:1, columns] += jnp.sum(wide, 0, keepdims=True)
-            dup_t[columns, here] = wide.T.astype(low)
+            grad = grad.astype(f32)
+            gb1_ref[0:1, columns] += jnp.sum(grad, 0, keepdims=True)
+            dup_t[columns, here] = grad.T.astype(low)
 
         tiles(units, body)
 
     def down_back(dst):
-        def body(columns):
-            part = lax.dot_general(
-                dup_ref[...], w1_ref[columns, :],
-                (((1,), (1,)), ((), ())), preferred_element_type=f32,
-            )
+        def body(at, columns):
+            weight = w1_all[at // 4, pl.ds(at % 4 * 4, 4)].reshape(SPLIT, units)
+            part = lax.dot_general(dup_ref[...], weight, NT, preferred_element_type=f32)
             dst[:, :, :, :, columns] = part.astype(low).reshape(2, 2, 2, rows, SPLIT)
 
         tiles(width, body)
 
-    def share_part(stage, chunk):
-        copy = push(
-            far_part.at[chunk % 2], pair_in.at[chunk],
-            pair_send.at[stage, chunk], pair_recv.at[stage, chunk], net.pair,
-        )
-        copy.start()
-        return copy
+    def out_back(chunk, side):
+        weight = wo_all[core].reshape(HEAD_DIM, width)
+        grad = lax.dot_general(flat(all_h, chunk, side), weight, NT, preferred_element_type=f32)
+        grad = grad.astype(low)
+        for slot, place in enumerate(pieces(chunk, side)):
+            dout_ref[pl.ds(pl.multiple_of(group * HALO + place, rows), rows), :] = grad[
+                slot * rows : (slot + 1) * rows
+            ]
 
     def keep(chunk):
         def finish(row, first, count, total):
@@ -994,145 +1160,258 @@
 
         return finish
 
-    def norms(chunk):
-        for row in range(chunk * rows, (chunk + 1) * rows, 16):
-            at = slice(row, row + 16)
-            res = hid_ref[at, :] + res_ref[at, :] + par_ref[0:1, :]
-            mean = jnp.mean(res, -1, keepdims=True)
-            res = res - mean
-            scale = lax.rsqrt(jnp.mean(res * res, -1, keepdims=True) + norm_eps)
-            res = res * scale
-            out_ref[at, :] = (res * par_ref[1:2, :] + par_ref[2:3, :]).astype(low)
-            grad = cot_ref[at, :].astype(f32)
-            vec_ref[2:3, :] += jnp.sum(grad, 0, keepdims=True)
-            vec_ref[1:2, :] += jnp.sum(grad * res, 0, keepdims=True)
-            grad = grad * par_ref[1:2, :]
-            first = jnp.mean(grad, -1, keepdims=True)
-            second = jnp.mean(grad * res, -1, keepdims=True)
-            grad = (grad - first - res * second) * scale
-            dhid_ref[at, :] = grad
-            grad_low = grad.astype(low)
-            vec_ref[0:1, :] += jnp.sum(grad_low.astype(f32), 0, keepdims=True)
-            at_rows = slice(row - chunk * rows, row - chunk * rows + 16)
-            all_m[(chunk,) + own_slot + (at_rows, slice(None))] = grad_low
+    def row_sets(chunk):
+        for row in range(0, rows, 16):
+            yield slice(chunk * rows + row, chunk * rows + row + 16), slice(row, row + 16)
+
+    def normal(res):
+        res = res - jnp.mean(res, -1, keepdims=True)
+        scale = lax.rsqrt(jnp.mean(res * res, -1, keepdims=True) + norm_eps)
+        return res * scale, scale
+
+    def normal_back(grad, res, gain, scale, at):
+        vecg_ref[at + 2 : at + 3, :] += jnp.sum(grad, 0, keepdims=True)
+        vecg_ref[at + 1 : at + 2, :] += jnp.sum(grad * res, 0, keepdims=True)
+        grad = grad * gain
+        first = jnp.mean(grad, -1, keepdims=True)
+        second = jnp.mean(grad * res, -1, keepdims=True)
+        grad = (grad - first - res * second) * scale
+        grad_low = grad.astype(low)
+        vecg_ref[at : at + 1, :] += jnp.sum(grad_low.astype(f32), 0, keepdims=True)
+        return grad, grad_low
+
+    def norm_one(chunk):
+        for at, place in row_sets(chunk):
+            res, scale = normal(tok_ref[at, :].astype(f32) + res_ref[at, :] + bo)
+            norm_ref[at, :] = res
+            scale_ref[at, :] = jnp.broadcast_to(scale, (16, 128))
+            hidden = res * gain_one + shift_one
+            hid_ref[at, :] = hidden
+            all_h[(chunk,) + own_slot + (place, slice(None))] = hidden.astype(low)
+
+    def norm_two(chunk):
+        for at, place in row_sets(chunk):
+            res, scale = normal(hid_ref[at, :] + res_ref[at, :] + b2)
+            out_ref[at, :] = (res * gain_two + shift_two).astype(low)
+            grad, grad_low = normal_back(cot_ref[at, :].astype(f32), res, gain_two, scale, 0)
+            dres_ref[at, :] = grad
+            all_m[(chunk,) + own_slot + (place, slice(None))] = grad_low
+
+    def norm_one_back(chunk):
+        for at, place in row_sets(chunk):
+            grad, grad_low = normal_back(
+                dres_ref[at, :] + res_ref[at, :], norm_ref[at, :], gain_one,
+                scale_ref[at, 0:1], 3,
+            )
+            dres_ref[at, :] = grad
+            all_h[(chunk,) + own_slot + (place, slice(None))] = grad_low
 
     def flow(chunk):
         incoming = (in_one.at[chunk], in_two.at[chunk], in_three.at[chunk])
-        places = (own_part.at[chunk], pair_in.at[chunk], sums.at[chunk], incoming)
-        yield from net.gather(all_h.at[chunk], 0, chunk)
-        share = net.share
+        own, other = own_part.at[chunk], far_part.at[chunk % 2]
+        arrived = pair_in.at[chunk]
+        branch_part(chunk, 1 - core, other)
+        share = net.share(other, arrived, 1, chunk)
+        branch_part(chunk, core, own)
+        yield
+        yield from net.scatter(own, arrived, incoming, share, 1, chunk, keep(chunk))
+        norm_one(chunk)
+        share = yield from net.gather(all_h.at[chunk], 2, chunk)
+        if chunk == 0:
+            far_w1.wait()
         upward(chunk, core)
-        downward(own_part.at[chunk])
+        if chunk == 0:
+            for copy in far_w2:
+                copy.wait()
+        downward(own)
         yield
         share.wait()
+        spills[1, chunk] = spill(all_h, h_all, chunk, 1)
         upward(chunk, 1 - core)
-        downward(far_part.at[chunk % 2])
-        share = share_part(1, chunk)
+        downward(other)
+        share = net.share(other, arrived, 3, chunk)
         yield
-        yield from net.scatter(*places, share, 1, chunk, keep(chunk))
-        norms(chunk)
-        yield from net.gather(all_m.at[chunk], 2, chunk)
-        share = net.share
+        yield from net.scatter(own, arrived, incoming, share, 3, chunk, keep(chunk))
+        norm_two(chunk)
+        spills[1, chunk].wait()
+        share = yield from net.gather(all_m.at[chunk], 4, chunk)
         up_back(chunk, core)
-        down_back(own_part.at[chunk])
+        down_back(own)
         yield
         share.wait()
         up_back(chunk, 1 - core)
-        down_back(far_part.at[chunk % 2])
-        share = share_part(3, chunk)
+        down_back(other)
+        share = net.share(other, arrived, 5, chunk)
+        state["backs"] += 1
         yield
-        yield from net.scatter(*places, share, 3, chunk, keep(chunk))
-        here = slice(chunk * rows, (chunk + 1) * rows)
-        dhid_ref[here, :] += res_ref[here, :]
-
-    def weight_grads():
-        def product(left_t, right, out, columns):
-            total = None
-            for chunk in range(CHUNKS):
-                for side in range(2):
-                    here = slice((chunk * 2 + side) * half_rows, (chunk * 2 + side + 1) * half_rows)
-                    term = jnp.dot(
-                        left_t[:, here], flat(right, chunk, side, columns),
-                        preferred_element_type=f32,
-                    )
-                    total = term if total is None else total + term
-            return total
-
-        def run(left_t, right, out):
-            def step(at, carry):
-                columns = pl.ds(pl.multiple_of(at * SPLIT, SPLIT), SPLIT)
-                slot = at % 2
-
-                @pl.when(at >= 2)
-                def _():
-                    pltpu.make_async_copy(
-                        stage_ref.at[slot], out.at[:, columns], out_sems.at[slot]
-                    ).wait()
-
-                stage_ref[slot] = product(left_t, right, out, columns)
-                pltpu.make_async_copy(
-                    stage_ref.at[slot], out.at[:, columns], out_sems.at[slot]
-                ).start()
-                return carry
-
-            lax.fori_loop(0, width // SPLIT, step, 0)
-            for slot in range(2):
-                pltpu.make_async_copy(
-                    stage_ref.at[slot], out.at[:, pl.ds(0, SPLIT)], out_sems.at[slot]
-                ).wait()
-
-        run(act_t, all_m, gw2_ref)
-        run(dup_t, all_h, gw1_ref)
-
-    step_through([flow(chunk) for chunk in range(CHUNKS)])
-    weight_grads()
-
-
-def feed_forward(low, hidden, cotangent, w1, w2, b1, params):
+        yield from net.scatter(own, arrived, incoming, share, 5, chunk, keep(chunk))
+        norm_one_back(chunk)
+        share = yield from net.gather(all_h.at[chunk], 6, chunk)
+        out_back(chunk, core)
+        yield
+        share.wait()
+        out_back(chunk, 1 - core)
+
+    def product(left_t, right, columns):
+        total = None
+        for chunk in range(CHUNKS):
+            for side in range(2):
+                here = slice((chunk * 2 + side) * half_rows, (chunk * 2 + side + 1) * half_rows)
+                term = jnp.dot(
+                    left_t[:, here], flat(right, chunk, side, columns), preferred_element_type=f32
+                )
+                total = term if total is None else total + term
+        return total
+
+    def run(first, last, write):
+        def step(at, carry):
+            write(at, at % 2, at >= 2)
+            return carry
+
+        lax.fori_loop(first, last, step, 0)
+
+    def emit(src, dst, sem, again):
+        copy = pltpu.make_async_copy(src, dst, sem)
+
+        @pl.when(again)
+        def _():
+            copy.wait()
+
+        return copy
+
+    def columns_at(at):
+        return pl.ds(pl.multiple_of(at * SPLIT, SPLIT), SPLIT)
+
+    def write_w2(at, slot, again):
+        own = emit(stage_ref.at[slot, 0:256, :], gw2_own.at[:, columns_at(at)], out_sems.at[0, slot], again)
+        there = emit(stage_low.at[slot, 0:256, :], gw2_far.at[:, columns_at(at)], out_sems.at[1, slot], again)
+        total = product(act_t, all_m, columns_at(at))
+        first = group == 0
+        stage_ref[slot, 0:256, :] = jnp.where(first, total[:256], total[256:])
+        stage_low[slot, 0:256, :] = jnp.where(first, total[256:], total[:256]).astype(low)
+        own.start()
+        there.start()
+
+    def write_w1_own(at, slot, again):
+        own = emit(stage_ref.at[slot], gw1_own.at[:, columns_at(at)], out_sems.at[2, slot], again)
+        stage_ref[slot] = product(dup_t, all_m, columns_at(group * 4 + at))
+        own.start()
+
+    def write_w1_far(at, slot, again):
+        there = emit(stage_low.at[slot], gw1_far.at[:, columns_at(at)], out_sems.at[3, slot], again)
+        stage_low[slot] = product(dup_t, all_m, columns_at((1 - group) * 4 + at)).astype(low)
+        there.start()
+
+    def write_wo(at, slot, again):
+        own = emit(stage_ref.at[slot, 0:HEAD_DIM, :], gwo_ref.at[:, columns_at(at)], out_sems.at[4, slot], again)
+        stage_ref[slot, 0:HEAD_DIM, :] = product(att_t, all_h, columns_at(at))
+        own.start()
+
+    def fill():
+        while state["backs"] < CHUNKS:
+            yield
+        run(0, width // SPLIT // 2, write_w2)
+        yield
+        run(width // SPLIT // 2, width // SPLIT, write_w2)
+        for slot in range(2):
+            emit(stage_ref.at[slot, 0:256, :], gw2_own.at[:, columns_at(0)], out_sems.at[0, slot], True)
+            emit(stage_low.at[slot, 0:256, :], gw2_far.at[:, columns_at(0)], out_sems.at[1, slot], True)
+        back = [pltpu.make_async_copy(h_all.at[at], all_m.at[at], spill_sems.at[2, at]) for at in range(CHUNKS)]
+        for copy in back:
+            copy.start()
+        yield
+        for copy in back:
+            copy.wait()
+        run(0, width // SPLIT // 2, write_w1_own)
+        for slot in range(2):
+            emit(stage_ref.at[slot], gw1_own.at[:, columns_at(0)], out_sems.at[2, slot], True)
+        yield
+        run(0, width // SPLIT // 2, write_w1_far)
+        for slot in range(2):
+            emit(stage_low.at[slot], gw1_far.at[:, columns_at(0)], out_sems.at[3, slot], True)
+
+    step_through([flow(chunk) for chunk in range(CHUNKS)], fill())
+    halo_src = pl.ds(pl.multiple_of(1792 - group * 1536, 64), HALO)
+    halo_dst = pl.ds(pl.multiple_of(2048 * group, 64), HALO)
+    far_dout = far(dout_ref.at[halo_src, :], dout_ref.at[halo_dst, :], 9)
+    run(0, width // SPLIT, write_wo)
+    for slot in range(2):
+        emit(stage_ref.at[slot, 0:HEAD_DIM, :], gwo_ref.at[:, columns_at(0)], out_sems.at[4, slot], True)
+    far_dout.wait()
+
+
+def layer(tokens, cotangent, pack_qkv, pack_w1, w2, wo, vector, seg_q, seg_k):
     f32, bf16 = jnp.float32, jnp.bfloat16
-    block, width = low.shape
+    block, width = tokens.shape
     rows = block // CHUNKS
-    units = w1.shape[1]
+    unit_rows = w2.shape[0]
+    units = 2 * unit_rows
     half_rows = rows * GROUP // 2
-    all_rows = GROUP * block
+    own_rows = GROUP * block
+    weight_rows = wo.shape[0]
+    peers = GROUP - 1
     vmem = pl.BlockSpec(memory_space=pltpu.VMEM)
     anywhere = pl.BlockSpec(memory_space=pl.ANY)
     sems = pltpu.SemaphoreType.DMA
+    shape = jax.ShapeDtypeStruct
 
     def slots(*lead):
         return pltpu.VMEM(lead + (rows, width), bf16)
 
     return pl.pallas_call(
-        ff_kernel,
+        layer_kernel,
         out_shape=[
-            jax.ShapeDtypeStruct((block, width), bf16),
-            jax.ShapeDtypeStruct((block, width), f32),
-            jax.ShapeDtypeStruct((8, width), f32),
-            jax.ShapeDtypeStruct((8, units), f32),
-            jax.ShapeDtypeStruct((units, width), f32),
-            jax.ShapeDtypeStruct((units, width), f32),
+            shape((block, width), bf16),
+            shape((block, width), f32),
+            shape((8, width), f32),
+            shape((8, units), f32),
+            shape((unit_rows, width), f32),
+            shape((unit_rows, width), bf16),
+            shape((units, width // 2), f32),
+            shape((units, width // 2), bf16),
+            shape((HEAD_DIM, width), f32),
+            shape((CHUNKS, 2, 2, 2, 2, rows, width), bf16),
+            shape((CHUNKS, 2, 2, 2, 2, rows, width), bf16),
+            shape((own_rows + HALO + 2 * PAD, 3 * HEAD_DIM), bf16),
+            shape((own_rows + HALO, HEAD_DIM), bf16),
+            shape((2, GROUP, weight_rows, 3 * HEAD_DIM), bf16),
         ],
-        in_specs=[vmem] * 7,
-        out_specs=[vmem] * 4 + [anywhere] * 2,
+        in_specs=[vmem, vmem, anywhere, anywhere, anywhere, anywhere, vmem, vmem, vmem],
+        out_specs=[vmem] * 4 + [anywhere] * 7 + [vmem] * 3,
         scratch_shapes=[
             slots(CHUNKS, 2, 2, 2, 2), slots(CHUNKS, 2, 2, 2, 2),
             slots(CHUNKS, 2, 2, 2), slots(2, 2, 2, 2), slots(CHUNKS, 2, 2, 2),
-            slots(CHUNKS, 2, 2, 2), slots(CHUNKS, 2, 2), slots(CHUNKS, 2), slots(CHUNKS),
-            pltpu.VMEM((all_rows, units), f32),
+            slots(CHUNKS, 2, 2), slots(CHUNKS, 2), slots(CHUNKS),
+            pltpu.VMEM((own_rows, units), f32),
             pltpu.VMEM((half_rows, units), bf16),
-            pltpu.VMEM((units, all_rows), bf16),
+            pltpu.VMEM((units, own_rows), bf16),
             pltpu.VMEM((half_rows, units), bf16),
-            pltpu.VMEM((units, all_rows), bf16),
+            pltpu.VMEM((units, own_rows), bf16),
+            pltpu.VMEM((own_rows, HEAD_DIM), bf16),
+            pltpu.VMEM((HEAD_DIM, own_rows), bf16),
             pltpu.VMEM((block, width), f32),
+            pltpu.VMEM((block, width), f32),
+            pltpu.VMEM((block, width), f32),
+            pltpu.VMEM((block, 128), f32),
+            pltpu.VMEM((2, GROUP, weight_rows, units), bf16),
+            pltpu.VMEM((2, unit_rows, width), bf16),
+            pltpu.VMEM((2, 2, weight_rows, width), bf16),
+            pltpu.VMEM((2, GROUP, 8, 128), f32),
+            pltpu.VMEM((8, width), f32),
+            pltpu.VMEM((8, width), f32),
+            pltpu.VMEM((8, units), f32),
             pltpu.VMEM((2, units, SPLIT), f32),
-            sems((4, CHUNKS, 3, 3)), sems((4, CHUNKS, 3, 3)), sems((4, CHUNKS)), sems((4, CHUNKS)),
-            sems((2,)),
+            pltpu.VMEM((2, units, SPLIT), bf16),
+            sems((STAGES, CHUNKS, 3, 3)), sems((STAGES, CHUNKS, 3, 3)),
+            sems((STAGES, CHUNKS)), sems((STAGES, CHUNKS)),
+            sems((2,)), sems((2, peers)), sems((2, peers)), sems((peers,)), sems((peers,)),
+            sems((10,)), sems((10,)), sems((3,)), sems((5, 2)), sems((3, CHUNKS)),
         ],
         compiler_params=pltpu.CompilerParams(
             collective_id=4, has_side_effects=True, vmem_limit_bytes=63 << 20
         ),
-        name="feed_forward",
-    )(low, hidden, cotangent, w1, w2, b1, params)
+        name="layer",
+    )(tokens, cotangent, pack_qkv, pack_w1, w2, wo, vector, seg_q, seg_k)
 
 
 def grouped_device(
@@ -1190,25 +1469,6 @@
     sizes = [item.shape[0] for item in vectors]
     vector = jnp.concatenate(vectors).astype(f32)
     vector = jnp.pad(vector, (0, 1024 - vector.shape[0])).reshape(8, 128)
-    own_qkv, own_w1, gathered = weights_out(pack_qkv, pack_w1, vector)
-    own_qkv = own_qkv.reshape(GROUP * weight_rows, 3 * HEAD_DIM)
-    own_w1 = own_w1.reshape(GROUP * weight_rows, 2 * unit_rows)
-    full_qkv = in_order(own_qkv, lax.ppermute(own_qkv, "dp", across))
-    wo_pairs = [
-        (GROUP * g + 2 * k + g, GROUP * (1 - g) + 2 * k + g) for g in range(2) for k in range(8)
-    ]
-    gathered = gathered.reshape(devices, -1)
-    whole, at = [], 0
-    for size in sizes:
-        whole.append(gathered[:, at : at + size].reshape(-1))
-        at += size
-    all_bq, all_bv, all_bo, gain_one, shift_one, all_b2, gain_two, shift_two, all_b1 = whole
-    my_b1 = lax.dynamic_index_in_dim(
-        all_b1.reshape(2, GROUP, unit_rows), member, 1, keepdims=False
-    ).reshape(-1)
-    my_bq = lax.dynamic_slice_in_dim(all_bq, head * HEAD_DIM, HEAD_DIM)
-    my_bv = lax.dynamic_slice_in_dim(all_bv, head * HEAD_DIM, HEAD_DIM)
-    my_bqkv = jnp.concatenate([my_bq, jnp.zeros_like(my_bq), my_bv])
 
     ext_rows = own_rows + HALO
     ext_first = group * (own_rows - HALO)
@@ -1216,45 +1476,22 @@
     starts = jnp.cumsum(lengths) - lengths
     ext_ids = ext_first + jnp.arange(ext_rows, dtype=jnp.int32)
     seg = jnp.sum((ext_ids[:, None] >= starts[None, :]).astype(jnp.int32), 1)
-    tile_rows = jnp.arange(ext_rows // TILE, dtype=jnp.int32) * TILE
-    tile_starts = jnp.clip(tile_rows - (WINDOW - TILE) // 2, 0, ext_rows - WINDOW)
-    key_ids = ext_first + tile_starts[:, None] + jnp.arange(WINDOW, dtype=jnp.int32)[None, :]
+    tile_rows = jnp.arange(ext_rows // TILE, dtype=jnp.int32) * TILE - PAD
+    key_rows = tile_rows[:, None] + jnp.arange(WINDOW, dtype=jnp.int32)[None, :]
+    key_ids = ext_first + key_rows
     seg_k = jnp.sum((key_ids[:, :, None] >= starts[None, None, :]).astype(jnp.int32), 2)
-    seg_k = seg_k[:, None, :]
+    seg_k = jnp.where((key_rows >= 0) & (key_rows < ext_rows), seg_k, -1)[:, None, :]
     seg_q = seg[:, None]
 
-    def with_halo(rows):
-        edge = jnp.where(first_group, rows[own_rows - HALO :], rows[:HALO])
-        halo = lax.ppermute(edge, "dp", across)
-        return jnp.where(
-            first_group, jnp.concatenate([rows, halo], 0), jnp.concatenate([halo, rows], 0)
-        )
-
-    all_tokens = group_gather(tokens, "gather_tokens", 2)
-    all_tokens, own_w1, own_wo = lax.optimization_barrier((all_tokens, own_w1, wo))
-    wo_beside = lax.ppermute(own_wo, "dp", beside)
-    chip_wo = jnp.concatenate(
-        [jnp.where(core == 0, own_wo, wo_beside), jnp.where(core == 0, wo_beside, own_wo)], 0
-    )
-    full_wo = jnp.where(core == group, chip_wo, lax.ppermute(chip_wo, "dp", wo_pairs))
-    full_w1 = in_order(own_w1, lax.ppermute(own_w1, "dp", across))
-    qkv = (jnp.dot(all_tokens, full_qkv, preferred_element_type=f32) + my_bqkv).astype(bf16)
-    qkv_ext = with_halo(qkv)
-    attended = attend(offset.reshape(1), qkv_ext, seg_q, seg_k, own_rows)
-    attended, own_w2 = lax.optimization_barrier((attended, w2))
-    full_w2 = in_order(own_w2, lax.ppermute(own_w2, "dp", across))
-    branch_part = jnp.dot(attended, full_wo, preferred_element_type=f32).astype(bf16)
-    branch = group_scatter(branch_part, "scatter_branch", 3) + all_bo
-    resid_one = tokens.astype(f32) + branch
-    hidden, norm_one_back = jax.vjp(layer_norm, resid_one, gain_one, shift_one)
-
-    params = jnp.pad(jnp.stack([all_b2, gain_two, shift_two]), ((0, 5), (0, 0)))
-    output, grad_hidden, vec_two, grad_b1, grad_w2, grad_w1_t = feed_forward(
-        hidden.astype(bf16), hidden, cotangent, full_w1, full_w2,
-        jnp.broadcast_to(my_b1, (8, my_b1.shape[0])), params,
-    )
-    grad_b2, grad_gain_two, grad_shift_two = vec_two[0], vec_two[1], vec_two[2]
+    (
+        output, grad_resid_one, vec_grads, grad_b1, w2_own, w2_far, w1_own, w1_far, grad_wo,
+        all_tokens, _, qkv, grad_out, full_qkv,
+    ) = layer(tokens, cotangent, pack_qkv, pack_w1, w2, wo, vector, seg_q, seg_k)
+    grad_b2, grad_gain_two, grad_shift_two, grad_bo, grad_gain_one, grad_shift_one = [
+        vec_grads[at] for at in range(6)
+    ]
     grad_b1 = grad_b1[0]
+    out_w2 = w2_own + lax.ppermute(w2_far, "dp", across).astype(f32)
 
     def across_sum(grad):
         halves = grad.reshape((2, grad.shape[0] // 2) + grad.shape[1:])
@@ -1262,32 +1499,28 @@
         theirs = jnp.where(first_group, halves[1], halves[0]).astype(bf16)
         return mine + lax.ppermute(theirs, "dp", across).astype(f32)
 
-    out_w2 = across_sum(grad_w2)
-
-    grad_resid_one, grad_gain_one, grad_shift_one = norm_one_back(grad_hidden)
-    grad_branch = grad_resid_one.astype(bf16)
-    grad_bo = jnp.sum(grad_branch.astype(f32), 0)
-    all_grad_branch = group_gather(grad_branch, "gather_grad_branch", 8)
-    all_grad_branch, grad_w1_t = lax.optimization_barrier((all_grad_branch, grad_w1_t))
-    halves_t = jnp.split(grad_w1_t, 2, 1)
-    theirs_t = jnp.where(first_group, halves_t[1], halves_t[0]).astype(bf16)
-    sum_w1_t = jnp.where(first_group, halves_t[0], halves_t[1])
-    sum_w1_t = sum_w1_t + lax.ppermute(theirs_t, "dp", across).astype(f32)
-    sum_w1 = sum_w1_t.astype(bf16).T
-    grad_attended = jnp.einsum(
-        "td,cd->tc", all_grad_branch, full_wo, preferred_element_type=f32
-    ).astype(bf16)
-    grad_wo = jnp.einsum("tc,td->cd", attended, all_grad_branch, preferred_element_type=f32)
-    grad_qkv_ext = attend_back(qkv_ext, with_halo(grad_attended), seg_q, seg_k)
-    grad_qkv = lax.dynamic_slice_in_dim(grad_qkv_ext, offset, own_rows, 0)
+    grad_qkv_ext = attend_back(qkv, grad_out, seg_q, seg_k)
+    grad_qkv = lax.dynamic_slice_in_dim(grad_qkv_ext, PAD + offset, own_rows, 0)
+    grad_qkv, w1_far = lax.optimization_barrier((grad_qkv, w1_far))
+    sum_w1 = (w1_own + lax.ppermute(w1_far, "dp", across).astype(f32)).astype(bf16).T
     grad_bqkv = jnp.sum(grad_qkv.astype(f32), 0)
+    full_qkv = full_qkv.reshape(width, 3 * HEAD_DIM)
     input_part = jnp.einsum("tf,df->td", grad_qkv, full_qkv, preferred_element_type=f32)
-    grad_wqkv = jnp.einsum("td,tf->df", all_tokens, grad_qkv, preferred_element_type=f32)
+    grad_by_chunk = (
+        grad_qkv.reshape(8, 2, CHUNKS, block // CHUNKS, 3 * HEAD_DIM)
+        .transpose(2, 1, 0, 3, 4)
+        .reshape(own_rows, 3 * HEAD_DIM)
+    )
+    grad_wqkv = jnp.einsum(
+        "td,tf->df", all_tokens.reshape(own_rows, width), grad_by_chunk, preferred_element_type=f32
+    )
     sum_qkv = across_sum(grad_wqkv)
     input_sum = group_scatter(input_part.astype(bf16), "scatter_input", 9)
     input_grad = (grad_resid_one + input_sum).astype(bf16)
 
-    back_pairs = [(dst, src) for src, dst in wo_pairs]
+    back_pairs = [
+        (GROUP * (1 - g) + 2 * k + g, GROUP * g + 2 * k + g) for g in range(2) for k in range(8)
+    ]
     sum_wo = grad_wo + lax.ppermute(grad_wo.astype(bf16), "dp", back_pairs).astype(f32)
     halves = sum_wo.reshape(2, weight_rows, width)
     mine_wo = jnp.where(core == 0, halves[0], halves[1])

time: 681 us -> 601 us (0.88)
  waiting for transfers between devices: 48.2 us -> 0.01 us
  Pallas kernels: 487 us -> 516 us
  matrix products: 42.5 us -> 15.4 us
  other arithmetic: 40.2 us -> 20.2 us
  local copies, waits for them, and re-layouts: 37.1 us -> 28.3 us
    pallas_call x5 -> x1, Pallas kernels: 315 us -> 366 us  [layer(): pl.pallas_call(layer_kernel, out_shape=[shape((block, width), bf16), shap...]
    ppermute x8 -> x2, waiting for transfers between devices: 48.2 us -> 0.01 us  [the longest x1 0.01 us: grouped_device(): lax.ppermute(w1_far, 'dp', across).astype(f32)]
    dot_general x5 -> x1, matrix products: 34.8 us -> 6.96 us  [grouped_device(): jnp.einsum('td,tf->df', all_tokens.reshape(own_rows, width), grad_by_chun...]
    pallas_call x2 -> x1, Pallas kernels: 127 us -> 104 us  [group_scatter(): pl.pallas_call(scatter_kernel, out_shape=jax.ShapeDtypeStruct((count, wid...]
  transfers between devices with their start and end apart: 12 -> 5, of which waited for: 1 -> 0; matrix products, arithmetic and copies ran while one was open for 14% -> 8% of each run, Pallas kernels for 47% -> 25%
where the time goes in v4:
time: 601 us; the launch traced here: 591 us
  Pallas kernels  516 us (86%)
  local copies, waits for them, and re-layouts  28.3 us (5%)
  other arithmetic  20.2 us (3%)
  matrix products  15.4 us (3%)
  starting transfers between devices  9.06 us (2%)
    pallas_call x1, Pallas kernels, layer(): pl.pallas_call(layer_kernel, out_shape=[shape((block, width), bf16), shap...  366 us
    pallas_call x1, Pallas kernels, group_scatter(): pl.pallas_call(scatter_kernel, out_shape=jax.ShapeDtypeStruct((count, wid...  104 us
    pallas_call x1, Pallas kernels, weights_back(): pl.pallas_call(weights_back_kernel, out_shape=[jax.ShapeDtypeStruct(rows_...  30.4 us
    pallas_call x1, Pallas kernels, attend_back(): pl.pallas_call(attend_back_kernel, out_shape=jax.ShapeDtypeStruct(qkv.sha...  15.1 us
  transfers between devices with their start and end apart: 5, of which 0 were waited for; matrix products, arithmetic and copies ran while one was open for 8% of the time, Pallas kernels for 25%

profile of v4, /device:TPU:7, one launch (start us, length us, event | category | flops | bytes accessed | tf_op | source)
XLA Modules:
  0.0 590.7 jit_solution(5219241435096689694)
XLA Ops:
  0.7 0.1 add_add_fusion
  0.8 0.8 copy.76
  1.7 0.1 reduce
  1.8 0.7 sub.16
  2.4 0.2 convert_reduce_fusion.1
  2.7 0.7 and_select_fusion.seg_k_ref
  3.4 0.1 convert_reduce_fusion.2
  3.5 1.9 broadcast_in_dim.20.seg_q_ref
  5.4 0.2 copy.96
  5.7 1.0 copy.105
  6.7 1.5 reshape.239.pack_w1
  8.7 0.2 copy-done.15
  9.0 0.1 concatenate.10
  9.1 0.6 bitcast_convert_fusion.vec_ref
  9.7 1.0 pad_maximum_fusion.pack_qkv
  10.7 366.5 %layer.1 = (bf16[128,2048]{1,0:T(8,128)(2,1)}, f32[128,2048]{1,0:T(8,128)}, f32[8,2048]{1,0:T(8,128)}, f32[8,512]{1,0:T(8,128)}, f32[256,2048]{1,0:T(8,128)}, /*...) custom-call(bf16[128,2048]{1,0:T(8,128)(2,1)} %tok_ref.1, ...), custom_call_target="tpu_custom_call" | custom-call | tf_op jit(solution)/shard_map/layer/pallas_call | solution.py:1361
  377.2 0.8 collective-permute-start.4
  377.9 2.1 convert_element_type.114
  380.0 3.6 collective-permute-start.2
  383.6 15.1 %attend_back.1 = bf16[2688,384]{1,0:T(8,128)(2,1)} custom-call(bf16[2688,384]{1,0:T(8,128)(2,1)} %get-tuple-element.37.qkv_ref, bf16[2304,128]{1,0:T(8,128)(2,1)} %get-tuple-element.38.grad_ref, s32[2304,1]{1,0:T(8,128)} %broadcast_in_dim.20.seg_q_ref, s32[18,1,512]{2,1,0:T(1,128)} %and_select_fusion.seg_k_ref), custom_call_target="tpu_custom_call" | custom-call | tf_op jit(solution)/shard_map/attend_back/pallas_call | solution.py:747
  398.7 1.6 constant_dynamic-slice_fusion
  400.3 0.2 copy.80
  400.5 7.0 %fusion.3 = f32[2048,384]{1,0:T(8,128)S(1)} fusion(bf16[2048,2048]{1,0:T(8,128)(2,1)} %bitcast.106, bf16[2048,384]{1,0:T(8,128)(2,1)S(1)} %bitcast.89), kind=kOutput, calls=%fused_computation.41 | convolution fusion | flops 3221225472 | bytes 13107200 | tf_op jit(solution)/shard_map/td,tf->df/dot_general | solution.py:1514
  407.5 1.7 copy-done
  409.2 1.0 select_convert_fusion
  410.3 2.4 collective-permute-start
  412.6 0.3 convert_reduce_fusion
  413.0 0.1 slice_dynamic-update-slice_fusion.1
  413.1 0.1 reshape.251
  413.2 0.1 slice_dynamic-update-slice_fusion
  413.3 0.1 reshape.252
  413.4 0.7 slice_reduce_fusion.6
  414.2 0.1 slice_reduce_fusion
  414.3 0.1 reshape_squeeze.21
  414.8 8.4 %convolution_convert_fusion = bf16[2048,2048]{1,0:T(8,128)(2,1)} fusion(bf16[2048,384]{1,0:T(8,128)(2,1)S(1)} %constant_dynamic-slice_fusion, bf16[2048,384]{1,0:T(8,128)(2,1)} %bitcast.107), kind=kOutput, calls=%fused_computation | convolution fusion | flops 3225419776 | bytes 11534336 | tf_op jit(solution)/shard_map/tf,df->td/dot_general | solution.py:1508
  423.2 0.2 concatenate.11
  423.5 0.8 reshape.253.vec_ref
  424.2 104.2 %scatter_input.1 = f32[128,2048]{1,0:T(8,128)} custom-call(bf16[2,2,2,2,128,2048]{5,4,3,2,1,0:T(8,128)(2,1)} %bitcast.78), custom_call_target="tpu_custom_call" | custom-call | tf_op jit(solution)/shard_map/scatter_input/pallas_call | solution.py:541
  528.5 2.2 add_convert_fusion.2
  530.7 0.1 convert_add_fusion.1
  530.9 0.9 slice_select_fusion
  531.7 2.3 collective-permute-start.3
  534.0 2.3 add_convert_fusion.1
  536.4 1.6 fusion
  538.0 1.3 copy.79
  539.3 30.4 %weights_back.1 = (bf16[16,64,512]{2,1,0:T(8,128)(2,1)}, bf16[16,64,384]{2,1,0:T(8,128)(2,1)}, f32[8,128]{1,0:T(8,128)}) custom-call(bf16[16,64,512]{2,1,0:T(8,128)(2,1)} %bitcast.83, bf16[16,64,384]{2,1,0:T(8,128)(2,1)} %bitcast.84, f32[16,16,128]{2,1,0:T(8,128)} %reshape.253.vec_ref), custom_call_target="tpu_custom_call" | custom-call | tf_op jit(solution)/shard_map/weights_back/pallas_call | solution.py:671
  569.7 1.6 fusion.2
  571.3 1.2 fusion.1
  572.4 0.8 convert_bitcast_fusion.1
  573.3 0.8 convert_bitcast_fusion
  574.1 0.8 convert_bitcast_fusion.2
  575.0 1.6 convert_add_fusion
  576.6 1.2 slice_bitcast_fusion
  577.8 2.4 reshape.264
  580.2 1.2 copy.92
  581.4 2.5 copy.100
  583.9 0.3 copy.90
  584.3 0.3 copy.91
  584.6 0.4 copy-done.7
  585.0 0.3 copy.89
  585.3 1.0 copy.106
  586.3 1.3 copy_bitcast_fusion.1
  587.6 1.9 select_select_fusion
  589.5 0.8 copy.111
  (79 shorter events, 1.1 us)
Async XLA Ops:
  0.7 4.8 copy-start.8
  5.7 2.6 copy-start.11
  6.7 1.7 copy-start.12
  6.7 1.8 copy-start.13
  8.2 0.7 copy-start.15
  8.2 0.7 copy-start.16
  8.2 0.7 copy-start.17
  8.2 0.7 copy-start.18
  8.2 0.7 copy-start.19
  8.2 0.7 copy-start.20
  8.2 0.7 copy-start.21
  8.3 0.7 copy-start.22
  8.3 0.7 copy-start.23
  377.2 197.8 %collective-permute-start.4 = (bf16[256,2048]{1,0:T(8,128)(2,1)}, bf16[256,2048]{1,0:T(8,128)(2,1)S(1)}, u32[]{:S(2)}, u32[]{:S(2)}) collective-permute-start(bf16[256,2048]{1,0:T(8,128)(2,1)} %get-tuple-element.52), channel_id=1, source_target_pairs={{0,16},{1,17},{2,18},{3,19},{4,20},{5,21},{6,22},{7,23},{8,24},{9,... | collective-permute-start | bytes 3145736 | tf_op jit(solution)/shard_map/ppermute | solution.py:1494
  380.0 150.7 %collective-permute-start.2 = (bf16[128,2048]{1,0:T(8,128)(2,1)}, bf16[128,2048]{1,0:T(8,128)(2,1)S(1)}, u32[]{:S(2)}, u32[]{:S(2)}) collective-permute-start(bf16[128,2048]{1,0:T(8,128)(2,1)} %convert_element_type.114), channel_id=1, source_target_pairs={{16,0},{18,2},{20,4},{22,6},{24,8},{26,10},{28,12},{30,14},{1,17},... | collective-permute-start | bytes 1572872 | tf_op jit(solution)/shard_map/ppermute | solution.py:1524
  407.5 1.8 copy-start
  409.2 4.9 copy-start.14
  410.3 123.8 %collective-permute-start.1 = (bf16[1024,384]{1,0:T(8,128)(2,1)}, bf16[1024,384]{1,0:T(8,128)(2,1)}, u32[]{:S(2)}, u32[]{:S(2)}) collective-permute-start(bf16[1024,384]{1,0:T(8,128)(2,1)} %select_convert_fusion), channel_id=1, source_target_pairs={{0,16},{1,17},{2,18},{3,19},{4,20},{5,21},{6,22},{7,23},{8,24},{9,... | collective-permute-start | bytes 2359304 | tf_op jit(solution)/shard_map/ppermute | solution.py:1500
  410.3 126.1 %collective-permute-start = (bf16[512,1024]{1,0:T(8,128)(2,1)}, bf16[512,1024]{1,0:T(8,128)(2,1)}, u32[]{:S(2)}, u32[]{:S(2)}) collective-permute-start(bf16[512,1024]{1,0:T(8,128)(2,1)} %get-tuple-element.43), channel_id=1, source_target_pairs={{0,16},{1,17},{2,18},{3,19},{4,20},{5,21},{6,22},{7,23},{8,24},{9,... | collective-permute-start | bytes 3145736 | tf_op jit(solution)/shard_map/ppermute | solution.py:1505
  424.2 104.3 %copy-start.9 = (f32[128,2048]{1,0:T(8,128)S(1)}, f32[128,2048]{1,0:T(8,128)}, u32[]{:S(2)}) copy-start(f32[128,2048]{1,0:T(8,128)} %get-tuple-element.36) | copy-start | bytes 3145732
  528.5 2.2 copy-start.2
  530.7 3.3 copy-start.1
  531.7 4.6 copy-start.4
  531.7 55.9 %collective-permute-start.3 = (f32[64,2048]{1,0:T(8,128)}, f32[64,2048]{1,0:T(8,128)}, u32[]{:S(2)}, u32[]{:S(2)}) collective-permute-start(f32[64,2048]{1,0:T(8,128)} %slice_select_fusion), channel_id=1, source_target_pairs={{0,1},{1,0},{2,3},{3,2},{4,5},{5,4},{6,7},{7,6},{8,9},{9,8},{10,11... | collective-permute-start | bytes 1572872 | tf_op jit(solution)/shard_map/ppermute | solution.py:1528
  569.7 5.3 copy-start.3
  581.4 2.5 copy-start.5
  581.4 2.8 copy-start.6
  583.9 1.0 copy-start.7
  586.2 3.2 copy-start.10

commit v5 on v4

--- a/solution.py
+++ b/solution.py
@@ -350,210 +350,6 @@
     )
 
 
-def gather_kernel(x_ref, o_ref, local_sem, send_sem, recv_sem, pair_send, pair_recv):
-    device = lax.axis_index("dp")
-    core = device % 2
-    bits = chip_bits(device)
-    partners = [flip(device, 1), flip(device, 2), flip(device, 3)]
-    pair = flip(device, 0)
-    enter(partners + [pair])
-
-    def at(values, rows):
-        return o_ref.at[values[2], values[1], values[0], core, rows, slice(None)]
-
-    own = o_ref.at[bits[2], bits[1], bits[0], core]
-    local = pltpu.make_async_copy(x_ref, own, local_sem)
-    local.start()
-    hops, shares = {}, {}
-
-    def hop(part, step):
-        first, count = PORTIONS[part]
-        rows = pl.ds(first, count)
-        values = list(bits)
-        for dim in ORDERS[part][:step]:
-            values[dim] = slice(None)
-        dst = at(values, rows)
-        src = x_ref.at[rows, :] if step == 0 else dst
-        copy = push(
-            src, dst, send_sem.at[part, step], recv_sem.at[part, step], partners[ORDERS[part][step]]
-        )
-        copy.start()
-        hops[part, step] = copy
-
-    def share(part, step):
-        first, count = PORTIONS[part]
-        rows = pl.ds(first, count)
-        values = list(bits)
-        if step:
-            for dim in ORDERS[part][: step - 1]:
-                values[dim] = slice(None)
-            dim = ORDERS[part][step - 1]
-            values[dim] = 1 - bits[dim]
-        dst = at(values, rows)
-        src = dst if step else x_ref.at[rows, :]
-        copy = push(src, dst, pair_send.at[part, step], pair_recv.at[part, step], pair)
-        copy.start()
-        shares[part, step] = copy
-
-    for part in range(3):
-        hop(part, 0)
-    for part in range(3):
-        share(part, 0)
-    local.wait()
-    for step in (1, 2, 3):
-        for part in range(3):
-            hops[part, step - 1].wait_recv()
-            if step < 3:
-                hop(part, step)
-            share(part, step)
-    for copy in shares.values():
-        copy.wait()
-    for copy in hops.values():
-        copy.wait_send()
-
-
-def group_gather(rows, name, collective_id):
-    count, width = rows.shape
-    vmem = pl.BlockSpec(memory_space=pltpu.VMEM)
-    sems = pltpu.SemaphoreType.DMA
-    out = pl.pallas_call(
-        gather_kernel,
-        out_shape=jax.ShapeDtypeStruct((2, 2, 2, 2, count, width), rows.dtype),
-        in_specs=[vmem],
-        out_specs=vmem,
-        scratch_shapes=[sems, sems((3, 3)), sems((3, 3)), sems((3, 4)), sems((3, 4))],
-        compiler_params=pltpu.CompilerParams(
-            collective_id=collective_id, has_side_effects=True, vmem_limit_bytes=VMEM_LIMIT
-        ),
-        name=name,
-    )(rows)
-    return out.reshape(GROUP * count, width)
-
-
-def scatter_kernel(
-    x_ref, o_ref, pair_in, sums, in_one, in_two, in_three, send_sem, recv_sem, pair_send, pair_recv
-):
-    device = lax.axis_index("dp")
-    core = device % 2
-    bits = chip_bits(device)
-    partners = [flip(device, 1), flip(device, 2), flip(device, 3)]
-    pair = flip(device, 0)
-    width = x_ref.shape[-1]
-    f32 = jnp.float32
-    incoming = (in_one, in_two, in_three)
-    enter(partners + [pair])
-
-    def view(ref, values, rows, with_core=None):
-        where = (values[2], values[1], values[0])
-        if with_core is not None:
-            where = where + (with_core,)
-        return ref.at[where + (rows, slice(None))]
-
-    shares, hops = {}, {}
-    for half in range(2):
-        for part in range(3):
-            first, count = PORTIONS[part]
-            rows = pl.ds(first, count)
-            dim = ORDERS[part][0]
-            values = [slice(None)] * 3
-            values[dim] = 1 - bits[dim] if half == 0 else bits[dim]
-            copy = push(
-                view(x_ref, values, rows, 1 - core),
-                view(pair_in, values, rows),
-                pair_send.at[part, half],
-                pair_recv.at[part, half],
-                pair,
-            )
-            copy.start()
-            shares[part, half] = copy
-
-    def add_up(part, values, arrived, store):
-        first, count = PORTIONS[part]
-
-        def body(index, carry):
-            rows = pl.ds(pl.multiple_of(first + index * 16, 16), 16)
-            where = (values[2], values[1], values[0])
-            total = x_ref[where + (core, rows, slice(None))].astype(f32)
-            total = total + pair_in[where + (rows, slice(None))].astype(f32)
-            for ref in incoming[:arrived]:
-                total = total + ref[where + (rows, slice(None))].astype(f32)
-            store(where, rows, total)
-            return carry
-
-        lax.fori_loop(0, count // 16, body, 0)
-
-    def keep_sum(where, rows, total):
-        sums[where + (rows, slice(None))] = total.astype(sums.dtype)
-
-    def finish(where, rows, total):
-        o_ref[rows, :] = total
-
-    def hop(part, step):
-        first, count = PORTIONS[part]
-        order = ORDERS[part]
-        values = list(bits)
-        values[order[step]] = 1 - bits[order[step]]
-        free = order[step + 1 :]
-        for mask in range(1 << len(free)):
-            slot = list(values)
-            for place, dim in enumerate(free):
-                slot[dim] = (mask >> place) & 1
-            add_up(part, slot, step, keep_sum)
-        for dim in free:
-            values[dim] = slice(None)
-        rows = pl.ds(first, count)
-        copy = push(
-            view(sums, values, rows),
-            view(incoming[step], values, rows),
-            send_sem.at[part, step],
-            recv_sem.at[part, step],
-            partners[order[step]],
-        )
-        copy.start()
-        hops[part, step] = copy
-
-    for part in range(3):
-        shares[part, 0].wait_recv()
-        hop(part, 0)
-    for part in range(3):
-        shares[part, 1].wait_recv()
-        hops[part, 0].wait_recv()
-        hop(part, 1)
-    for part in range(3):
-        hops[part, 1].wait_recv()
-        hop(part, 2)
-    for part in range(3):
-        hops[part, 2].wait_recv()
-        add_up(part, bits, 3, finish)
-    for copy in shares.values():
-        copy.wait_send()
-    for copy in hops.values():
-        copy.wait_send()
-
-
-def group_scatter(partial, name, collective_id):
-    width = partial.shape[-1]
-    count = partial.shape[0] // GROUP
-    low = partial.dtype
-    vmem = pl.BlockSpec(memory_space=pltpu.VMEM)
-    sems = pltpu.SemaphoreType.DMA
-    slots = pltpu.VMEM((2, 2, 2, count, width), low)
-    return pl.pallas_call(
-        scatter_kernel,
-        out_shape=jax.ShapeDtypeStruct((count, width), jnp.float32),
-        in_specs=[vmem],
-        out_specs=vmem,
-        scratch_shapes=[
-            slots, slots, slots, slots, slots,
-            sems((3, 3)), sems((3, 3)), sems((3, 2)), sems((3, 2)),
-        ],
-        compiler_params=pltpu.CompilerParams(
-            collective_id=collective_id, has_side_effects=True, vmem_limit_bytes=VMEM_LIMIT
-        ),
-        name=name,
-    )(partial.reshape(2, 2, 2, 2, count, width))
-
-
 def exchange_blocks(pairs, sems, base, mine, others):
     local_sem, send_sem, recv_sem = sems
     copies = []
@@ -583,114 +379,6 @@
     return device // GROUP, base, mine, others, across
 
 
-def weights_out_kernel(
-    qkv_ref, w1_ref, vec_ref, qkv_out, w1_out, vec_out,
-    local_sem, send_sem, recv_sem, vec_local, far_send, far_recv, vec_send, vec_recv,
-):
-    group, base, mine, others, across = group_places()
-    enter(others + [across])
-    far = push(vec_ref, vec_out.at[group, mine], far_send, far_recv, across)
-    far.start()
-    local = pltpu.make_async_copy(vec_ref, vec_out.at[group, mine], vec_local)
-    local.start()
-    copies = exchange_blocks(
-        [(qkv_ref, qkv_out), (w1_ref, w1_out)], (local_sem, send_sem, recv_sem), base, mine, others
-    )
-    local.wait()
-    far.wait()
-    both = vec_out.at[:, mine]
-    for step, other in enumerate(others):
-        copy = push(both, both, vec_send.at[step], vec_recv.at[step], other)
-        copy.start()
-        copies.append(copy)
-    for copy in copies:
-        copy.wait()
-
-
-def weights_out(pack_qkv, pack_w1, vector):
-    anywhere = pl.BlockSpec(memory_space=pl.ANY)
-    vmem = pl.BlockSpec(memory_space=pltpu.VMEM)
-    sems = pltpu.SemaphoreType.DMA
-    peers = GROUP - 1
-    return pl.pallas_call(
-        weights_out_kernel,
-        out_shape=[
-            jax.ShapeDtypeStruct(pack_qkv.shape, pack_qkv.dtype),
-            jax.ShapeDtypeStruct(pack_w1.shape, pack_w1.dtype),
-            jax.ShapeDtypeStruct((2, GROUP) + vector.shape, vector.dtype),
-        ],
-        in_specs=[anywhere, anywhere, vmem],
-        out_specs=[anywhere, anywhere, vmem],
-        scratch_shapes=[
-            sems((2,)), sems((2, peers)), sems((2, peers)),
-            sems, sems, sems, sems((peers,)), sems((peers,)),
-        ],
-        compiler_params=pltpu.CompilerParams(
-            collective_id=1, has_side_effects=True, vmem_limit_bytes=VMEM_LIMIT
-        ),
-        name="weights_out",
-    )(pack_qkv, pack_w1, vector)
-
-
-def weights_back_kernel(
-    w1_ref, qkv_ref, vec_ref, w1_out, qkv_out, vec_out,
-    arrived, theirs, far_in, local_sem, send_sem, recv_sem, vec_sems, vec_send, vec_recv,
-    far_send, far_recv,
-):
-    group, base, mine, others, across = group_places()
-    enter(others + [across])
-    first = exchange_blocks(
-        [(vec_ref, arrived)], (vec_sems, vec_send, vec_recv), base, mine, others
-    )
-    copies = exchange_blocks(
-        [(w1_ref, w1_out), (qkv_ref, qkv_out)], (local_sem, send_sem, recv_sem), base, mine, others
-    )
-    for copy in first:
-        copy.wait()
-    total = arrived[0]
-    for at in range(1, GROUP):
-        total = total + arrived[at]
-    rows = total.shape[0] // 2
-    low, high = total[:rows], total[rows:]
-    theirs[...] = jnp.where(group == 0, high, low)
-    far = push(theirs, far_in, far_send, far_recv, across)
-    far.start()
-    own = jnp.where(group == 0, low, high)
-    far.wait()
-    vec_out[...] = own + far_in[...]
-    for copy in copies:
-        copy.wait()
-
-
-def weights_back(rows_w1, rows_qkv, vectors):
-    anywhere = pl.BlockSpec(memory_space=pl.ANY)
-    vmem = pl.BlockSpec(memory_space=pltpu.VMEM)
-    sems = pltpu.SemaphoreType.DMA
-    peers = GROUP - 1
-    half = (vectors.shape[1] // 2, vectors.shape[2])
-    return pl.pallas_call(
-        weights_back_kernel,
-        out_shape=[
-            jax.ShapeDtypeStruct(rows_w1.shape, rows_w1.dtype),
-            jax.ShapeDtypeStruct(rows_qkv.shape, rows_qkv.dtype),
-            jax.ShapeDtypeStruct(half, vectors.dtype),
-        ],
-        in_specs=[anywhere, anywhere, vmem],
-        out_specs=[anywhere, anywhere, vmem],
-        scratch_shapes=[
-            pltpu.VMEM(vectors.shape, vectors.dtype),
-            pltpu.VMEM(half, vectors.dtype),
-            pltpu.VMEM(half, vectors.dtype),
-            sems((2,)), sems((2, peers)), sems((2, peers)),
-            sems((1,)), sems((1, peers)), sems((1, peers)), sems, sems,
-        ],
-        compiler_params=pltpu.CompilerParams(
-            collective_id=10, has_side_effects=True, vmem_limit_bytes=VMEM_LIMIT
-        ),
-        name="weights_back",
-    )(rows_w1, rows_qkv, vectors)
-
-
 def tile_probs(qkv_ref, row, start, seg_q, seg_k):
     f32 = jnp.float32
     queries = qkv_ref[pl.ds(row, TILE), 0:HEAD_DIM]
@@ -701,62 +389,13 @@
     return queries, keys, weights / jnp.sum(weights, -1, keepdims=True)
 
 
-def attend_back_kernel(qkv_ref, grad_ref, seg_q_ref, seg_k_ref, o_ref, dq_sum, dk_sum, dv_sum):
-    total = qkv_ref.shape[0]
-    f32 = jnp.float32
-    low = qkv_ref.dtype
-    scale = HEAD_DIM ** (-0.5)
-    dq_sum[...] = jnp.zeros_like(dq_sum)
-    dk_sum[...] = jnp.zeros_like(dk_sum)
-    dv_sum[...] = jnp.zeros_like(dv_sum)
-
-    def body(tile, carry):
-        place = pl.multiple_of(tile * TILE, TILE)
-        row = pl.multiple_of(PAD + place, 64)
-        start = place
-        queries, keys, probs = tile_probs(
-            qkv_ref, row, start, seg_q_ref[pl.ds(place, TILE), :], seg_k_ref[tile]
-        )
-        window = pl.ds(start, WINDOW)
-        values = qkv_ref[window, 2 * HEAD_DIM : 3 * HEAD_DIM]
-        grads = grad_ref[pl.ds(place, TILE), :]
-        grad_probs = lax.dot_general(
-            grads, values, (((1,), (1,)), ((), ())), preferred_element_type=f32
-        )
-        inner = jnp.sum(probs * grad_probs, -1, keepdims=True)
-        grad_scores = (probs * (grad_probs - inner)).astype(low)
-        dq_sum[pl.ds(row, TILE), :] = jnp.dot(grad_scores, keys, preferred_element_type=f32)
-        dk_sum[window, :] += lax.dot_general(
-            grad_scores, queries, (((0,), (0,)), ((), ())), preferred_element_type=f32
-        )
-        dv_sum[window, :] += lax.dot_general(
-            probs.astype(low), grads, (((0,), (0,)), ((), ())), preferred_element_type=f32
-        )
-        return carry
-
-    lax.fori_loop(0, grad_ref.shape[0] // TILE, body, 0, unroll=2)
-    o_ref[:, 0:HEAD_DIM] = (dq_sum[...] * scale).astype(low)
-    o_ref[:, HEAD_DIM : 2 * HEAD_DIM] = (dk_sum[...] * scale).astype(low)
-    o_ref[:, 2 * HEAD_DIM : 3 * HEAD_DIM] = dv_sum[...].astype(low)
-
-
-def attend_back(qkv, grads, seg_q, seg_k):
-    vmem = pl.BlockSpec(memory_space=pltpu.VMEM)
-    total = qkv.shape[0]
-    acc = pltpu.VMEM((total, HEAD_DIM), jnp.float32)
-    return pl.pallas_call(
-        attend_back_kernel,
-        out_shape=jax.ShapeDtypeStruct(qkv.shape, qkv.dtype),
-        in_specs=[vmem, vmem, vmem, vmem],
-        out_specs=vmem,
-        scratch_shapes=[acc, acc, acc],
-        compiler_params=pltpu.CompilerParams(vmem_limit_bytes=VMEM_LIMIT),
-        name="attend_back",
-    )(qkv, grads, seg_q, seg_k)
-
-
 CHUNKS = 4
-COLUMNS = ((0, 768), (768, 640), (1408, 640))
+THIRDS = (((0, 768), (0, 1, 2)), ((768, 640), (1, 2, 0)), ((1408, 640), (2, 0, 1)))
+LIGHT = (
+    ((0, 512), (1, 2, 0)), ((512, 512), (0, 2, 1)), ((1024, 512), (1, 0, 2)), ((1536, 512), (0, 1, 2)),
+)
+PLANS = (THIRDS, LIGHT) + (THIRDS,) * 5
+TAIL_PLANS = (LIGHT,)
 SPLIT = 256
 PAD = (WINDOW - TILE) // 2
 STAGES = 7
@@ -776,7 +415,8 @@
 
 
 class Traffic:
-    def __init__(self, sems):
+    def __init__(self, sems, plans):
+        self.plans = plans
         self.hop_send, self.hop_recv, self.pair_send, self.pair_recv = sems
         device = lax.axis_index("dp")
         self.core = device % 2
@@ -792,7 +432,7 @@
             src, dst,
             self.hop_send.at[stage, chunk, part, step],
             self.hop_recv.at[stage, chunk, part, step],
-            self.partners[ORDERS[part][step]],
+            self.partners[self.plans[stage][part][1][step]],
         )
         copy.start()
         return copy
@@ -808,16 +448,16 @@
         mine = slots.at[self.core]
         hops = {}
         for step in range(3):
-            for part, (first, count) in enumerate(COLUMNS):
+            for part, ((first, count), order) in enumerate(self.plans[stage]):
                 if step:
                     hops[part, step - 1].wait_recv()
                 values = list(self.bits)
-                for dim in ORDERS[part][:step]:
+                for dim in order[:step]:
                     values[dim] = slice(None)
                 view = self.chips(mine, values, pl.ds(first, count))
                 hops[part, step] = self.push(view, view, stage, chunk, part, step)
             yield
-        for part in range(3):
+        for part in range(len(self.plans[stage])):
             hops[part, 2].wait_recv()
         share = self.share(mine, mine, stage, chunk)
         for copy in hops.values():
@@ -830,8 +470,7 @@
         hops = {}
         share.wait()
         for step in range(4):
-            for part, (first, count) in enumerate(COLUMNS):
-                order = ORDERS[part]
+            for part, ((first, count), order) in enumerate(self.plans[stage]):
                 columns = pl.ds(first, count)
                 if step:
                     hops[part, step - 1].wait_recv()
@@ -880,15 +519,16 @@
 
 
 NT = (((1,), (1,)), ((), ()))
+TN = (((0,), (0,)), ((), ()))
 
 
 def layer_kernel(
     tok_ref, cot_ref, pack_qkv, pack_w1, w2_ref, wo_ref, vec_ref, seg_q_ref, seg_k_ref,
-    out_ref, dres_ref, vecg_ref, gb1_ref, gw2_own, gw2_far, gw1_own, gw1_far, gwo_ref,
+    out_ref, dres_ref, vecg_ref, gb1_ref, gw2_own, gw2_far, gw2_in, gw1_own, gw1_far, gw1_in, gwo_ref,
     x_all, h_all, qkv_ref, dout_ref, wqkv_ref,
     all_h, all_m, own_part, far_part, pair_in, in_one, in_two, in_three,
     up_ref, act_ref, act_t, dup_ref, dup_t, att_ref, att_t, res_ref, hid_ref, norm_ref, scale_ref,
-    w1_all, w2_all, wo_all, vec_all, low_ref, high_ref, b1_ref, stage_ref, stage_low,
+    w1_all, w2_all, wo_all, vec_all, low_ref, high_ref, b1_ref, stage_ref, stage_low, stage_w1, stage_w1_low,
     hop_send, hop_recv, pair_send, pair_recv,
     block_local, block_send, block_recv, vec_send, vec_recv, far_send, far_recv,
     local_sems, out_sems, spill_sems,
@@ -900,7 +540,7 @@
     own_rows = GROUP * block
     units = w1_all.shape[-1]
     group, base, mine, others, across = group_places()
-    net = Traffic((hop_send, hop_recv, pair_send, pair_recv))
+    net = Traffic((hop_send, hop_recv, pair_send, pair_recv), PLANS)
     core, bits = net.core, net.bits
     chip = mine // 2
     head = core * 8 + chip
@@ -918,7 +558,7 @@
         copy.start()
         return copy
 
-    early = w2_ref.shape[0] // 4
+    early = w2_ref.shape[0] // 2
     far_vec = far(vec_ref, vec_all.at[group, mine], 0)
     near = [
         local(vec_ref, vec_all.at[group, mine], 0),
@@ -1051,6 +691,7 @@
     for copy in state["w1_blocks"]:
         copy.wait()
     far_w1 = far(w1_all.at[group], w1_all.at[group], 7)
+    far_w2.append(far(w2_ref.at[w2_last, :], w2_all.at[group, w2_last, :], 8))
 
     def attend_tile(at):
         tile = at + group * (GROUP - 1 - 2 * at)
@@ -1087,8 +728,6 @@
                 far_wo_to,
             ).wait_recv()
 
-    far_w2.append(far(w2_ref.at[w2_last, :], w2_all.at[group, w2_last, :], 8))
-
     def branch_part(chunk, side, dst):
         rows_in = jnp.concatenate([att_ref[pl.ds(at, rows), :] for at in pieces(chunk, side)], 0)
         att_t[:, pl.ds(row_at(chunk, side), half_rows)] = rows_in.astype(f32).T.astype(low)
@@ -1283,23 +922,23 @@
         return pl.ds(pl.multiple_of(at * SPLIT, SPLIT), SPLIT)
 
     def write_w2(at, slot, again):
-        own = emit(stage_ref.at[slot, 0:256, :], gw2_own.at[:, columns_at(at)], out_sems.at[0, slot], again)
-        there = emit(stage_low.at[slot, 0:256, :], gw2_far.at[:, columns_at(at)], out_sems.at[1, slot], again)
+        own = emit(stage_ref.at[slot], gw2_own.at[:, columns_at(at)], out_sems.at[0, slot], again)
+        there = emit(stage_low.at[slot], gw2_far.at[:, columns_at(at)], out_sems.at[1, slot], again)
         total = product(act_t, all_m, columns_at(at))
         first = group == 0
-        stage_ref[slot, 0:256, :] = jnp.where(first, total[:256], total[256:])
-        stage_low[slot, 0:256, :] = jnp.where(first, total[256:], total[:256]).astype(low)
+        stage_ref[slot] = jnp.where(first, total[:256], total[256:])
+        stage_low[slot] = jnp.where(first, total[256:], total[:256]).astype(low)
         own.start()
         there.start()
 
     def write_w1_own(at, slot, again):
-        own = emit(stage_ref.at[slot], gw1_own.at[:, columns_at(at)], out_sems.at[2, slot], again)
-        stage_ref[slot] = product(dup_t, all_m, columns_at(group * 4 + at))
+        own = emit(stage_w1.at[slot], gw1_own.at[columns_at(at), :], out_sems.at[2, slot], again)
+        stage_w1[slot] = product(dup_t, all_m, columns_at(group * 4 + at)).T
         own.start()
 
     def write_w1_far(at, slot, again):
-        there = emit(stage_low.at[slot], gw1_far.at[:, columns_at(at)], out_sems.at[3, slot], again)
-        stage_low[slot] = product(dup_t, all_m, columns_at((1 - group) * 4 + at)).astype(low)
+        there = emit(stage_w1_low.at[slot], gw1_far.at[columns_at(at), :], out_sems.at[3, slot], again)
+        stage_w1_low[slot] = product(dup_t, all_m, columns_at((1 - group) * 4 + at)).T.astype(low)
         there.start()
 
     def write_wo(at, slot, again):
@@ -1314,22 +953,26 @@
         yield
         run(width // SPLIT // 2, width // SPLIT, write_w2)
         for slot in range(2):
-            emit(stage_ref.at[slot, 0:256, :], gw2_own.at[:, columns_at(0)], out_sems.at[0, slot], True)
-            emit(stage_low.at[slot, 0:256, :], gw2_far.at[:, columns_at(0)], out_sems.at[1, slot], True)
+            emit(stage_ref.at[slot], gw2_own.at[:, columns_at(0)], out_sems.at[0, slot], True)
+            emit(stage_low.at[slot], gw2_far.at[:, columns_at(0)], out_sems.at[1, slot], True)
+        swaps.append(far(gw2_far, gw2_in, 10))
         back = [pltpu.make_async_copy(h_all.at[at], all_m.at[at], spill_sems.at[2, at]) for at in range(CHUNKS)]
         for copy in back:
             copy.start()
         yield
         for copy in back:
             copy.wait()
+        run(0, width // SPLIT // 2, write_w1_far)
+        for slot in range(2):
+            emit(stage_w1_low.at[slot], gw1_far.at[columns_at(0), :], out_sems.at[3, slot], True)
+        early_w1 = gw1_far.at[pl.ds(0, width // 4), :]
+        swaps.append(far(early_w1, gw1_in, 11))
+        yield
         run(0, width // SPLIT // 2, write_w1_own)
         for slot in range(2):
-            emit(stage_ref.at[slot], gw1_own.at[:, columns_at(0)], out_sems.at[2, slot], True)
-        yield
-        run(0, width // SPLIT // 2, write_w1_far)
-        for slot in range(2):
-            emit(stage_low.at[slot], gw1_far.at[:, columns_at(0)], out_sems.at[3, slot], True)
-
+            emit(stage_w1.at[slot], gw1_own.at[columns_at(0), :], out_sems.at[2, slot], True)
+
+    swaps = []
     step_through([flow(chunk) for chunk in range(CHUNKS)], fill())
     halo_src = pl.ds(pl.multiple_of(1792 - group * 1536, 64), HALO)
     halo_dst = pl.ds(pl.multiple_of(2048 * group, 64), HALO)
@@ -1338,6 +981,8 @@
     for slot in range(2):
         emit(stage_ref.at[slot, 0:HEAD_DIM, :], gwo_ref.at[:, columns_at(0)], out_sems.at[4, slot], True)
     far_dout.wait()
+    for copy in swaps:
+        copy.wait()
 
 
 def layer(tokens, cotangent, pack_qkv, pack_w1, w2, wo, vector, seg_q, seg_k):
@@ -1367,8 +1012,10 @@
             shape((8, units), f32),
             shape((unit_rows, width), f32),
             shape((unit_rows, width), bf16),
-            shape((units, width // 2), f32),
-            shape((units, width // 2), bf16),
+            shape((unit_rows, width), bf16),
+            shape((width // 2, units), f32),
+            shape((width // 2, units), bf16),
+            shape((width // 4, units), bf16),
             shape((HEAD_DIM, width), f32),
             shape((CHUNKS, 2, 2, 2, 2, rows, width), bf16),
             shape((CHUNKS, 2, 2, 2, 2, rows, width), bf16),
@@ -1377,7 +1024,7 @@
             shape((2, GROUP, weight_rows, 3 * HEAD_DIM), bf16),
         ],
         in_specs=[vmem, vmem, anywhere, anywhere, anywhere, anywhere, vmem, vmem, vmem],
-        out_specs=[vmem] * 4 + [anywhere] * 7 + [vmem] * 3,
+        out_specs=[vmem] * 4 + [anywhere] * 9 + [vmem] * 3,
         scratch_shapes=[
             slots(CHUNKS, 2, 2, 2, 2), slots(CHUNKS, 2, 2, 2, 2),
             slots(CHUNKS, 2, 2, 2), slots(2, 2, 2, 2), slots(CHUNKS, 2, 2, 2),
@@ -1400,18 +1047,361 @@
             pltpu.VMEM((8, width), f32),
             pltpu.VMEM((8, width), f32),
             pltpu.VMEM((8, units), f32),
-            pltpu.VMEM((2, units, SPLIT), f32),
-            pltpu.VMEM((2, units, SPLIT), bf16),
-            sems((STAGES, CHUNKS, 3, 3)), sems((STAGES, CHUNKS, 3, 3)),
+            pltpu.VMEM((2, SPLIT, SPLIT), f32),
+            pltpu.VMEM((2, SPLIT, SPLIT), bf16),
+            pltpu.VMEM((2, SPLIT, units), f32),
+            pltpu.VMEM((2, SPLIT, units), bf16),
+            sems((STAGES, CHUNKS, 4, 3)), sems((STAGES, CHUNKS, 4, 3)),
             sems((STAGES, CHUNKS)), sems((STAGES, CHUNKS)),
             sems((2,)), sems((2, peers)), sems((2, peers)), sems((peers,)), sems((peers,)),
-            sems((10,)), sems((10,)), sems((3,)), sems((5, 2)), sems((3, CHUNKS)),
+            sems((12,)), sems((12,)), sems((3,)), sems((5, 2)), sems((3, CHUNKS)),
         ],
         compiler_params=pltpu.CompilerParams(
             collective_id=4, has_side_effects=True, vmem_limit_bytes=63 << 20
         ),
         name="layer",
     )(tokens, cotangent, pack_qkv, pack_w1, w2, wo, vector, seg_q, seg_k)
+
+
+def tail_kernel(
+    qkv_ref, dout_ref, seg_q_ref, seg_k_ref, wqkv_ref, dres_ref, gwo_ref, parts_ref,
+    x_all, w1_own, w1_far, w1_early, w2_own, w2_early,
+    input_ref, out_q, out_k, out_v, out_wo, out_w1, out_w2, vec_ref,
+    xs_ref, own_part, far_part, pair_in, in_one, in_two, in_three, res_ref,
+    dqkv_ref, dk_sum, dv_sum, dqkv_t, gq_own, gq_far, gq_in, gq_send, gq_recv,
+    w1_sum, w1_in, w1_send, w1_recv, w2_sum, w2_in, wo_low, wo_in, wo_pair, wo_pair_in,
+    blocks_ref, arrived, theirs, far_vec_in,
+    hop_send, hop_recv, pair_send, pair_recv, load_sems,
+    block_local, block_send, block_recv, far_send, far_recv,
+):
+    f32, low = jnp.float32, qkv_ref.dtype
+    block, width = dres_ref.shape
+    rows = block // CHUNKS
+    half_rows = rows * GROUP // 2
+    weight_rows = out_q.shape[0]
+    scale = HEAD_DIM ** (-0.5)
+    group, base, mine, others, across = group_places()
+    net = Traffic((hop_send, hop_recv, pair_send, pair_recv), TAIL_PLANS)
+    core, chip = net.core, mine // 2
+    enter(others + [across, flip(across, 0)])
+
+    def far(src, dst, at, device=across):
+        copy = push(src, dst, far_send.at[at], far_recv.at[at], device)
+        copy.start()
+        return copy
+
+    def load(src, dst, at):
+        copy = pltpu.make_async_copy(src, dst, load_sems.at[at])
+        copy.start()
+        return copy
+
+    far_wo = push(
+        wo_low, wo_in, far_send.at[0], far_recv.at[0], core * GROUP + 2 * chip + core
+    )
+
+    @pl.when(core != group)
+    def _():
+        wo_low[...] = gwo_ref[...].astype(low)
+        far_wo.start()
+
+    half = w1_far.shape[0] // 2
+    late = pl.ds(half, half)
+    far_w1 = far(w1_far.at[late, :], w1_in.at[late, :], 1)
+    x_loads = [load(x_all.at[at], xs_ref.at[at], at) for at in range(CHUNKS)]
+    loads = [
+        load(w1_own, w1_sum, CHUNKS),
+        load(w1_early, w1_in.at[pl.ds(0, half), :], CHUNKS + 1),
+        load(w2_own, w2_sum, CHUNKS + 2),
+        load(w2_early, w2_in, CHUNKS + 3),
+    ]
+    blocks_ref[...] = parts_ref[...]
+    dk_sum[...] = jnp.zeros_like(dk_sum)
+    dv_sum[...] = jnp.zeros_like(dv_sum)
+
+    def attend_back_tile(tile):
+        place = pl.multiple_of(tile * TILE, TILE)
+        row = pl.multiple_of(PAD + place, 64)
+        window = pl.ds(place, WINDOW)
+        queries, keys, probs = tile_probs(
+            qkv_ref, row, place, seg_q_ref[pl.ds(place, TILE), :], seg_k_ref[tile]
+        )
+        values = qkv_ref[window, 2 * HEAD_DIM : 3 * HEAD_DIM]
+        grads = dout_ref[pl.ds(place, TILE), :]
+        grad_probs = lax.dot_general(grads, values, NT, preferred_element_type=f32)
+        inner = jnp.sum(probs * grad_probs, -1, keepdims=True)
+        grad_scores = (probs * (grad_probs - inner)).astype(low)
+        grad_q = jnp.dot(grad_scores, keys, preferred_element_type=f32)
+        dqkv_ref[pl.ds(place, TILE), 0:HEAD_DIM] = (grad_q * scale).astype(low)
+        dk_sum[window, :] += lax.dot_general(grad_scores, queries, TN, preferred_element_type=f32)
+        dv_sum[window, :] += lax.dot_general(
+            probs.astype(low), grads, TN, preferred_element_type=f32
+        )
+
+    def attend_back_two(at, carry):
+        attend_back_tile(2 * at)
+        attend_back_tile(2 * at + 1)
+        return carry
+
+    ext_rows = dout_ref.shape[0]
+    lax.fori_loop(0, ext_rows // TILE // 2, attend_back_two, 0)
+    inside = slice(PAD, PAD + ext_rows)
+    dqkv_ref[:, HEAD_DIM : 2 * HEAD_DIM] = (dk_sum[inside, :] * scale).astype(low)
+    dqkv_ref[:, 2 * HEAD_DIM : 3 * HEAD_DIM] = dv_sum[inside, :].astype(low)
+
+    def rows_of(chunk, side):
+        return jnp.concatenate(
+            [
+                dqkv_ref[
+                    pl.ds(
+                        pl.multiple_of(
+                            group * HALO + (slot * 2 + side) * block + chunk * rows, rows
+                        ),
+                        rows,
+                    ),
+                    :,
+                ]
+                for slot in range(GROUP // 2)
+            ],
+            0,
+        )
+
+    bias = jnp.zeros((1, 3 * HEAD_DIM), f32)
+    for chunk in range(CHUNKS):
+        for side in range(2):
+            part = rows_of(chunk, side).astype(f32)
+            bias = bias + jnp.sum(part, 0, keepdims=True)
+            here = slice((chunk * 2 + side) * half_rows, (chunk * 2 + side + 1) * half_rows)
+            dqkv_t[:, here] = part.T.astype(low)
+
+    for copy in x_loads:
+        copy.wait()
+
+    def product(at):
+        columns = pl.ds(pl.multiple_of(at * SPLIT, SPLIT), SPLIT)
+        total = None
+        for chunk in range(CHUNKS):
+            for side in range(2):
+                here = slice((chunk * 2 + side) * half_rows, (chunk * 2 + side + 1) * half_rows)
+                right = xs_ref[chunk, side, :, :, :, :, columns].reshape(half_rows, SPLIT)
+                term = jnp.dot(dqkv_t[:, here], right, preferred_element_type=f32)
+                total = term if total is None else total + term
+        return total.T
+
+    quarter = width // SPLIT // 2
+
+    def far_tile(at, carry):
+        here = pl.ds(pl.multiple_of(at * SPLIT, SPLIT), SPLIT)
+        gq_far[here, :] = product((1 - group) * quarter + at).astype(low)
+        return carry
+
+    def own_tile(at, carry):
+        here = pl.ds(pl.multiple_of(at * SPLIT, SPLIT), SPLIT)
+        gq_own[here, :] = product(group * quarter + at)
+        return carry
+
+    lax.fori_loop(0, quarter, far_tile, 0)
+    far_qkv = far(gq_far, gq_in, 2)
+
+    bias_q, bias_v = bias[:, 0:HEAD_DIM], bias[:, 2 * HEAD_DIM : 3 * HEAD_DIM]
+    lane = lax.broadcasted_iota(jnp.int32, (1, 128), 1)
+    blocks_ref[2 * chip, pl.ds(core * 8, 1), :] = jnp.where(
+        lane < 64, bias_q, pltpu.roll(bias_v, 64, 1)
+    )
+    blocks_ref[2 * chip + 1, pl.ds(core * 8, 1), :] = jnp.where(
+        lane < 64, pltpu.roll(bias_q, 64, 1), bias_v
+    )
+
+    def blocks(pairs, at):
+        here = slice(at, at + len(pairs))
+        return exchange_blocks(
+            pairs, (block_local.at[here], block_send.at[here], block_recv.at[here]),
+            base, mine, others,
+        )
+
+    vec_blocks = blocks([(blocks_ref, arrived)], 0)
+
+    def input_part(chunk, side, dst):
+        left = rows_of(chunk, side)
+
+        def body(at, carry):
+            weight = wqkv_ref[at // 4, pl.ds(at % 4 * 4, 4)].reshape(SPLIT, 3 * HEAD_DIM)
+            part = lax.dot_general(left, weight, NT, preferred_element_type=f32)
+            columns = pl.ds(pl.multiple_of(at * SPLIT, SPLIT), SPLIT)
+            dst[:, :, :, :, columns] = part.astype(low).reshape(2, 2, 2, rows, SPLIT)
+            return carry
+
+        lax.fori_loop(0, width // SPLIT, body, 0)
+
+    def flow(chunk):
+        def finish(row, first, count, total):
+            res_ref[chunk * rows + row : chunk * rows + row + 16, first : first + count] = total
+
+        incoming = (in_one.at[chunk], in_two.at[chunk], in_three.at[chunk])
+        other = far_part.at[chunk % 2]
+        input_part(chunk, 1 - core, other)
+        share = net.share(other, pair_in.at[chunk], 0, chunk)
+        input_part(chunk, core, own_part.at[chunk])
+        yield
+        yield from net.scatter(
+            own_part.at[chunk], pair_in.at[chunk], incoming, share, 0, chunk, finish
+        )
+        here = slice(chunk * rows, (chunk + 1) * rows)
+        input_ref[here, :] = (dres_ref[here, :] + res_ref[here, :]).astype(low)
+
+    def fill():
+        yield
+        yield
+        for copy in loads:
+            copy.wait()
+        out_w2[...] = w2_sum[...] + w2_in[...].astype(f32)
+        yield
+        lax.fori_loop(0, quarter, own_tile, 0)
+        yield
+        for copy in vec_blocks:
+            copy.wait()
+        total = arrived[0]
+        for at in range(1, GROUP):
+            total = total + arrived[at]
+        first, second = total[:8], total[8:]
+        theirs[...] = jnp.where(group == 0, second, first)
+        vec_ref[...] = jnp.where(group == 0, first, second)
+        state["vec"] = far(theirs, far_vec_in, 3)
+
+    state = {}
+    step_through([flow(chunk) for chunk in range(CHUNKS)], fill())
+
+    share_wo = push(wo_pair, wo_pair_in, far_send.at[4], far_recv.at[4], net.pair)
+
+    @pl.when(core == group)
+    def _():
+        far_wo.wait_recv()
+        total = gwo_ref[...] + wo_in[...].astype(f32)
+        first, second = total[:weight_rows], total[weight_rows:]
+        out_wo[...] = jnp.where(core == 0, first, second)
+        wo_pair[...] = jnp.where(core == 0, second, first)
+        share_wo.start()
+
+    far_w1.wait()
+
+    def add_w1(at, carry):
+        here = pl.ds(pl.multiple_of(at * weight_rows, weight_rows), weight_rows)
+        w1_send[at] = (w1_sum[here, :] + w1_in[here, :].astype(f32)).astype(low)
+        return carry
+
+    lax.fori_loop(0, GROUP, add_w1, 0)
+    w1_blocks = blocks([(w1_send, w1_recv)], 1)
+    state["vec"].wait()
+    vec_ref[...] += far_vec_in[...]
+
+    @pl.when(core != group)
+    def _():
+        far_wo.wait_send()
+        share_wo.wait_recv()
+        out_wo[...] = wo_pair_in[...]
+
+    @pl.when(core == group)
+    def _():
+        share_wo.wait_send()
+
+    far_qkv.wait()
+
+    def add_qkv(at, carry):
+        here = pl.ds(pl.multiple_of(at * weight_rows, weight_rows), weight_rows)
+        gq_send[at] = (gq_own[here, :] + gq_in[here, :].astype(f32)).astype(low)
+        return carry
+
+    lax.fori_loop(0, GROUP, add_qkv, 0)
+    qkv_blocks = blocks([(gq_send, gq_recv)], 2)
+    for copy in w1_blocks:
+        copy.wait()
+    unit_rows = w1_recv.shape[-1] // 2
+    for at in range(GROUP):
+        for part in range(2):
+            first = (part * GROUP + at) * unit_rows
+            out_w1[:, first : first + unit_rows] = w1_recv[
+                at, :, part * unit_rows : (part + 1) * unit_rows
+            ].astype(f32)
+    for copy in qkv_blocks:
+        copy.wait()
+    for at in range(GROUP):
+        first = (at % 2 * 8 + at // 2) * HEAD_DIM
+        for part, ref in enumerate((out_q, out_k, out_v)):
+            ref[:, first : first + HEAD_DIM] = gq_recv[
+                at, :, part * HEAD_DIM : (part + 1) * HEAD_DIM
+            ].astype(f32)
+
+
+def layer_tail(
+    qkv, dout, seg_q, seg_k, wqkv, dres, gwo, parts, x_all, w1_own, w1_far, w1_early, w2_own, w2_early
+):
+    f32, bf16 = jnp.float32, jnp.bfloat16
+    block, width = dres.shape
+    rows = block // CHUNKS
+    weight_rows = wqkv.shape[2]
+    units = w1_own.shape[1]
+    unit_rows = units // 2
+    own_rows = GROUP * block
+    half_width = width // 2
+    peers = GROUP - 1
+    vmem = pl.BlockSpec(memory_space=pltpu.VMEM)
+    anywhere = pl.BlockSpec(memory_space=pl.ANY)
+    sems = pltpu.SemaphoreType.DMA
+    shape, scratch = jax.ShapeDtypeStruct, pltpu.VMEM
+    heads = 3 * HEAD_DIM
+
+    def slots(*lead):
+        return scratch(lead + (rows, width), bf16)
+
+    return pl.pallas_call(
+        tail_kernel,
+        out_shape=[
+            shape((block, width), bf16),
+            shape((weight_rows, width), f32),
+            shape((weight_rows, width), f32),
+            shape((weight_rows, width), f32),
+            shape((weight_rows, width), f32),
+            shape((weight_rows, GROUP * units), f32),
+            shape((unit_rows, width), f32),
+            shape((8, 128), f32),
+        ],
+        in_specs=[vmem] * 8 + [anywhere] * 6,
+        out_specs=[vmem] * 8,
+        scratch_shapes=[
+            slots(CHUNKS, 2, 2, 2, 2),
+            slots(CHUNKS, 2, 2, 2), slots(2, 2, 2, 2), slots(CHUNKS, 2, 2, 2),
+            slots(CHUNKS, 2, 2), slots(CHUNKS, 2), slots(CHUNKS),
+            scratch((block, width), f32),
+            scratch((own_rows + HALO, heads), bf16),
+            scratch(qkv.shape[:1] + (HEAD_DIM,), f32),
+            scratch(qkv.shape[:1] + (HEAD_DIM,), f32),
+            scratch((heads, own_rows), bf16),
+            scratch((half_width, heads), f32),
+            scratch((half_width, heads), bf16),
+            scratch((half_width, heads), bf16),
+            scratch((GROUP, weight_rows, heads), bf16),
+            scratch((GROUP, weight_rows, heads), bf16),
+            scratch((half_width, units), f32),
+            scratch((half_width, units), bf16),
+            scratch((GROUP, weight_rows, units), bf16),
+            scratch((GROUP, weight_rows, units), bf16),
+            scratch((unit_rows, width), f32),
+            scratch((unit_rows, width), bf16),
+            scratch((HEAD_DIM, width), bf16),
+            scratch((HEAD_DIM, width), bf16),
+            scratch((weight_rows, width), f32),
+            scratch((weight_rows, width), f32),
+            scratch(parts.shape, f32),
+            scratch(parts.shape, f32),
+            scratch((8, 128), f32),
+            scratch((8, 128), f32),
+            sems((1, CHUNKS, 4, 3)), sems((1, CHUNKS, 4, 3)), sems((1, CHUNKS)), sems((1, CHUNKS)),
+            sems((CHUNKS + 4,)), sems((3,)), sems((3, peers)), sems((3, peers)), sems((5,)), sems((5,)),
+        ],
+        compiler_params=pltpu.CompilerParams(
+            collective_id=5, has_side_effects=True, vmem_limit_bytes=63 << 20
+        ),
+        name="layer_tail",
+    )(qkv, dout, seg_q, seg_k, wqkv, dres, gwo, parts, x_all, w1_own, w1_far, w1_early, w2_own, w2_early)
 
 
 def grouped_device(
@@ -1446,15 +1436,6 @@
     group, member = device // GROUP, device % GROUP
     chip, core = member // 2, member % 2
     head = core * 8 + chip
-    first_group = group == 0
-    across = [(at, (at + GROUP) % devices) for at in range(devices)]
-    beside = [(at, at + 1 - 2 * (at % 2)) for at in range(devices)]
-
-    def swap(own, other):
-        return jnp.where(first_group, own, other), jnp.where(first_group, other, own)
-
-    def in_order(own, other):
-        return jnp.concatenate(swap(own, other), 0)
 
     def by_head(weight):
         return weight.reshape(weight_rows, 2, 8, HEAD_DIM).transpose(2, 1, 0, 3).reshape(
@@ -1484,67 +1465,27 @@
     seg_q = seg[:, None]
 
     (
-        output, grad_resid_one, vec_grads, grad_b1, w2_own, w2_far, w1_own, w1_far, grad_wo,
-        all_tokens, _, qkv, grad_out, full_qkv,
+        output, grad_resid_one, vec_grads, grad_b1, w2_own, _, w2_early, w1_own, w1_far, w1_early,
+        grad_wo, all_tokens, _, qkv, grad_out, full_qkv,
     ) = layer(tokens, cotangent, pack_qkv, pack_w1, w2, wo, vector, seg_q, seg_k)
+
+    spread_b1 = lax.dynamic_update_slice_in_dim(
+        jnp.zeros((2, GROUP, unit_rows), f32), grad_b1[0].reshape(2, 1, unit_rows), member, 1
+    )
     grad_b2, grad_gain_two, grad_shift_two, grad_bo, grad_gain_one, grad_shift_one = [
         vec_grads[at] for at in range(6)
     ]
-    grad_b1 = grad_b1[0]
-    out_w2 = w2_own + lax.ppermute(w2_far, "dp", across).astype(f32)
-
-    def across_sum(grad):
-        halves = grad.reshape((2, grad.shape[0] // 2) + grad.shape[1:])
-        mine = jnp.where(first_group, halves[0], halves[1])
-        theirs = jnp.where(first_group, halves[1], halves[0]).astype(bf16)
-        return mine + lax.ppermute(theirs, "dp", across).astype(f32)
-
-    grad_qkv_ext = attend_back(qkv, grad_out, seg_q, seg_k)
-    grad_qkv = lax.dynamic_slice_in_dim(grad_qkv_ext, PAD + offset, own_rows, 0)
-    grad_qkv, w1_far = lax.optimization_barrier((grad_qkv, w1_far))
-    sum_w1 = (w1_own + lax.ppermute(w1_far, "dp", across).astype(f32)).astype(bf16).T
-    grad_bqkv = jnp.sum(grad_qkv.astype(f32), 0)
-    full_qkv = full_qkv.reshape(width, 3 * HEAD_DIM)
-    input_part = jnp.einsum("tf,df->td", grad_qkv, full_qkv, preferred_element_type=f32)
-    grad_by_chunk = (
-        grad_qkv.reshape(8, 2, CHUNKS, block // CHUNKS, 3 * HEAD_DIM)
-        .transpose(2, 1, 0, 3, 4)
-        .reshape(own_rows, 3 * HEAD_DIM)
-    )
-    grad_wqkv = jnp.einsum(
-        "td,tf->df", all_tokens.reshape(own_rows, width), grad_by_chunk, preferred_element_type=f32
-    )
-    sum_qkv = across_sum(grad_wqkv)
-    input_sum = group_scatter(input_part.astype(bf16), "scatter_input", 9)
-    input_grad = (grad_resid_one + input_sum).astype(bf16)
-
-    back_pairs = [
-        (GROUP * (1 - g) + 2 * k + g, GROUP * g + 2 * k + g) for g in range(2) for k in range(8)
-    ]
-    sum_wo = grad_wo + lax.ppermute(grad_wo.astype(bf16), "dp", back_pairs).astype(f32)
-    halves = sum_wo.reshape(2, weight_rows, width)
-    mine_wo = jnp.where(core == 0, halves[0], halves[1])
-    theirs_wo = jnp.where(core == 0, halves[1], halves[0])
-    out_wo = jnp.where(core == group, mine_wo, lax.ppermute(theirs_wo, "dp", beside))
-    def place_head(vector):
-        return lax.dynamic_update_slice_in_dim(
-            jnp.zeros((width,), f32), vector, head * HEAD_DIM, 0
-        )
-
-    spread_b1 = lax.dynamic_update_slice_in_dim(
-        jnp.zeros((2, GROUP, unit_rows), f32), grad_b1.reshape(2, 1, unit_rows), member, 1
-    )
+    none = jnp.zeros((width,), f32)
     items = [
-        place_head(grad_bqkv[:HEAD_DIM]), place_head(grad_bqkv[2 * HEAD_DIM :]), grad_bo,
-        grad_gain_one, grad_shift_one, grad_b2, grad_gain_two, grad_shift_two, spread_b1,
+        none, none, grad_bo, grad_gain_one, grad_shift_one, grad_b2, grad_gain_two, grad_shift_two,
+        spread_b1,
     ]
     parts = jnp.concatenate([item.reshape(2, GROUP, -1) for item in items], 2)
     parts = jnp.pad(parts, ((0, 0), (0, 0), (0, 1024 - parts.shape[2])))
     parts = parts.transpose(1, 0, 2).reshape(GROUP, 16, 128)
-    rows_w1, rows_qkv, sums = weights_back(
-        sum_w1.astype(bf16).reshape(GROUP, weight_rows, 2 * unit_rows),
-        sum_qkv.astype(bf16).reshape(GROUP, weight_rows, 3 * HEAD_DIM),
-        parts,
+    input_grad, out_q, out_k, out_v, out_wo, out_w1, out_w2, sums = layer_tail(
+        qkv, grad_out, seg_q, seg_k, full_qkv, grad_resid_one, grad_wo, parts,
+        all_tokens, w1_own, w1_far, w1_early, w2_own, w2_early,
     )
     sums, at = sums.reshape(-1), 0
     small = []
@@ -1552,21 +1493,6 @@
         small.append(sums[at : at + size])
         at += size
     out_bq, out_bv, out_bo, out_g1, out_s1, out_b2, out_g2, out_s2, out_b1 = small
-    out_w1 = (
-        rows_w1.reshape(GROUP, weight_rows, 2, unit_rows)
-        .transpose(1, 2, 0, 3)
-        .reshape(weight_rows, units)
-        .astype(f32)
-    )
-    out_q, out_k, out_v = [
-        rows_qkv[:, :, at * HEAD_DIM : (at + 1) * HEAD_DIM]
-        .reshape(8, 2, weight_rows, HEAD_DIM)
-        .transpose(2, 1, 0, 3)
-        .reshape(weight_rows, width)
-        .astype(f32)
-        for at in range(3)
-    ]
-
     return (
         output, input_grad, out_q, out_bq, out_k, out_v, out_bv, out_wo, out_bo, out_g1, out_s1,
         out_w1, out_b1, out_w2, out_b2, out_g2, out_s2,

time: 601 us -> 575 us (0.957)
  Pallas kernels: 516 us -> 539 us
  other arithmetic: 20.2 us -> 3.69 us
  matrix products: 15.4 us -> 0 us
  starting transfers between devices: 9.06 us -> 0 us
    pallas_call x1, Pallas kernels: 366 us -> 417 us  [layer(): pl.pallas_call(layer_kernel, out_shape=[shape((block, width), bf16), shap...]
    pallas_call x3 -> x1, Pallas kernels: 150 us -> 122 us  [layer_tail(): pl.pallas_call(tail_kernel, out_shape=[shape((block, width), bf16), shape...]
    dot_general x2 -> x0, matrix products: 15.4 us -> none  [the longest x1 8.4 us: grouped_device(): jnp.einsum('tf,df->td', grad_qkv, full_qkv, preferred_element_type=f32)]
    convert_element_type x7 -> x0, other arithmetic: 10.2 us -> none  [the longest x3 2.54 us: grouped_device(): out_q, out_k, out_v = [rows_qkv[:, :, at * HEAD_DIM:(at + 1) * HEAD_DIM]....]
    ppermute x5 -> x0, starting transfers between devices: 9.06 us -> none  [the longest x1 3.6 us: grouped_device(): lax.ppermute(grad_wo.astype(bf16), 'dp', back_pairs).astype(f32)]
  transfers between devices with their start and end apart: 5 -> 0, of which waited for: 0 -> 0; matrix products, arithmetic and copies ran while one was open for 8% -> 0% of each run, Pallas kernels for 25% -> 0%
where the time goes in v5:
time: 575 us; the launch traced here: 566 us
  Pallas kernels  539 us (94%)
  local copies, waits for them, and re-layouts  22.4 us (4%)
    pallas_call x1, Pallas kernels, layer(): pl.pallas_call(layer_kernel, out_shape=[shape((block, width), bf16), shap...  417 us
    pallas_call x1, Pallas kernels, layer_tail(): pl.pallas_call(tail_kernel, out_shape=[shape((block, width), bf16), shape...  122 us

profile of v5, /device:TPU:7, one launch (start us, length us, event | category | flops | bytes accessed | tf_op | source)
XLA Modules:
  0.0 566.3 jit_solution(717339401400930256)
XLA Ops:
  0.7 0.0 copy-start.2
  0.7 0.1 add_add_fusion
  0.8 0.8 copy.63
  1.6 0.1 reduce-window.9
  1.6 0.1 reduce
  1.7 0.7 sub.13
  2.4 0.2 convert_reduce_fusion
  2.7 0.7 and_select_fusion.seg_k_ref
  3.4 0.1 convert_reduce_fusion.1
  3.5 1.9 broadcast_in_dim.20.seg_q_ref
  5.4 0.0 copy-done.2
  5.4 0.2 copy.75
  5.7 1.0 copy.77
  6.7 0.0 copy-start.8
  6.7 0.0 copy-start.9
  6.7 1.5 reshape.178.pack_w1
  8.2 0.0 copy-done.8
  8.2 0.1 copy.59
  8.3 0.0 copy-done.9
  8.4 0.0 copy-start.11
  8.4 0.0 copy-start.12
  8.4 0.0 copy-start.13
  8.4 0.0 copy-start.14
  8.4 0.0 copy-start.15
  8.4 0.0 copy-start.16
  8.4 0.0 copy-start.17
  8.4 0.0 copy-start.18
  8.5 0.0 copy-start.19
  8.5 0.1 copy.60
  8.5 0.6 copy-done.10
  9.2 0.1 copy.61
  9.3 1.1 pad_maximum_fusion.pack_qkv
  10.3 0.0 copy-done.11
  10.3 0.0 copy-done.12
  10.3 0.0 copy-done.13
  10.4 0.1 concatenate.13
  10.5 0.6 bitcast_convert_fusion.vec_ref
  11.1 417.1 %layer.1 = (bf16[128,2048]{1,0:T(8,128)(2,1)}, f32[128,2048]{1,0:T(8,128)}, f32[8,2048]{1,0:T(8,128)}, f32[8,512]{1,0:T(8,128)}, f32[256,2048]{1,0:T(8,128)}, /*...) custom-call(bf16[128,2048]{1,0:T(8,128)(2,1)} %tok_ref.1, ...), custom_call_target="tpu_custom_call" | custom-call | tf_op jit(solution)/shard_map/layer/pallas_call | solution.py:1006
  428.1 0.7 slice_reduce_fusion.6
  428.9 1.2 slice_reduce_fusion
  430.2 0.1 reshape_squeeze.21
  430.2 0.1 reshape_squeeze.22
  430.3 0.1 reshape_squeeze.23
  430.4 0.1 reshape_squeeze.24
  430.5 0.1 reshape_squeeze.25
  430.6 0.1 reshape_squeeze.26
  430.7 0.2 concatenate.15
  430.9 0.8 reshape.183.parts_ref
  431.7 121.8 %layer_tail.1 = (bf16[128,2048]{1,0:T(8,128)(2,1)}, f32[64,2048]{1,0:T(8,128)}, f32[64,2048]{1,0:T(8,128)}, f32[64,2048]{1,0:T(8,128)}, f32[64,2048]{1,0:T(8,128...) custom-call(bf16[2688,384]{1,0:T(8,128)(2,1)} %get-tuple-element.40.qkv_ref, ...), custom_call_target="tpu_custom_call" | custom-call | tf_op jit(solution)/shard_map/layer_tail/pallas_call | solution.py:1355
  553.5 0.0 copy-start.7
  553.5 1.6 fusion
  555.1 1.2 slice_bitcast_fusion
  556.3 0.8 copy.87
  557.1 1.9 copy.88
  559.0 0.0 copy-done.7
  559.0 0.8 copy.89
  559.8 0.0 copy-done.6
  559.8 0.8 copy.90
  560.6 0.0 copy-done.5
  560.6 0.8 copy.91
  561.4 0.8 copy.92
  562.2 1.3 copy.93
  563.6 1.0 copy-done
  564.6 1.3 copy.94
  (32 shorter events, 0.3 us)
Async XLA Ops:
  0.7 4.7 copy-start.2
  6.7 1.5 copy-start.8
  6.7 1.6 copy-start.9
  8.2 0.9 copy-start.10
  8.4 2.0 copy-start.11
  8.4 2.0 copy-start.12
  8.4 1.9 copy-start.13
  8.4 1.9 copy-start.14
  8.4 1.9 copy-start.15
  8.4 1.9 copy-start.16
  8.4 1.9 copy-start.17
  8.4 1.9 copy-start.18
  8.5 1.9 copy-start.19
  431.7 124.6 %copy-start.3 = (bf16[128,2048]{1,0:T(8,128)(2,1)S(1)}, bf16[128,2048]{1,0:T(8,128)(2,1)}, u32[]{:S(2)}) copy-start(bf16[128,2048]{1,0:T(8,128)(2,1)} %get-tuple-element.92) | copy-start | bytes 1572868
  553.5 5.6 copy-start.7
  556.3 3.5 copy-start.6
  557.1 3.5 copy-start.5
  559.0 2.4 copy-start.4
  559.8 2.4 copy-start.1
  562.2 2.3 copy-start

commit v6 on v5

--- a/solution.py
+++ b/solution.py
@@ -370,13 +370,30 @@
     return copies
 
 
+def far_blocks(src, dst, send_sem, recv_sem, group, mine):
+    copies = []
+    for step in range(GROUP):
+        member = (mine + step) % GROUP
+        copy = push(
+            src.at[member],
+            dst.at[mine],
+            send_sem.at[step],
+            recv_sem.at[step],
+            (1 - group) * GROUP + member,
+        )
+        copy.start()
+        copies.append(copy)
+    return copies
+
+
 def group_places():
     device = lax.axis_index("dp")
     base = device // GROUP * GROUP
     mine = device % GROUP
     others = [base + (mine + step) % GROUP for step in range(1, GROUP)]
     across = (device + GROUP) % (2 * GROUP)
-    return device // GROUP, base, mine, others, across
+    there = [GROUP - base + (mine + step) % GROUP for step in range(GROUP)]
+    return device // GROUP, base, mine, others, across, there
 
 
 def tile_probs(qkv_ref, row, start, seg_q, seg_k):
@@ -390,6 +407,7 @@
 
 
 CHUNKS = 4
+TAIL_CHUNKS = 2
 THIRDS = (((0, 768), (0, 1, 2)), ((768, 640), (1, 2, 0)), ((1408, 640), (2, 0, 1)))
 LIGHT = (
     ((0, 512), (1, 2, 0)), ((512, 512), (0, 2, 1)), ((1024, 512), (1, 0, 2)), ((1536, 512), (0, 1, 2)),
@@ -398,6 +416,7 @@
 TAIL_PLANS = (LIGHT,)
 SPLIT = 256
 PAD = (WINDOW - TILE) // 2
+REACH = SEQ_MAX
 STAGES = 7
 
 
@@ -524,13 +543,13 @@
 
 def layer_kernel(
     tok_ref, cot_ref, pack_qkv, pack_w1, w2_ref, wo_ref, vec_ref, seg_q_ref, seg_k_ref,
-    out_ref, dres_ref, vecg_ref, gb1_ref, gw2_own, gw2_far, gw2_in, gw1_own, gw1_far, gw1_in, gwo_ref,
+    out_ref, dres_ref, vecg_ref, gb1_ref, gw2_own, gw2_far, gw2_in, gw1_ref, gw1_in, gwo_ref,
     x_all, h_all, qkv_ref, dout_ref, wqkv_ref,
     all_h, all_m, own_part, far_part, pair_in, in_one, in_two, in_three,
     up_ref, act_ref, act_t, dup_ref, dup_t, att_ref, att_t, res_ref, hid_ref, norm_ref, scale_ref,
-    w1_all, w2_all, wo_all, vec_all, low_ref, high_ref, b1_ref, stage_ref, stage_low, stage_w1, stage_w1_low,
+    w1_all, w2_all, wo_all, vec_all, low_ref, high_ref, b1_ref, stage_ref, stage_low, stage_w1,
     hop_send, hop_recv, pair_send, pair_recv,
-    block_local, block_send, block_recv, vec_send, vec_recv, far_send, far_recv,
+    block_local, block_send, block_recv, there_send, there_recv, vec_send, vec_recv, far_send, far_recv,
     local_sems, out_sems, spill_sems,
 ):
     f32, low = jnp.float32, tok_ref.dtype
@@ -539,14 +558,14 @@
     half_rows = rows * GROUP // 2
     own_rows = GROUP * block
     units = w1_all.shape[-1]
-    group, base, mine, others, across = group_places()
+    group, base, mine, others, across, there = group_places()
     net = Traffic((hop_send, hop_recv, pair_send, pair_recv), PLANS)
     core, bits = net.core, net.bits
     chip = mine // 2
     head = core * 8 + chip
     own_slot = (core, bits[2], bits[1], bits[0])
     ext = PAD + group * HALO
-    enter(others + [across, flip(across, 0)])
+    enter(others + there)
 
     def far(src, dst, at, device=across):
         copy = push(src, dst, far_send.at[at], far_recv.at[at], device)
@@ -578,8 +597,15 @@
     )
     wo_near.start()
 
-    qkv_ref[0:PAD, :] = jnp.zeros((PAD, qkv_ref.shape[1]), low)
-    qkv_ref[qkv_ref.shape[0] - PAD :, :] = jnp.zeros((PAD, qkv_ref.shape[1]), low)
+    unsent = own_rows + REACH - group * (own_rows + REACH)
+    for first in (0, qkv_ref.shape[0] - PAD):
+        qkv_ref[first : first + PAD, :] = jnp.zeros((PAD, qkv_ref.shape[1]), low)
+    qkv_ref[pl.ds(pl.multiple_of(PAD + unsent, 32), HALO - REACH), :] = jnp.zeros(
+        (HALO - REACH, qkv_ref.shape[1]), low
+    )
+    dout_ref[pl.ds(pl.multiple_of(unsent, 32), HALO - REACH), :] = jnp.zeros(
+        (HALO - REACH, HEAD_DIM), low
+    )
     vecg_ref[...] = jnp.zeros_like(vecg_ref)
     gb1_ref[...] = jnp.zeros_like(gb1_ref)
 
@@ -630,10 +656,6 @@
         for copy in qkv_blocks:
             copy.wait()
         state["far_qkv"] = far(wqkv_ref.at[group], wqkv_ref.at[group], 3)
-        state["w1_blocks"] = exchange_blocks(
-            [(pack_w1, w1_all.at[group])],
-            (block_local.at[1:2], block_send.at[1:2], block_recv.at[1:2]), base, mine, others,
-        )
         yield
         for copy in near:
             copy.wait()
@@ -671,11 +693,6 @@
     gain_one, b2, shift_two = high_ref[1:2, :], high_ref[2:3, :], high_ref[3:4, :]
 
     state["far_qkv"].wait()
-    far_wo_to = (1 - group) * GROUP + 2 * chip + group
-    far_wo = push(
-        wo_ref, wo_all.at[group, core], far_send.at[4 + core], far_recv.at[4 + core], far_wo_to
-    )
-    far_wo.start()
     for chunk in range(CHUNKS):
         for side in range(2):
             here = pl.ds((chunk * 2 + side) * half_rows, half_rows)
@@ -685,13 +702,22 @@
                 qkv_ref[pl.ds(pl.multiple_of(ext + place, rows), rows), :] = total[
                     slot * rows : (slot + 1) * rows
                 ]
-    halo_src = pl.ds(pl.multiple_of(PAD + 1792 - group * 1536, 64), HALO)
-    halo_dst = pl.ds(pl.multiple_of(PAD + 2048 * group, 64), HALO)
-    far_halo = far(qkv_ref.at[halo_src, :], qkv_ref.at[halo_dst, :], 6)
-    for copy in state["w1_blocks"]:
-        copy.wait()
-    far_w1 = far(w1_all.at[group], w1_all.at[group], 7)
+    near_edge = own_rows - REACH - group * (own_rows - REACH - HALO)
+    far_edge = HALO - REACH + group * (own_rows - HALO + REACH)
+    halo_src = pl.ds(pl.multiple_of(PAD + near_edge, 32), REACH)
+    halo_dst = pl.ds(pl.multiple_of(PAD + far_edge, 32), REACH)
+    key_value = pl.ds(HEAD_DIM, 2 * HEAD_DIM)
+    far_halo = far(qkv_ref.at[halo_src, key_value], qkv_ref.at[halo_dst, key_value], 6)
+    far_wo_to = (1 - group) * GROUP + 2 * chip + group
+    far_wo = push(
+        wo_ref, wo_all.at[group, core], far_send.at[4 + core], far_recv.at[4 + core], far_wo_to
+    )
+    far_wo.start()
     far_w2.append(far(w2_ref.at[w2_last, :], w2_all.at[group, w2_last, :], 8))
+    w1_blocks = exchange_blocks(
+        [(pack_w1, w1_all.at[group])],
+        (block_local.at[1:2], block_send.at[1:2], block_recv.at[1:2]), base, mine, others,
+    )
 
     def attend_tile(at):
         tile = at + group * (GROUP - 1 - 2 * at)
@@ -713,6 +739,9 @@
 
     lax.fori_loop(0, own_rows // TILE // 2 - 1, attend_two, 0)
     far_halo.wait()
+    for copy in w1_blocks:
+        copy.wait()
+    far_w1 = far(w1_all.at[group], w1_all.at[group], 7)
     attend_tile(own_rows // TILE - 2)
     attend_tile(own_rows // TILE - 1)
     for chunk in range(CHUNKS):
@@ -931,15 +960,16 @@
         own.start()
         there.start()
 
-    def write_w1_own(at, slot, again):
-        own = emit(stage_w1.at[slot], gw1_own.at[columns_at(at), :], out_sems.at[2, slot], again)
-        stage_w1[slot] = product(dup_t, all_m, columns_at(group * 4 + at)).T
-        own.start()
-
-    def write_w1_far(at, slot, again):
-        there = emit(stage_w1_low.at[slot], gw1_far.at[columns_at(at), :], out_sems.at[3, slot], again)
-        stage_w1_low[slot] = product(dup_t, all_m, columns_at((1 - group) * 4 + at)).T.astype(low)
-        there.start()
+    def write_w1(first):
+        def write(at, slot, again):
+            tile = first + at
+            here = gw1_ref.at[pl.ds(pl.multiple_of(tile * 4, 4), 4)]
+            copy = emit(stage_w1.at[slot], here, out_sems.at[2, slot], again)
+            total = product(dup_t, all_m, columns_at(tile)).T.astype(low)
+            stage_w1[slot] = total.reshape(4, SPLIT // 4, units)
+            copy.start()
+
+        return write
 
     def write_wo(at, slot, again):
         own = emit(stage_ref.at[slot, 0:HEAD_DIM, :], gwo_ref.at[:, columns_at(at)], out_sems.at[4, slot], again)
@@ -962,25 +992,33 @@
         yield
         for copy in back:
             copy.wait()
-        run(0, width // SPLIT // 2, write_w1_far)
+        run(0, width // SPLIT // 2, write_w1((1 - group) * 4))
         for slot in range(2):
-            emit(stage_w1_low.at[slot], gw1_far.at[columns_at(0), :], out_sems.at[3, slot], True)
-        early_w1 = gw1_far.at[pl.ds(0, width // 4), :]
-        swaps.append(far(early_w1, gw1_in, 11))
-        yield
-        run(0, width // SPLIT // 2, write_w1_own)
+            emit(stage_w1.at[slot], gw1_ref.at[pl.ds(0, 4)], out_sems.at[2, slot], True)
+        first = pl.ds(pl.multiple_of((1 - group) * GROUP, GROUP), GROUP)
+        swaps.extend(
+            far_blocks(
+                gw1_ref.at[first, :, pl.ds(0, units // 2)], gw1_in,
+                there_send, there_recv, group, mine,
+            )
+        )
+        yield
+        run(0, width // SPLIT // 2, write_w1(group * 4))
         for slot in range(2):
-            emit(stage_w1.at[slot], gw1_own.at[columns_at(0), :], out_sems.at[2, slot], True)
+            emit(stage_w1.at[slot], gw1_ref.at[pl.ds(0, 4)], out_sems.at[2, slot], True)
 
     swaps = []
     step_through([flow(chunk) for chunk in range(CHUNKS)], fill())
-    halo_src = pl.ds(pl.multiple_of(1792 - group * 1536, 64), HALO)
-    halo_dst = pl.ds(pl.multiple_of(2048 * group, 64), HALO)
-    far_dout = far(dout_ref.at[halo_src, :], dout_ref.at[halo_dst, :], 9)
+    query = pl.ds(0, HEAD_DIM)
+    far_query = far(qkv_ref.at[halo_src, query], qkv_ref.at[halo_dst, query], 12)
+    dout_src = pl.ds(pl.multiple_of(near_edge, 32), REACH)
+    dout_dst = pl.ds(pl.multiple_of(far_edge, 32), REACH)
+    far_dout = far(dout_ref.at[dout_src, :], dout_ref.at[dout_dst, :], 9)
     run(0, width // SPLIT, write_wo)
     for slot in range(2):
         emit(stage_ref.at[slot, 0:HEAD_DIM, :], gwo_ref.at[:, columns_at(0)], out_sems.at[4, slot], True)
     far_dout.wait()
+    far_query.wait()
     for copy in swaps:
         copy.wait()
 
@@ -1013,9 +1051,8 @@
             shape((unit_rows, width), f32),
             shape((unit_rows, width), bf16),
             shape((unit_rows, width), bf16),
-            shape((width // 2, units), f32),
-            shape((width // 2, units), bf16),
-            shape((width // 4, units), bf16),
+            shape((2 * GROUP, weight_rows, units), bf16),
+            shape((GROUP, weight_rows, unit_rows), bf16),
             shape((HEAD_DIM, width), f32),
             shape((CHUNKS, 2, 2, 2, 2, rows, width), bf16),
             shape((CHUNKS, 2, 2, 2, 2, rows, width), bf16),
@@ -1024,7 +1061,7 @@
             shape((2, GROUP, weight_rows, 3 * HEAD_DIM), bf16),
         ],
         in_specs=[vmem, vmem, anywhere, anywhere, anywhere, anywhere, vmem, vmem, vmem],
-        out_specs=[vmem] * 4 + [anywhere] * 9 + [vmem] * 3,
+        out_specs=[vmem] * 4 + [anywhere] * 8 + [vmem] * 3,
         scratch_shapes=[
             slots(CHUNKS, 2, 2, 2, 2), slots(CHUNKS, 2, 2, 2, 2),
             slots(CHUNKS, 2, 2, 2), slots(2, 2, 2, 2), slots(CHUNKS, 2, 2, 2),
@@ -1049,12 +1086,12 @@
             pltpu.VMEM((8, units), f32),
             pltpu.VMEM((2, SPLIT, SPLIT), f32),
             pltpu.VMEM((2, SPLIT, SPLIT), bf16),
-            pltpu.VMEM((2, SPLIT, units), f32),
-            pltpu.VMEM((2, SPLIT, units), bf16),
+            pltpu.VMEM((2, 4, SPLIT // 4, units), bf16),
             sems((STAGES, CHUNKS, 4, 3)), sems((STAGES, CHUNKS, 4, 3)),
             sems((STAGES, CHUNKS)), sems((STAGES, CHUNKS)),
-            sems((2,)), sems((2, peers)), sems((2, peers)), sems((peers,)), sems((peers,)),
-            sems((12,)), sems((12,)), sems((3,)), sems((5, 2)), sems((3, CHUNKS)),
+            sems((2,)), sems((2, peers)), sems((2, peers)), sems((GROUP,)), sems((GROUP,)),
+            sems((peers,)), sems((peers,)),
+            sems((13,)), sems((13,)), sems((3,)), sems((5, 2)), sems((3, CHUNKS)),
         ],
         compiler_params=pltpu.CompilerParams(
             collective_id=4, has_side_effects=True, vmem_limit_bytes=63 << 20
@@ -1065,25 +1102,24 @@
 
 def tail_kernel(
     qkv_ref, dout_ref, seg_q_ref, seg_k_ref, wqkv_ref, dres_ref, gwo_ref, parts_ref,
-    x_all, w1_own, w1_far, w1_early, w2_own, w2_early,
+    x_all, gw1_ref, w1_early, w2_own, w2_early,
     input_ref, out_q, out_k, out_v, out_wo, out_w1, out_w2, vec_ref,
     xs_ref, own_part, far_part, pair_in, in_one, in_two, in_three, res_ref,
-    dqkv_ref, dk_sum, dv_sum, dqkv_t, gq_own, gq_far, gq_in, gq_send, gq_recv,
-    w1_sum, w1_in, w1_send, w1_recv, w2_sum, w2_in, wo_low, wo_in, wo_pair, wo_pair_in,
+    dqkv_ref, dk_sum, dv_sum, dqkv_t, gq_own, gq_far, gq_here, gq_there,
+    w1_here, w1_there, w2_sum, w2_in, wo_low, wo_in, wo_pair, wo_pair_in,
     blocks_ref, arrived, theirs, far_vec_in,
     hop_send, hop_recv, pair_send, pair_recv, load_sems,
-    block_local, block_send, block_recv, far_send, far_recv,
+    block_local, block_send, block_recv, there_send, there_recv, far_send, far_recv,
 ):
     f32, low = jnp.float32, qkv_ref.dtype
     block, width = dres_ref.shape
-    rows = block // CHUNKS
-    half_rows = rows * GROUP // 2
+    rows = block // TAIL_CHUNKS
     weight_rows = out_q.shape[0]
     scale = HEAD_DIM ** (-0.5)
-    group, base, mine, others, across = group_places()
+    group, base, mine, others, across, there = group_places()
     net = Traffic((hop_send, hop_recv, pair_send, pair_recv), TAIL_PLANS)
     core, chip = net.core, mine // 2
-    enter(others + [across, flip(across, 0)])
+    enter(others + there)
 
     def far(src, dst, at, device=across):
         copy = push(src, dst, far_send.at[at], far_recv.at[at], device)
@@ -1104,15 +1140,25 @@
         wo_low[...] = gwo_ref[...].astype(low)
         far_wo.start()
 
-    half = w1_far.shape[0] // 2
-    late = pl.ds(half, half)
-    far_w1 = far(w1_far.at[late, :], w1_in.at[late, :], 1)
+    def blocks(pairs, at):
+        here = slice(at, at + len(pairs))
+        return exchange_blocks(
+            pairs, (block_local.at[here], block_send.at[here], block_recv.at[here]),
+            base, mine, others,
+        )
+
+    unit_rows = w1_early.shape[-1]
+    early, late = pl.ds(0, unit_rows), pl.ds(unit_rows, unit_rows)
+    first = pl.ds(pl.multiple_of((1 - group) * GROUP, GROUP), GROUP)
+    w1_far = far_blocks(
+        gw1_ref.at[first, :, late], w1_there.at[:, :, late],
+        there_send.at[0], there_recv.at[0], group, mine,
+    )
     x_loads = [load(x_all.at[at], xs_ref.at[at], at) for at in range(CHUNKS)]
     loads = [
-        load(w1_own, w1_sum, CHUNKS),
-        load(w1_early, w1_in.at[pl.ds(0, half), :], CHUNKS + 1),
-        load(w2_own, w2_sum, CHUNKS + 2),
-        load(w2_early, w2_in, CHUNKS + 3),
+        load(w1_early, w1_there.at[:, :, early], CHUNKS),
+        load(w2_own, w2_sum, CHUNKS + 1),
+        load(w2_early, w2_in, CHUNKS + 2),
     ]
     blocks_ref[...] = parts_ref[...]
     dk_sum[...] = jnp.zeros_like(dk_sum)
@@ -1148,29 +1194,22 @@
     dqkv_ref[:, HEAD_DIM : 2 * HEAD_DIM] = (dk_sum[inside, :] * scale).astype(low)
     dqkv_ref[:, 2 * HEAD_DIM : 3 * HEAD_DIM] = dv_sum[inside, :].astype(low)
 
-    def rows_of(chunk, side):
+    def rows_of(chunk, side, rows):
+        places = [
+            group * HALO + (slot * 2 + side) * block + chunk * rows for slot in range(GROUP // 2)
+        ]
         return jnp.concatenate(
-            [
-                dqkv_ref[
-                    pl.ds(
-                        pl.multiple_of(
-                            group * HALO + (slot * 2 + side) * block + chunk * rows, rows
-                        ),
-                        rows,
-                    ),
-                    :,
-                ]
-                for slot in range(GROUP // 2)
-            ],
-            0,
+            [dqkv_ref[pl.ds(pl.multiple_of(place, rows), rows), :] for place in places], 0
         )
 
+    x_rows = block // CHUNKS
+    x_half = x_rows * GROUP // 2
     bias = jnp.zeros((1, 3 * HEAD_DIM), f32)
     for chunk in range(CHUNKS):
         for side in range(2):
-            part = rows_of(chunk, side).astype(f32)
+            part = rows_of(chunk, side, x_rows).astype(f32)
             bias = bias + jnp.sum(part, 0, keepdims=True)
-            here = slice((chunk * 2 + side) * half_rows, (chunk * 2 + side + 1) * half_rows)
+            here = slice((chunk * 2 + side) * x_half, (chunk * 2 + side + 1) * x_half)
             dqkv_t[:, here] = part.T.astype(low)
 
     for copy in x_loads:
@@ -1181,26 +1220,24 @@
         total = None
         for chunk in range(CHUNKS):
             for side in range(2):
-                here = slice((chunk * 2 + side) * half_rows, (chunk * 2 + side + 1) * half_rows)
-                right = xs_ref[chunk, side, :, :, :, :, columns].reshape(half_rows, SPLIT)
+                here = slice((chunk * 2 + side) * x_half, (chunk * 2 + side + 1) * x_half)
+                right = xs_ref[chunk, side, :, :, :, :, columns].reshape(x_half, SPLIT)
                 term = jnp.dot(dqkv_t[:, here], right, preferred_element_type=f32)
                 total = term if total is None else total + term
         return total.T
 
     quarter = width // SPLIT // 2
 
-    def far_tile(at, carry):
-        here = pl.ds(pl.multiple_of(at * SPLIT, SPLIT), SPLIT)
-        gq_far[here, :] = product((1 - group) * quarter + at).astype(low)
-        return carry
-
-    def own_tile(at, carry):
-        here = pl.ds(pl.multiple_of(at * SPLIT, SPLIT), SPLIT)
-        gq_own[here, :] = product(group * quarter + at)
-        return carry
-
-    lax.fori_loop(0, quarter, far_tile, 0)
-    far_qkv = far(gq_far, gq_in, 2)
+    def tile_of(ref, first):
+        def body(at, carry):
+            total = product(first + at).astype(low)
+            ref[pl.ds(pl.multiple_of(at * 4, 4), 4)] = total.reshape(4, SPLIT // 4, 3 * HEAD_DIM)
+            return carry
+
+        lax.fori_loop(0, quarter, body, 0)
+
+    tile_of(gq_far, (1 - group) * quarter)
+    qkv_far = far_blocks(gq_far, gq_there, there_send.at[1], there_recv.at[1], group, mine)
 
     bias_q, bias_v = bias[:, 0:HEAD_DIM], bias[:, 2 * HEAD_DIM : 3 * HEAD_DIM]
     lane = lax.broadcasted_iota(jnp.int32, (1, 128), 1)
@@ -1211,17 +1248,10 @@
         lane < 64, pltpu.roll(bias_q, 64, 1), bias_v
     )
 
-    def blocks(pairs, at):
-        here = slice(at, at + len(pairs))
-        return exchange_blocks(
-            pairs, (block_local.at[here], block_send.at[here], block_recv.at[here]),
-            base, mine, others,
-        )
-
     vec_blocks = blocks([(blocks_ref, arrived)], 0)
 
     def input_part(chunk, side, dst):
-        left = rows_of(chunk, side)
+        left = rows_of(chunk, side, rows)
 
         def body(at, carry):
             weight = wqkv_ref[at // 4, pl.ds(at % 4 * 4, 4)].reshape(SPLIT, 3 * HEAD_DIM)
@@ -1255,7 +1285,8 @@
             copy.wait()
         out_w2[...] = w2_sum[...] + w2_in[...].astype(f32)
         yield
-        lax.fori_loop(0, quarter, own_tile, 0)
+        tile_of(gq_own, group * quarter)
+        state["qkv"] = blocks([(gq_own, gq_here)], 2)
         yield
         for copy in vec_blocks:
             copy.wait()
@@ -1268,7 +1299,7 @@
         state["vec"] = far(theirs, far_vec_in, 3)
 
     state = {}
-    step_through([flow(chunk) for chunk in range(CHUNKS)], fill())
+    step_through([flow(chunk) for chunk in range(TAIL_CHUNKS)], fill())
 
     share_wo = push(wo_pair, wo_pair_in, far_send.at[4], far_recv.at[4], net.pair)
 
@@ -1281,15 +1312,8 @@
         wo_pair[...] = jnp.where(core == 0, second, first)
         share_wo.start()
 
-    far_w1.wait()
-
-    def add_w1(at, carry):
-        here = pl.ds(pl.multiple_of(at * weight_rows, weight_rows), weight_rows)
-        w1_send[at] = (w1_sum[here, :] + w1_in[here, :].astype(f32)).astype(low)
-        return carry
-
-    lax.fori_loop(0, GROUP, add_w1, 0)
-    w1_blocks = blocks([(w1_send, w1_recv)], 1)
+    own_first = pl.ds(pl.multiple_of(group * GROUP, GROUP), GROUP)
+    w1_blocks = blocks([(gw1_ref.at[own_first], w1_here)], 1)
     state["vec"].wait()
     vec_ref[...] += far_vec_in[...]
 
@@ -1303,45 +1327,36 @@
     def _():
         share_wo.wait_send()
 
-    far_qkv.wait()
-
-    def add_qkv(at, carry):
-        here = pl.ds(pl.multiple_of(at * weight_rows, weight_rows), weight_rows)
-        gq_send[at] = (gq_own[here, :] + gq_in[here, :].astype(f32)).astype(low)
-        return carry
-
-    lax.fori_loop(0, GROUP, add_qkv, 0)
-    qkv_blocks = blocks([(gq_send, gq_recv)], 2)
-    for copy in w1_blocks:
+    for copy in w1_blocks + w1_far:
         copy.wait()
-    unit_rows = w1_recv.shape[-1] // 2
     for at in range(GROUP):
         for part in range(2):
-            first = (part * GROUP + at) * unit_rows
-            out_w1[:, first : first + unit_rows] = w1_recv[
-                at, :, part * unit_rows : (part + 1) * unit_rows
+            here = slice(part * unit_rows, (part + 1) * unit_rows)
+            to = (part * GROUP + at) * unit_rows
+            out_w1[:, to : to + unit_rows] = w1_here[at, :, here].astype(f32) + w1_there[
+                at, :, here
             ].astype(f32)
-    for copy in qkv_blocks:
+    for copy in state["qkv"] + qkv_far:
         copy.wait()
     for at in range(GROUP):
-        first = (at % 2 * 8 + at // 2) * HEAD_DIM
+        to = (at % 2 * 8 + at // 2) * HEAD_DIM
         for part, ref in enumerate((out_q, out_k, out_v)):
-            ref[:, first : first + HEAD_DIM] = gq_recv[
-                at, :, part * HEAD_DIM : (part + 1) * HEAD_DIM
+            here = slice(part * HEAD_DIM, (part + 1) * HEAD_DIM)
+            ref[:, to : to + HEAD_DIM] = gq_here[at, :, here].astype(f32) + gq_there[
+                at, :, here
             ].astype(f32)
 
 
 def layer_tail(
-    qkv, dout, seg_q, seg_k, wqkv, dres, gwo, parts, x_all, w1_own, w1_far, w1_early, w2_own, w2_early
+    qkv, dout, seg_q, seg_k, wqkv, dres, gwo, parts, x_all, gw1, w1_early, w2_own, w2_early
 ):
     f32, bf16 = jnp.float32, jnp.bfloat16
     block, width = dres.shape
-    rows = block // CHUNKS
+    rows = block // TAIL_CHUNKS
     weight_rows = wqkv.shape[2]
-    units = w1_own.shape[1]
+    units = gw1.shape[2]
     unit_rows = units // 2
     own_rows = GROUP * block
-    half_width = width // 2
     peers = GROUP - 1
     vmem = pl.BlockSpec(memory_space=pltpu.VMEM)
     anywhere = pl.BlockSpec(memory_space=pl.ANY)
@@ -1364,24 +1379,21 @@
             shape((unit_rows, width), f32),
             shape((8, 128), f32),
         ],
-        in_specs=[vmem] * 8 + [anywhere] * 6,
+        in_specs=[vmem] * 8 + [anywhere] * 5,
         out_specs=[vmem] * 8,
         scratch_shapes=[
-            slots(CHUNKS, 2, 2, 2, 2),
-            slots(CHUNKS, 2, 2, 2), slots(2, 2, 2, 2), slots(CHUNKS, 2, 2, 2),
-            slots(CHUNKS, 2, 2), slots(CHUNKS, 2), slots(CHUNKS),
+            scratch(x_all.shape, bf16),
+            slots(TAIL_CHUNKS, 2, 2, 2), slots(2, 2, 2, 2), slots(TAIL_CHUNKS, 2, 2, 2),
+            slots(TAIL_CHUNKS, 2, 2), slots(TAIL_CHUNKS, 2), slots(TAIL_CHUNKS),
             scratch((block, width), f32),
             scratch((own_rows + HALO, heads), bf16),
             scratch(qkv.shape[:1] + (HEAD_DIM,), f32),
             scratch(qkv.shape[:1] + (HEAD_DIM,), f32),
             scratch((heads, own_rows), bf16),
-            scratch((half_width, heads), f32),
-            scratch((half_width, heads), bf16),
-            scratch((half_width, heads), bf16),
             scratch((GROUP, weight_rows, heads), bf16),
             scratch((GROUP, weight_rows, heads), bf16),
-            scratch((half_width, units), f32),
-            scratch((half_width, units), bf16),
+            scratch((GROUP, weight_rows, heads), bf16),
+            scratch((GROUP, weight_rows, heads), bf16),
             scratch((GROUP, weight_rows, units), bf16),
             scratch((GROUP, weight_rows, units), bf16),
             scratch((unit_rows, width), f32),
@@ -1394,14 +1406,16 @@
             scratch(parts.shape, f32),
             scratch((8, 128), f32),
             scratch((8, 128), f32),
-            sems((1, CHUNKS, 4, 3)), sems((1, CHUNKS, 4, 3)), sems((1, CHUNKS)), sems((1, CHUNKS)),
-            sems((CHUNKS + 4,)), sems((3,)), sems((3, peers)), sems((3, peers)), sems((5,)), sems((5,)),
+            sems((1, TAIL_CHUNKS, 4, 3)), sems((1, TAIL_CHUNKS, 4, 3)),
+            sems((1, TAIL_CHUNKS)), sems((1, TAIL_CHUNKS)),
+            sems((CHUNKS + 3,)), sems((3,)), sems((3, peers)), sems((3, peers)),
+            sems((2, GROUP)), sems((2, GROUP)), sems((5,)), sems((5,)),
         ],
         compiler_params=pltpu.CompilerParams(
             collective_id=5, has_side_effects=True, vmem_limit_bytes=63 << 20
         ),
         name="layer_tail",
-    )(qkv, dout, seg_q, seg_k, wqkv, dres, gwo, parts, x_all, w1_own, w1_far, w1_early, w2_own, w2_early)
+    )(qkv, dout, seg_q, seg_k, wqkv, dres, gwo, parts, x_all, gw1, w1_early, w2_own, w2_early)
 
 
 def grouped_device(
@@ -1465,8 +1479,8 @@
     seg_q = seg[:, None]
 
     (
-        output, grad_resid_one, vec_grads, grad_b1, w2_own, _, w2_early, w1_own, w1_far, w1_early,
-        grad_wo, all_tokens, _, qkv, grad_out, full_qkv,
+        output, grad_resid_one, vec_grads, grad_b1, w2_own, _, w2_early, grad_w1, w1_early, grad_wo,
+        all_tokens, _, qkv, grad_out, full_qkv,
     ) = layer(tokens, cotangent, pack_qkv, pack_w1, w2, wo, vector, seg_q, seg_k)
 
     spread_b1 = lax.dynamic_update_slice_in_dim(
@@ -1485,7 +1499,7 @@
     parts = parts.transpose(1, 0, 2).reshape(GROUP, 16, 128)
     input_grad, out_q, out_k, out_v, out_wo, out_w1, out_w2, sums = layer_tail(
         qkv, grad_out, seg_q, seg_k, full_qkv, grad_resid_one, grad_wo, parts,
-        all_tokens, w1_own, w1_far, w1_early, w2_own, w2_early,
+        all_tokens, grad_w1, w1_early, w2_own, w2_early,
     )
     sums, at = sums.reshape(-1), 0
     small = []

time: 575 us -> 545 us (0.948)
  Pallas kernels: 539 us -> 508 us
    pallas_call x1, Pallas kernels: 417 us -> 400 us  [layer(): pl.pallas_call(layer_kernel, out_shape=[shape((block, width), bf16), shap...]
    pallas_call x1, Pallas kernels: 122 us -> 108 us  [layer_tail(): pl.pallas_call(tail_kernel, out_shape=[shape((block, width), bf16), shape...]
where the time goes in v6:
time: 545 us; the launch traced here: 536 us
  Pallas kernels  508 us (93%)
  local copies, waits for them, and re-layouts  22.3 us (4%)
    pallas_call x1, Pallas kernels, layer(): pl.pallas_call(layer_kernel, out_shape=[shape((block, width), bf16), shap...  400 us
    pallas_call x1, Pallas kernels, layer_tail(): pl.pallas_call(tail_kernel, out_shape=[shape((block, width), bf16), shape...  108 us

profile of v6, /device:TPU:7, one launch (start us, length us, event | category | flops | bytes accessed | tf_op | source)
XLA Modules:
  0.0 535.7 jit_solution(9953015348083221906)
XLA Ops:
  0.7 0.0 copy-start.2
  0.7 0.1 add_add_fusion
  0.8 0.8 copy.63
  1.6 0.1 reduce-window.9
  1.6 0.1 reduce
  1.7 0.7 sub.13
  2.4 0.2 convert_reduce_fusion
  2.7 0.7 and_select_fusion.seg_k_ref
  3.4 0.1 convert_reduce_fusion.1
  3.5 1.9 broadcast_in_dim.20.seg_q_ref
  5.4 0.2 copy.75
  5.7 1.0 copy.77
  6.7 0.0 copy-start.8
  6.7 0.0 copy-start.9
  6.7 1.5 reshape.178.pack_w1
  8.2 0.1 copy.59
  8.3 0.0 copy-done.9
  8.4 0.0 copy-start.11
  8.4 0.0 copy-start.12
  8.4 0.0 copy-start.13
  8.4 0.0 copy-start.14
  8.4 0.0 copy-start.15
  8.4 0.0 copy-start.16
  8.4 0.0 copy-start.17
  8.4 0.0 copy-start.18
  8.5 0.0 copy-start.19
  8.5 0.1 copy.60
  8.5 0.6 copy-done.10
  9.2 0.1 copy.61
  9.3 1.0 pad_maximum_fusion.pack_qkv
  10.3 0.0 copy-done.11
  10.3 0.0 copy-done.15
  10.3 0.0 copy-done.16
  10.3 0.0 copy-done.17
  10.3 0.0 copy-done.18
  10.3 0.0 copy-done.19
  10.3 0.1 concatenate.13
  10.4 0.6 bitcast_convert_fusion.vec_ref
  11.0 400.1 %layer.1 = (bf16[128,2048]{1,0:T(8,128)(2,1)}, f32[128,2048]{1,0:T(8,128)}, f32[8,2048]{1,0:T(8,128)}, f32[8,512]{1,0:T(8,128)}, f32[256,2048]{1,0:T(8,128)}, /*...) custom-call(bf16[128,2048]{1,0:T(8,128)(2,1)} %tok_ref.1, ...), custom_call_target="tpu_custom_call" | custom-call | tf_op jit(solution)/shard_map/layer/pallas_call | solution.py:1044
  411.1 0.7 slice_reduce_fusion.6
  411.9 1.2 slice_reduce_fusion
  413.1 0.1 reshape_squeeze.21
  413.2 0.1 reshape_squeeze.22
  413.3 0.1 reshape_squeeze.23
  413.4 0.1 reshape_squeeze.24
  413.5 0.1 reshape_squeeze.25
  413.6 0.1 reshape_squeeze.26
  413.7 0.2 concatenate.15
  413.9 0.8 reshape.183.parts_ref
  414.6 108.2 %layer_tail.1 = (bf16[128,2048]{1,0:T(8,128)(2,1)}, f32[64,2048]{1,0:T(8,128)}, f32[64,2048]{1,0:T(8,128)}, f32[64,2048]{1,0:T(8,128)}, f32[64,2048]{1,0:T(8,128...) custom-call(bf16[2688,384]{1,0:T(8,128)(2,1)} %get-tuple-element.39.qkv_ref, ...), custom_call_target="tpu_custom_call" | custom-call | tf_op jit(solution)/shard_map/layer_tail/pallas_call | solution.py:1370
  522.8 1.6 fusion
  524.4 1.2 slice_bitcast_fusion
  525.6 0.8 copy.87
  526.4 1.9 copy.88
  528.4 0.0 copy-done.7
  528.4 0.8 copy.89
  529.2 0.0 copy-done.6
  529.2 0.8 copy.90
  530.0 0.8 copy.91
  530.8 0.0 copy-done.4
  530.8 0.8 copy.92
  531.6 1.3 copy.93
  532.9 1.0 copy-done
  533.9 1.3 copy.94
  (32 shorter events, 0.3 us)
Async XLA Ops:
  0.7 4.7 copy-start.2
  6.7 1.5 copy-start.8
  6.7 1.6 copy-start.9
  8.2 0.9 copy-start.10
  8.4 1.9 copy-start.11
  8.4 1.9 copy-start.12
  8.4 1.9 copy-start.13
  8.4 1.9 copy-start.14
  8.4 1.9 copy-start.15
  8.4 1.9 copy-start.16
  8.4 1.9 copy-start.17
  8.4 1.9 copy-start.18
  8.5 1.9 copy-start.19
  414.6 111.0 %copy-start.3 = (bf16[128,2048]{1,0:T(8,128)(2,1)S(1)}, bf16[128,2048]{1,0:T(8,128)(2,1)}, u32[]{:S(2)}) copy-start(bf16[128,2048]{1,0:T(8,128)(2,1)} %get-tuple-element.90) | copy-start | bytes 1572868
  522.8 5.6 %copy-start.7 = (f32[64,2048]{1,0:T(8,128)S(1)}, f32[64,2048]{1,0:T(8,128)}, u32[]{:S(2)}) copy-start(f32[64,2048]{1,0:T(8,128)} %get-tuple-element.92) | copy-start | bytes 1572868
  525.6 3.5 copy-start.6
  526.4 3.5 copy-start.5
  528.4 2.4 copy-start.4
  529.2 2.4 copy-start.1
  531.6 2.3 copy-start

commit v7 on v6

--- a/solution.py
+++ b/solution.py
@@ -370,6 +370,18 @@
     return copies
 
 
+def exchange_columns(source, to, sems, base, mine, others):
+    local_sem, send_sem, recv_sem = sems
+    copies = []
+    for step, other in enumerate(others):
+        copy = push(source(other - base), to, send_sem.at[step], recv_sem.at[step], other)
+        copy.start()
+        copies.append(copy)
+    copy = pltpu.make_async_copy(source(mine), to, local_sem)
+    copy.start()
+    return copies + [copy]
+
+
 def far_blocks(src, dst, send_sem, recv_sem, group, mine):
     copies = []
     for step in range(GROUP):
@@ -396,14 +408,37 @@
     return device // GROUP, base, mine, others, across, there
 
 
-def tile_probs(qkv_ref, row, start, seg_q, seg_k):
+def write_segments(lengths_ref, first, keys_ref, queries_ref):
     f32 = jnp.float32
+    rows = queries_ref.shape[1]
+
+    def numbers(ref, ahead):
+        ids = first - ahead + lax.broadcasted_iota(jnp.int32, ref.shape, 1)
+        total = jnp.zeros(ref.shape, jnp.int32)
+        start = jnp.int32(0)
+        for at in range(lengths_ref.shape[0]):
+            total = total + (ids >= start).astype(jnp.int32)
+            start = start + lengths_ref[at]
+        return total.astype(f32)
+
+    queries_ref[...] = numbers(queries_ref, 0)
+    place = lax.broadcasted_iota(jnp.int32, keys_ref.shape, 1)
+    inside = (place >= PAD) & (place < PAD + rows)
+    keys_ref[...] = jnp.where(inside, numbers(keys_ref, PAD), -1.0)
+
+
+def tile_probs(qkv_ref, queries_ref, keys_ref, tile):
+    f32 = jnp.float32
+    place = pl.multiple_of(tile * TILE, TILE)
+    row = pl.multiple_of(PAD + place, 64)
+    window = pl.ds(place, WINDOW)
     queries = qkv_ref[pl.ds(row, TILE), 0:HEAD_DIM]
-    keys = qkv_ref[pl.ds(start, WINDOW), HEAD_DIM : 2 * HEAD_DIM]
-    scores = lax.dot_general(queries, keys, (((1,), (1,)), ((), ())), preferred_element_type=f32)
-    scores = jnp.where(seg_q == seg_k, scores * HEAD_DIM ** (-0.5), -1e30)
+    keys = qkv_ref[window, HEAD_DIM : 2 * HEAD_DIM]
+    scores = lax.dot_general(queries, keys, NT, preferred_element_type=f32)
+    own = jnp.broadcast_to(queries_ref[0:1, pl.ds(place, TILE)], (TILE, TILE)).T[:, 0:1]
+    scores = jnp.where(own == keys_ref[0:1, window], scores * HEAD_DIM ** (-0.5), -1e30)
     weights = jnp.exp(scores - jnp.max(scores, -1, keepdims=True))
-    return queries, keys, weights / jnp.sum(weights, -1, keepdims=True)
+    return queries, keys, weights * (1.0 / jnp.sum(weights, -1, keepdims=True))
 
 
 CHUNKS = 4
@@ -503,16 +538,24 @@
                     for place, dim in enumerate(free):
                         slot[dim] = (mask >> place) & 1
                     where = (slot[2], slot[1], slot[0])
-                    for row in range(0, rows, 16):
-                        at = (slice(row, row + 16), columns)
+                    lefts = [
+                        tuple(slot[dim] for dim in (2, 1, 0) if dim not in order[: back + 1])
+                        for back in range(step)
+                    ]
+
+                    def add(index, carry, step=step, where=where, lefts=lefts, columns=columns):
+                        row = pl.multiple_of(index * 16, 16)
+                        at = (pl.ds(row, 16), columns)
                         total = own[where + at].astype(f32) + pair_in[where + at].astype(f32)
                         for back in range(step):
-                            left = [slot[dim] for dim in (2, 1, 0) if dim not in order[: back + 1]]
-                            total = total + incoming[back][tuple(left) + at].astype(f32)
+                            total = total + incoming[back][lefts[back] + at].astype(f32)
                         if step < 3:
                             own[where + at] = total.astype(own.dtype)
                         else:
-                            finish(row, first, count, total)
+                            finish(row, columns, total)
+                        return carry
+
+                    lax.fori_loop(0, rows // 16, add, 0)
                 if step == 3:
                     continue
                 for dim in free:
@@ -542,14 +585,15 @@
 
 
 def layer_kernel(
-    tok_ref, cot_ref, pack_qkv, pack_w1, w2_ref, wo_ref, vec_ref, seg_q_ref, seg_k_ref,
-    out_ref, dres_ref, vecg_ref, gb1_ref, gw2_own, gw2_far, gw2_in, gw1_ref, gw1_in, gwo_ref,
+    tok_ref, cot_ref, wq_ref, wk_ref, wv_ref, w1_ref, w2_ref, wo_ref, vec_ref, lengths_ref,
+    out_ref, dres_ref, vecg_ref, gb1_ref, gw2_own, gw2_far, gw2_in, gw1_ref, gwo_ref,
     x_all, h_all, qkv_ref, dout_ref, wqkv_ref,
     all_h, all_m, own_part, far_part, pair_in, in_one, in_two, in_three,
     up_ref, act_ref, act_t, dup_ref, dup_t, att_ref, att_t, res_ref, hid_ref, norm_ref, scale_ref,
     w1_all, w2_all, wo_all, vec_all, low_ref, high_ref, b1_ref, stage_ref, stage_low, stage_w1,
+    queries_ref, keys_ref,
     hop_send, hop_recv, pair_send, pair_recv,
-    block_local, block_send, block_recv, there_send, there_recv, vec_send, vec_recv, far_send, far_recv,
+    block_local, block_send, block_recv, vec_send, vec_recv, far_send, far_recv,
     local_sems, out_sems, spill_sems,
 ):
     f32, low = jnp.float32, tok_ref.dtype
@@ -577,7 +621,7 @@
         copy.start()
         return copy
 
-    early = w2_ref.shape[0] // 2
+    early = w2_ref.shape[0] // 4 * 3
     far_vec = far(vec_ref, vec_all.at[group, mine], 0)
     near = [
         local(vec_ref, vec_all.at[group, mine], 0),
@@ -586,10 +630,21 @@
     ]
     w2_first, w2_last = pl.ds(0, early), pl.ds(early, w2_ref.shape[0] - early)
     far_w2 = [far(w2_ref.at[w2_first, :], w2_all.at[group, w2_first, :], 1)]
-    qkv_blocks = exchange_blocks(
-        [(pack_qkv, wqkv_ref.at[group])],
-        (block_local.at[0:1], block_send.at[0:1], block_recv.at[0:1]), base, mine, others,
-    )
+
+    def block_sems(at):
+        return block_local.at[at], block_send.at[at], block_recv.at[at]
+
+    qkv_blocks = []
+    for part, ref in enumerate((wq_ref, wk_ref, wv_ref)):
+
+        def head_columns(member, ref=ref):
+            first = pl.multiple_of((member % 2 * 8 + member // 2) * HEAD_DIM, HEAD_DIM)
+            return ref.at[:, pl.ds(first, HEAD_DIM)]
+
+        qkv_blocks += exchange_columns(
+            head_columns, wqkv_ref.at[group, mine, :, pl.ds(part * HEAD_DIM, HEAD_DIM)],
+            block_sems(part), base, mine, others,
+        )
     for chunk in range(CHUNKS):
         all_m[(chunk,) + own_slot] = tok_ref[chunk * rows : (chunk + 1) * rows, :]
     wo_near = push(
@@ -608,6 +663,8 @@
     )
     vecg_ref[...] = jnp.zeros_like(vecg_ref)
     gb1_ref[...] = jnp.zeros_like(gb1_ref)
+
+    write_segments(lengths_ref, group * (own_rows - HALO), keys_ref, queries_ref)
 
     def row_at(chunk, side):
         return pl.multiple_of((chunk * 2 + side) * half_rows, half_rows)
@@ -714,21 +771,24 @@
     )
     far_wo.start()
     far_w2.append(far(w2_ref.at[w2_last, :], w2_all.at[group, w2_last, :], 8))
-    w1_blocks = exchange_blocks(
-        [(pack_w1, w1_all.at[group])],
-        (block_local.at[1:2], block_send.at[1:2], block_recv.at[1:2]), base, mine, others,
-    )
+    w1_blocks = []
+    for part in range(2):
+
+        def w1_columns(member, part=part):
+            first = pl.multiple_of((part * GROUP + member) * SPLIT, SPLIT)
+            return w1_ref.at[:, pl.ds(first, SPLIT)]
+
+        w1_blocks += exchange_columns(
+            w1_columns, w1_all.at[group, mine, :, pl.ds(part * SPLIT, SPLIT)],
+            block_sems(3 + part), base, mine, others,
+        )
 
     def attend_tile(at):
         tile = at + group * (GROUP - 1 - 2 * at)
-        row = pl.multiple_of(ext + tile * TILE, 64)
-        start = pl.multiple_of(ext - PAD + tile * TILE, 64)
-        place = pl.multiple_of(group * HALO + tile * TILE, TILE)
-        _, _, probs = tile_probs(
-            qkv_ref, row, start, seg_q_ref[pl.ds(place, TILE), :],
-            seg_k_ref[group * (HALO // TILE) + tile],
-        )
-        values = qkv_ref[pl.ds(start, WINDOW), 2 * HEAD_DIM : 3 * HEAD_DIM]
+        inner = group * (HALO // TILE) + tile
+        _, _, probs = tile_probs(qkv_ref, queries_ref, keys_ref, inner)
+        window = pl.ds(pl.multiple_of(inner * TILE, TILE), WINDOW)
+        values = qkv_ref[window, 2 * HEAD_DIM : 3 * HEAD_DIM]
         out = jnp.dot(probs.astype(low), values, preferred_element_type=f32)
         att_ref[pl.ds(pl.multiple_of(tile * TILE, TILE), TILE), :] = out.astype(low)
 
@@ -823,14 +883,18 @@
             ]
 
     def keep(chunk):
-        def finish(row, first, count, total):
-            res_ref[chunk * rows + row : chunk * rows + row + 16, first : first + count] = total
+        def finish(row, columns, total):
+            res_ref[pl.ds(pl.multiple_of(chunk * rows + row, 16), 16), columns] = total
 
         return finish
 
-    def row_sets(chunk):
-        for row in range(0, rows, 16):
-            yield slice(chunk * rows + row, chunk * rows + row + 16), slice(row, row + 16)
+    def row_sets(chunk, body):
+        def step(index, carry):
+            row = pl.multiple_of(index * 16, 16)
+            body(pl.ds(pl.multiple_of(chunk * rows + row, 16), 16), pl.ds(row, 16))
+            return carry
+
+        lax.fori_loop(0, rows // 16, step, 0)
 
     def normal(res):
         res = res - jnp.mean(res, -1, keepdims=True)
@@ -849,7 +913,7 @@
         return grad, grad_low
 
     def norm_one(chunk):
-        for at, place in row_sets(chunk):
+        def body(at, place):
             res, scale = normal(tok_ref[at, :].astype(f32) + res_ref[at, :] + bo)
             norm_ref[at, :] = res
             scale_ref[at, :] = jnp.broadcast_to(scale, (16, 128))
@@ -857,22 +921,28 @@
             hid_ref[at, :] = hidden
             all_h[(chunk,) + own_slot + (place, slice(None))] = hidden.astype(low)
 
+        row_sets(chunk, body)
+
     def norm_two(chunk):
-        for at, place in row_sets(chunk):
+        def body(at, place):
             res, scale = normal(hid_ref[at, :] + res_ref[at, :] + b2)
             out_ref[at, :] = (res * gain_two + shift_two).astype(low)
             grad, grad_low = normal_back(cot_ref[at, :].astype(f32), res, gain_two, scale, 0)
             dres_ref[at, :] = grad
             all_m[(chunk,) + own_slot + (place, slice(None))] = grad_low
 
+        row_sets(chunk, body)
+
     def norm_one_back(chunk):
-        for at, place in row_sets(chunk):
+        def body(at, place):
             grad, grad_low = normal_back(
                 dres_ref[at, :] + res_ref[at, :], norm_ref[at, :], gain_one,
                 scale_ref[at, 0:1], 3,
             )
             dres_ref[at, :] = grad
             all_h[(chunk,) + own_slot + (place, slice(None))] = grad_low
+
+        row_sets(chunk, body)
 
     def flow(chunk):
         incoming = (in_one.at[chunk], in_two.at[chunk], in_three.at[chunk])
@@ -995,13 +1065,6 @@
         run(0, width // SPLIT // 2, write_w1((1 - group) * 4))
         for slot in range(2):
             emit(stage_w1.at[slot], gw1_ref.at[pl.ds(0, 4)], out_sems.at[2, slot], True)
-        first = pl.ds(pl.multiple_of((1 - group) * GROUP, GROUP), GROUP)
-        swaps.extend(
-            far_blocks(
-                gw1_ref.at[first, :, pl.ds(0, units // 2)], gw1_in,
-                there_send, there_recv, group, mine,
-            )
-        )
         yield
         run(0, width // SPLIT // 2, write_w1(group * 4))
         for slot in range(2):
@@ -1023,7 +1086,7 @@
         copy.wait()
 
 
-def layer(tokens, cotangent, pack_qkv, pack_w1, w2, wo, vector, seg_q, seg_k):
+def layer(tokens, cotangent, wq, wk, wv, w1, w2, wo, vector, lengths):
     f32, bf16 = jnp.float32, jnp.bfloat16
     block, width = tokens.shape
     rows = block // CHUNKS
@@ -1035,6 +1098,7 @@
     peers = GROUP - 1
     vmem = pl.BlockSpec(memory_space=pltpu.VMEM)
     anywhere = pl.BlockSpec(memory_space=pl.ANY)
+    smem = pl.BlockSpec(memory_space=pltpu.SMEM)
     sems = pltpu.SemaphoreType.DMA
     shape = jax.ShapeDtypeStruct
 
@@ -1052,7 +1116,6 @@
             shape((unit_rows, width), bf16),
             shape((unit_rows, width), bf16),
             shape((2 * GROUP, weight_rows, units), bf16),
-            shape((GROUP, weight_rows, unit_rows), bf16),
             shape((HEAD_DIM, width), f32),
             shape((CHUNKS, 2, 2, 2, 2, rows, width), bf16),
             shape((CHUNKS, 2, 2, 2, 2, rows, width), bf16),
@@ -1060,8 +1123,8 @@
             shape((own_rows + HALO, HEAD_DIM), bf16),
             shape((2, GROUP, weight_rows, 3 * HEAD_DIM), bf16),
         ],
-        in_specs=[vmem, vmem, anywhere, anywhere, anywhere, anywhere, vmem, vmem, vmem],
-        out_specs=[vmem] * 4 + [anywhere] * 8 + [vmem] * 3,
+        in_specs=[vmem] * 2 + [anywhere] * 6 + [vmem, smem],
+        out_specs=[vmem] * 4 + [anywhere] * 7 + [vmem] * 3,
         scratch_shapes=[
             slots(CHUNKS, 2, 2, 2, 2), slots(CHUNKS, 2, 2, 2, 2),
             slots(CHUNKS, 2, 2, 2), slots(2, 2, 2, 2), slots(CHUNKS, 2, 2, 2),
@@ -1087,9 +1150,11 @@
             pltpu.VMEM((2, SPLIT, SPLIT), f32),
             pltpu.VMEM((2, SPLIT, SPLIT), bf16),
             pltpu.VMEM((2, 4, SPLIT // 4, units), bf16),
+            pltpu.VMEM((1, own_rows + HALO), f32),
+            pltpu.VMEM((1, own_rows + HALO + 2 * PAD), f32),
             sems((STAGES, CHUNKS, 4, 3)), sems((STAGES, CHUNKS, 4, 3)),
             sems((STAGES, CHUNKS)), sems((STAGES, CHUNKS)),
-            sems((2,)), sems((2, peers)), sems((2, peers)), sems((GROUP,)), sems((GROUP,)),
+            sems((5,)), sems((5, peers)), sems((5, peers)),
             sems((peers,)), sems((peers,)),
             sems((13,)), sems((13,)), sems((3,)), sems((5, 2)), sems((3, CHUNKS)),
         ],
@@ -1097,17 +1162,18 @@
             collective_id=4, has_side_effects=True, vmem_limit_bytes=63 << 20
         ),
         name="layer",
-    )(tokens, cotangent, pack_qkv, pack_w1, w2, wo, vector, seg_q, seg_k)
+    )(tokens, cotangent, wq, wk, wv, w1, w2, wo, vector, lengths)
 
 
 def tail_kernel(
-    qkv_ref, dout_ref, seg_q_ref, seg_k_ref, wqkv_ref, dres_ref, gwo_ref, parts_ref,
-    x_all, gw1_ref, w1_early, w2_own, w2_early,
+    qkv_ref, dout_ref, wqkv_ref, dres_ref, gwo_ref, vecg_ref, gb1_ref, lengths_ref,
+    x_all, gw1_ref, w2_own, w2_early,
     input_ref, out_q, out_k, out_v, out_wo, out_w1, out_w2, vec_ref,
     xs_ref, own_part, far_part, pair_in, in_one, in_two, in_three, res_ref,
     dqkv_ref, dk_sum, dv_sum, dqkv_t, gq_own, gq_far, gq_here, gq_there,
     w1_here, w1_there, w2_sum, w2_in, wo_low, wo_in, wo_pair, wo_pair_in,
     blocks_ref, arrived, theirs, far_vec_in,
+    queries_ref, keys_ref,
     hop_send, hop_recv, pair_send, pair_recv, load_sems,
     block_local, block_send, block_recv, there_send, there_recv, far_send, far_recv,
 ):
@@ -1147,30 +1213,24 @@
             base, mine, others,
         )
 
-    unit_rows = w1_early.shape[-1]
-    early, late = pl.ds(0, unit_rows), pl.ds(unit_rows, unit_rows)
     first = pl.ds(pl.multiple_of((1 - group) * GROUP, GROUP), GROUP)
     w1_far = far_blocks(
-        gw1_ref.at[first, :, late], w1_there.at[:, :, late],
-        there_send.at[0], there_recv.at[0], group, mine,
+        gw1_ref.at[first], w1_there, there_send.at[0], there_recv.at[0], group, mine
     )
     x_loads = [load(x_all.at[at], xs_ref.at[at], at) for at in range(CHUNKS)]
     loads = [
-        load(w1_early, w1_there.at[:, :, early], CHUNKS),
-        load(w2_own, w2_sum, CHUNKS + 1),
-        load(w2_early, w2_in, CHUNKS + 2),
+        load(w2_own, w2_sum, CHUNKS),
+        load(w2_early, w2_in, CHUNKS + 1),
     ]
-    blocks_ref[...] = parts_ref[...]
+    own_rows = GROUP * block
+    write_segments(lengths_ref, group * (own_rows - HALO), keys_ref, queries_ref)
     dk_sum[...] = jnp.zeros_like(dk_sum)
     dv_sum[...] = jnp.zeros_like(dv_sum)
 
     def attend_back_tile(tile):
         place = pl.multiple_of(tile * TILE, TILE)
-        row = pl.multiple_of(PAD + place, 64)
         window = pl.ds(place, WINDOW)
-        queries, keys, probs = tile_probs(
-            qkv_ref, row, place, seg_q_ref[pl.ds(place, TILE), :], seg_k_ref[tile]
-        )
+        queries, keys, probs = tile_probs(qkv_ref, queries_ref, keys_ref, tile)
         values = qkv_ref[window, 2 * HEAD_DIM : 3 * HEAD_DIM]
         grads = dout_ref[pl.ds(place, TILE), :]
         grad_probs = lax.dot_general(grads, values, NT, preferred_element_type=f32)
@@ -1239,14 +1299,31 @@
     tile_of(gq_far, (1 - group) * quarter)
     qkv_far = far_blocks(gq_far, gq_there, there_send.at[1], there_recv.at[1], group, mine)
 
+    blocks_ref[...] = jnp.zeros_like(blocks_ref)
+    lane = lax.broadcasted_iota(jnp.int32, (1, 128), 1)
+
+    def pieces_of(low_row, high_row):
+        return (
+            jnp.where(lane < 64, low_row, pltpu.roll(high_row, 64, 1)),
+            jnp.where(lane < 64, pltpu.roll(low_row, 64, 1), high_row),
+        )
+
+    for tile in range(GROUP):
+        here = slice(tile * 128, tile * 128 + 128)
+        for at, (low_row, high_row) in enumerate(((3, 4), (5, 0), (1, 2))):
+            to = tile // 8 * 8 + 1 + at
+            both = pieces_of(vecg_ref[low_row : low_row + 1, here], vecg_ref[high_row : high_row + 1, here])
+            for odd in range(2):
+                blocks_ref[tile % 8 * 2 + odd, to : to + 1, :] = both[odd]
+    for half in range(2):
+        for part in range(2):
+            to = half * 8 + 4 + part
+            here = slice((half * 2 + part) * 128, (half * 2 + part + 1) * 128)
+            blocks_ref[mine, to : to + 1, :] = gb1_ref[0:1, here]
     bias_q, bias_v = bias[:, 0:HEAD_DIM], bias[:, 2 * HEAD_DIM : 3 * HEAD_DIM]
-    lane = lax.broadcasted_iota(jnp.int32, (1, 128), 1)
-    blocks_ref[2 * chip, pl.ds(core * 8, 1), :] = jnp.where(
-        lane < 64, bias_q, pltpu.roll(bias_v, 64, 1)
-    )
-    blocks_ref[2 * chip + 1, pl.ds(core * 8, 1), :] = jnp.where(
-        lane < 64, pltpu.roll(bias_q, 64, 1), bias_v
-    )
+    both = pieces_of(bias_q, bias_v)
+    for odd in range(2):
+        blocks_ref[2 * chip + odd, pl.ds(core * 8, 1), :] = both[odd]
 
     vec_blocks = blocks([(blocks_ref, arrived)], 0)
 
@@ -1263,8 +1340,8 @@
         lax.fori_loop(0, width // SPLIT, body, 0)
 
     def flow(chunk):
-        def finish(row, first, count, total):
-            res_ref[chunk * rows + row : chunk * rows + row + 16, first : first + count] = total
+        def finish(row, columns, total):
+            res_ref[pl.ds(pl.multiple_of(chunk * rows + row, 16), 16), columns] = total
 
         incoming = (in_one.at[chunk], in_two.at[chunk], in_three.at[chunk])
         other = far_part.at[chunk % 2]
@@ -1329,6 +1406,7 @@
 
     for copy in w1_blocks + w1_far:
         copy.wait()
+    unit_rows = out_w2.shape[0]
     for at in range(GROUP):
         for part in range(2):
             here = slice(part * unit_rows, (part + 1) * unit_rows)
@@ -1348,7 +1426,7 @@
 
 
 def layer_tail(
-    qkv, dout, seg_q, seg_k, wqkv, dres, gwo, parts, x_all, gw1, w1_early, w2_own, w2_early
+    qkv, dout, wqkv, dres, gwo, vecg, gb1, lengths, x_all, gw1, w2_own, w2_early
 ):
     f32, bf16 = jnp.float32, jnp.bfloat16
     block, width = dres.shape
@@ -1360,6 +1438,7 @@
     peers = GROUP - 1
     vmem = pl.BlockSpec(memory_space=pltpu.VMEM)
     anywhere = pl.BlockSpec(memory_space=pl.ANY)
+    smem = pl.BlockSpec(memory_space=pltpu.SMEM)
     sems = pltpu.SemaphoreType.DMA
     shape, scratch = jax.ShapeDtypeStruct, pltpu.VMEM
     heads = 3 * HEAD_DIM
@@ -1379,7 +1458,7 @@
             shape((unit_rows, width), f32),
             shape((8, 128), f32),
         ],
-        in_specs=[vmem] * 8 + [anywhere] * 5,
+        in_specs=[vmem] * 7 + [smem] + [anywhere] * 4,
         out_specs=[vmem] * 8,
         scratch_shapes=[
             scratch(x_all.shape, bf16),
@@ -1402,20 +1481,22 @@
             scratch((HEAD_DIM, width), bf16),
             scratch((weight_rows, width), f32),
             scratch((weight_rows, width), f32),
-            scratch(parts.shape, f32),
-            scratch(parts.shape, f32),
+            scratch((GROUP, 16, 128), f32),
+            scratch((GROUP, 16, 128), f32),
             scratch((8, 128), f32),
             scratch((8, 128), f32),
+            pltpu.VMEM((1, own_rows + HALO), f32),
+            pltpu.VMEM((1, own_rows + HALO + 2 * PAD), f32),
             sems((1, TAIL_CHUNKS, 4, 3)), sems((1, TAIL_CHUNKS, 4, 3)),
             sems((1, TAIL_CHUNKS)), sems((1, TAIL_CHUNKS)),
-            sems((CHUNKS + 3,)), sems((3,)), sems((3, peers)), sems((3, peers)),
+            sems((CHUNKS + 2,)), sems((3,)), sems((3, peers)), sems((3, peers)),
             sems((2, GROUP)), sems((2, GROUP)), sems((5,)), sems((5,)),
         ],
         compiler_params=pltpu.CompilerParams(
             collective_id=5, has_side_effects=True, vmem_limit_bytes=63 << 20
         ),
         name="layer_tail",
-    )(qkv, dout, seg_q, seg_k, wqkv, dres, gwo, parts, x_all, gw1, w1_early, w2_own, w2_early)
+    )(qkv, dout, wqkv, dres, gwo, vecg, gb1, lengths, x_all, gw1, w2_own, w2_early)
 
 
 def grouped_device(
@@ -1439,67 +1520,22 @@
     norm2_bias,
 ):
     f32 = jnp.float32
-    bf16 = jnp.bfloat16
-    devices = lax.axis_size("dp")
-    block, width = tokens.shape
-    own_rows = GROUP * block
-    total_tokens = devices * block
-    weight_rows = wq.shape[0]
-    unit_rows, units = w2.shape[0], w1.shape[1]
-    device = lax.axis_index("dp")
-    group, member = device // GROUP, device % GROUP
-    chip, core = member // 2, member % 2
-    head = core * 8 + chip
-
-    def by_head(weight):
-        return weight.reshape(weight_rows, 2, 8, HEAD_DIM).transpose(2, 1, 0, 3).reshape(
-            GROUP, weight_rows, HEAD_DIM
-        )
-
-    pack_qkv = jnp.concatenate([by_head(wq), by_head(wk), by_head(wv)], -1)
-    pack_w1 = w1.reshape(weight_rows, 2, GROUP, unit_rows).transpose(2, 0, 1, 3).reshape(
-        GROUP, weight_rows, 2 * unit_rows
-    )
     vectors = [bq, bv, bo, norm1_gain, norm1_bias, b2, norm2_gain, norm2_bias, b1]
     sizes = [item.shape[0] for item in vectors]
-    vector = jnp.concatenate(vectors).astype(f32)
-    vector = jnp.pad(vector, (0, 1024 - vector.shape[0])).reshape(8, 128)
-
-    ext_rows = own_rows + HALO
-    ext_first = group * (own_rows - HALO)
-    offset = group * HALO
-    starts = jnp.cumsum(lengths) - lengths
-    ext_ids = ext_first + jnp.arange(ext_rows, dtype=jnp.int32)
-    seg = jnp.sum((ext_ids[:, None] >= starts[None, :]).astype(jnp.int32), 1)
-    tile_rows = jnp.arange(ext_rows // TILE, dtype=jnp.int32) * TILE - PAD
-    key_rows = tile_rows[:, None] + jnp.arange(WINDOW, dtype=jnp.int32)[None, :]
-    key_ids = ext_first + key_rows
-    seg_k = jnp.sum((key_ids[:, :, None] >= starts[None, None, :]).astype(jnp.int32), 2)
-    seg_k = jnp.where((key_rows >= 0) & (key_rows < ext_rows), seg_k, -1)[:, None, :]
-    seg_q = seg[:, None]
+    vector, at = jnp.zeros((1024,), f32), 0
+    for item, size in zip(vectors, sizes):
+        vector = vector + jnp.pad(item.astype(f32), (at, 1024 - at - size))
+        at += size
+    vector = vector.reshape(8, 128)
 
     (
-        output, grad_resid_one, vec_grads, grad_b1, w2_own, _, w2_early, grad_w1, w1_early, grad_wo,
+        output, grad_resid_one, vec_grads, grad_b1, w2_own, _, w2_early, grad_w1, grad_wo,
         all_tokens, _, qkv, grad_out, full_qkv,
-    ) = layer(tokens, cotangent, pack_qkv, pack_w1, w2, wo, vector, seg_q, seg_k)
-
-    spread_b1 = lax.dynamic_update_slice_in_dim(
-        jnp.zeros((2, GROUP, unit_rows), f32), grad_b1[0].reshape(2, 1, unit_rows), member, 1
-    )
-    grad_b2, grad_gain_two, grad_shift_two, grad_bo, grad_gain_one, grad_shift_one = [
-        vec_grads[at] for at in range(6)
-    ]
-    none = jnp.zeros((width,), f32)
-    items = [
-        none, none, grad_bo, grad_gain_one, grad_shift_one, grad_b2, grad_gain_two, grad_shift_two,
-        spread_b1,
-    ]
-    parts = jnp.concatenate([item.reshape(2, GROUP, -1) for item in items], 2)
-    parts = jnp.pad(parts, ((0, 0), (0, 0), (0, 1024 - parts.shape[2])))
-    parts = parts.transpose(1, 0, 2).reshape(GROUP, 16, 128)
+    ) = layer(tokens, cotangent, wq, wk, wv, w1, w2, wo, vector, lengths)
+
     input_grad, out_q, out_k, out_v, out_wo, out_w1, out_w2, sums = layer_tail(
-        qkv, grad_out, seg_q, seg_k, full_qkv, grad_resid_one, grad_wo, parts,
-        all_tokens, grad_w1, w1_early, w2_own, w2_early,
+        qkv, grad_out, full_qkv, grad_resid_one, grad_wo, vec_grads, grad_b1, lengths,
+        all_tokens, grad_w1, w2_own, w2_early,
     )
     sums, at = sums.reshape(-1), 0
     small = []

time: 545 us -> 527 us (0.967)
  local copies, waits for them, and re-layouts: 22.3 us -> 12.5 us
    pallas_call x1, Pallas kernels: 400 us -> 382 us  [layer(): pl.pallas_call(layer_kernel, out_shape=[shape((block, width), bf16), shap...]
    pallas_call x1, Pallas kernels: 108 us -> 120 us  [layer_tail(): pl.pallas_call(tail_kernel, out_shape=[shape((block, width), bf16), shape...]
where the time goes in v7:
time: 527 us; the launch traced here: 518 us
  Pallas kernels  503 us (95%)
  local copies, waits for them, and re-layouts  12.5 us (2%)
    pallas_call x1, Pallas kernels, layer(): pl.pallas_call(layer_kernel, out_shape=[shape((block, width), bf16), shap...  382 us
    pallas_call x1, Pallas kernels, layer_tail(): pl.pallas_call(tail_kernel, out_shape=[shape((block, width), bf16), shape...  120 us

profile of v7, /device:TPU:7, one launch (start us, length us, event | category | flops | bytes accessed | tf_op | source)
XLA Modules:
  0.0 517.8 jit_solution(7584915293152302793)
XLA Ops:
  0.7 1.5 add_bitcast_fusion.vec_ref
  2.1 382.4 %layer.1 = (bf16[128,2048]{1,0:T(8,128)(2,1)}, f32[128,2048]{1,0:T(8,128)}, f32[8,2048]{1,0:T(8,128)}, f32[8,512]{1,0:T(8,128)}, f32[256,2048]{1,0:T(8,128)}, /*...) custom-call(bf16[128,2048]{1,0:T(8,128)(2,1)} %tok_ref.1, ...), custom_call_target="tpu_custom_call" | custom-call | tf_op jit(solution)/shard_map/layer/pallas_call | solution.py:1108
  384.5 0.0 copy-start.2
  384.5 120.3 %layer_tail.1 = (bf16[128,2048]{1,0:T(8,128)(2,1)}, f32[64,2048]{1,0:T(8,128)}, f32[64,2048]{1,0:T(8,128)}, f32[64,2048]{1,0:T(8,128)}, f32[64,2048]{1,0:T(8,128...) custom-call(bf16[2688,384]{1,0:T(8,128)(2,1)} %get-tuple-element.38.qkv_ref, ...), custom_call_target="tpu_custom_call" | custom-call | tf_op jit(solution)/shard_map/layer_tail/pallas_call | solution.py:1449
  504.8 0.0 copy-start.6
  504.8 0.0 copy-start.5
  504.8 1.3 slice_bitcast_fusion
  506.2 1.6 fusion
  507.7 0.0 copy-done.2
  507.7 0.0 copy-start.4
  507.7 0.8 copy.43
  508.5 0.0 copy-start.3
  508.5 1.9 copy.44
  510.5 0.0 copy-done.6
  510.5 0.0 copy-start.1
  510.5 0.8 copy.45
  511.3 0.0 copy-done.5
  511.3 0.8 copy.46
  512.1 0.0 copy-done.4
  512.1 0.8 copy.47
  512.9 0.0 copy-done.3
  512.9 0.8 copy.48
  513.7 0.0 copy-done.1
  513.7 0.0 copy-start
  513.7 1.3 copy.49
  515.0 1.0 copy-done
  516.0 1.3 copy.50
Async XLA Ops:
  384.5 123.2 %copy-start.2 = (bf16[128,2048]{1,0:T(8,128)(2,1)S(1)}, bf16[128,2048]{1,0:T(8,128)(2,1)}, u32[]{:S(2)}) copy-start(bf16[128,2048]{1,0:T(8,128)(2,1)} %get-tuple-element.82) | copy-start | bytes 1572868
  504.8 5.7 %copy-start.6 = (f32[64,2048]{1,0:T(8,128)S(1)}, f32[64,2048]{1,0:T(8,128)}, u32[]{:S(2)}) copy-start(f32[64,2048]{1,0:T(8,128)} %get-tuple-element.84) | copy-start | bytes 1572868
  504.8 6.5 %copy-start.5 = (f32[64,2048]{1,0:T(8,128)S(1)}, f32[64,2048]{1,0:T(8,128)}, u32[]{:S(2)}) copy-start(f32[64,2048]{1,0:T(8,128)} %get-tuple-element.86) | copy-start | bytes 1572868
  507.7 4.3 copy-start.4
  508.5 4.3 copy-start.3
  510.5 3.2 copy-start.1
  513.7 2.3 copy-start

commit v8 on v7

--- a/solution.py
+++ b/solution.py
@@ -18,8 +18,6 @@
 TILE = 128
 MESH_ID = pl.DeviceIdType.MESH
 VMEM_LIMIT = 60 << 20
-PORTIONS = ((0, 48), (48, 48), (96, 32))
-ORDERS = ((0, 1, 2), (1, 2, 0), (2, 0, 1))
 
 
 norm_eps = 1e-05
@@ -441,7 +439,7 @@
     return queries, keys, weights * (1.0 / jnp.sum(weights, -1, keepdims=True))
 
 
-CHUNKS = 4
+CHUNKS = 2
 TAIL_CHUNKS = 2
 THIRDS = (((0, 768), (0, 1, 2)), ((768, 640), (1, 2, 0)), ((1408, 640), (2, 0, 1)))
 LIGHT = (

time: 527 us -> 516 us (0.979); the launches traced: 518 us -> 515 us
  no operation moved by 1% of the time
where the time goes in v8:
time: 516 us; the launch traced here: 515 us
  Pallas kernels  501 us (97%)
  local copies, waits for them, and re-layouts  12.5 us (2%)
    pallas_call x1, Pallas kernels, layer(): pl.pallas_call(layer_kernel, out_shape=[shape((block, width), bf16), shap...  380 us
    pallas_call x1, Pallas kernels, layer_tail(): pl.pallas_call(tail_kernel, out_shape=[shape((block, width), bf16), shape...  120 us

profile of v8, /device:TPU:7, one launch (start us, length us, event | category | flops | bytes accessed | tf_op | source)
XLA Modules:
  0.0 515.4 jit_solution(7913718542018074697)
XLA Ops:
  0.7 1.5 add_bitcast_fusion.vec_ref
  2.1 380.5 %layer.1 = (bf16[128,2048]{1,0:T(8,128)(2,1)}, f32[128,2048]{1,0:T(8,128)}, f32[8,2048]{1,0:T(8,128)}, f32[8,512]{1,0:T(8,128)}, f32[256,2048]{1,0:T(8,128)}, /*...) custom-call(bf16[128,2048]{1,0:T(8,128)(2,1)} %tok_ref.1, ...), custom_call_target="tpu_custom_call" | custom-call | tf_op jit(solution)/shard_map/layer/pallas_call | solution.py:1106
  382.6 0.0 copy-start.2
  382.6 120.3 %layer_tail.1 = (bf16[128,2048]{1,0:T(8,128)(2,1)}, f32[64,2048]{1,0:T(8,128)}, f32[64,2048]{1,0:T(8,128)}, f32[64,2048]{1,0:T(8,128)}, f32[64,2048]{1,0:T(8,128...) custom-call(bf16[2688,384]{1,0:T(8,128)(2,1)} %get-tuple-element.38.qkv_ref, ...), custom_call_target="tpu_custom_call" | custom-call | tf_op jit(solution)/shard_map/layer_tail/pallas_call | solution.py:1447
  502.9 0.0 copy-start.6
  502.9 0.0 copy-start.5
  502.9 1.3 slice_bitcast_fusion
  504.2 1.6 fusion
  505.8 0.0 copy-done.2
  505.8 0.0 copy-start.4
  505.8 0.8 copy.43
  506.6 0.0 copy-start.3
  506.6 1.9 copy.44
  508.6 0.0 copy-done.6
  508.6 0.0 copy-start.1
  508.6 0.8 copy.45
  509.4 0.0 copy-done.5
  509.4 0.8 copy.46
  510.1 0.0 copy-done.4
  510.1 0.8 copy.47
  510.9 0.0 copy-done.3
  510.9 0.8 copy.48
  511.7 0.0 copy-done.1
  511.7 0.0 copy-start
  511.7 1.3 copy.49
  513.1 1.0 copy-done
  514.1 1.3 copy.50
Async XLA Ops:
  382.6 123.2 %copy-start.2 = (bf16[128,2048]{1,0:T(8,128)(2,1)S(1)}, bf16[128,2048]{1,0:T(8,128)(2,1)}, u32[]{:S(2)}) copy-start(bf16[128,2048]{1,0:T(8,128)(2,1)} %get-tuple-element.82) | copy-start | bytes 1572868
  502.9 5.7 %copy-start.6 = (f32[64,2048]{1,0:T(8,128)S(1)}, f32[64,2048]{1,0:T(8,128)}, u32[]{:S(2)}) copy-start(f32[64,2048]{1,0:T(8,128)} %get-tuple-element.84) | copy-start | bytes 1572868
  502.9 6.5 %copy-start.5 = (f32[64,2048]{1,0:T(8,128)S(1)}, f32[64,2048]{1,0:T(8,128)}, u32[]{:S(2)}) copy-start(f32[64,2048]{1,0:T(8,128)} %get-tuple-element.86) | copy-start | bytes 1572868
  505.8 4.3 copy-start.4
  506.6 4.3 copy-start.3
  508.6 3.2 copy-start.1
  511.7 2.3 copy-start

commit v9 on v8

--- a/solution.py
+++ b/solution.py
@@ -542,8 +542,8 @@
                     ]
 
                     def add(index, carry, step=step, where=where, lefts=lefts, columns=columns):
-                        row = pl.multiple_of(index * 16, 16)
-                        at = (pl.ds(row, 16), columns)
+                        row = pl.multiple_of(index * 32, 32)
+                        at = (pl.ds(row, 32), columns)
                         total = own[where + at].astype(f32) + pair_in[where + at].astype(f32)
                         for back in range(step):
                             total = total + incoming[back][lefts[back] + at].astype(f32)
@@ -553,7 +553,7 @@
                             finish(row, columns, total)
                         return carry
 
-                    lax.fori_loop(0, rows // 16, add, 0)
+                    lax.fori_loop(0, rows // 32, add, 0)
                 if step == 3:
                     continue
                 for dim in free:
@@ -882,7 +882,7 @@
 
     def keep(chunk):
         def finish(row, columns, total):
-            res_ref[pl.ds(pl.multiple_of(chunk * rows + row, 16), 16), columns] = total
+            res_ref[pl.ds(pl.multiple_of(chunk * rows + row, 32), 32), columns] = total
 
         return finish
 
@@ -1215,6 +1215,8 @@
     w1_far = far_blocks(
         gw1_ref.at[first], w1_there, there_send.at[0], there_recv.at[0], group, mine
     )
+    own_first = pl.ds(pl.multiple_of(group * GROUP, GROUP), GROUP)
+    w1_blocks = blocks([(gw1_ref.at[own_first], w1_here)], 1)
     x_loads = [load(x_all.at[at], xs_ref.at[at], at) for at in range(CHUNKS)]
     loads = [
         load(w2_own, w2_sum, CHUNKS),
@@ -1339,7 +1341,7 @@
 
     def flow(chunk):
         def finish(row, columns, total):
-            res_ref[pl.ds(pl.multiple_of(chunk * rows + row, 16), 16), columns] = total
+            res_ref[pl.ds(pl.multiple_of(chunk * rows + row, 32), 32), columns] = total
 
         incoming = (in_one.at[chunk], in_two.at[chunk], in_three.at[chunk])
         other = far_part.at[chunk % 2]
@@ -1387,8 +1389,6 @@
         wo_pair[...] = jnp.where(core == 0, second, first)
         share_wo.start()
 
-    own_first = pl.ds(pl.multiple_of(group * GROUP, GROUP), GROUP)
-    w1_blocks = blocks([(gw1_ref.at[own_first], w1_here)], 1)
     state["vec"].wait()
     vec_ref[...] += far_vec_in[...]
 

time: 516 us -> 507 us (0.983)
  Pallas kernels: 501 us -> 492 us
    pallas_call x1, Pallas kernels: 120 us -> 112 us  [layer_tail(): pl.pallas_call(tail_kernel, out_shape=[shape((block, width), bf16), shape...]
where the time goes in v9:
time: 507 us; the launch traced here: 506 us
  Pallas kernels  492 us (97%)
  local copies, waits for them, and re-layouts  12.5 us (2%)
    pallas_call x1, Pallas kernels, layer(): pl.pallas_call(layer_kernel, out_shape=[shape((block, width), bf16), shap...  380 us
    pallas_call x1, Pallas kernels, layer_tail(): pl.pallas_call(tail_kernel, out_shape=[shape((block, width), bf16), shape...  112 us

profile of v9, /device:TPU:7, one launch (start us, length us, event | category | flops | bytes accessed | tf_op | source)
XLA Modules:
  0.0 506.5 jit_solution(15189917612424323498)
XLA Ops:
  0.7 1.5 add_bitcast_fusion.vec_ref
  2.1 380.2 %layer.1 = (bf16[128,2048]{1,0:T(8,128)(2,1)}, f32[128,2048]{1,0:T(8,128)}, f32[8,2048]{1,0:T(8,128)}, f32[8,512]{1,0:T(8,128)}, f32[256,2048]{1,0:T(8,128)}, /*...) custom-call(bf16[128,2048]{1,0:T(8,128)(2,1)} %tok_ref.1, ...), custom_call_target="tpu_custom_call" | custom-call | tf_op jit(solution)/shard_map/layer/pallas_call | solution.py:1106
  382.4 0.0 copy-start.2
  382.4 111.6 %layer_tail.1 = (bf16[128,2048]{1,0:T(8,128)(2,1)}, f32[64,2048]{1,0:T(8,128)}, f32[64,2048]{1,0:T(8,128)}, f32[64,2048]{1,0:T(8,128)}, f32[64,2048]{1,0:T(8,128...) custom-call(bf16[2688,384]{1,0:T(8,128)(2,1)} %get-tuple-element.38.qkv_ref, ...), custom_call_target="tpu_custom_call" | custom-call | tf_op jit(solution)/shard_map/layer_tail/pallas_call | solution.py:1447
  494.0 0.0 copy-start.6
  494.0 0.0 copy-start.5
  494.0 1.3 slice_bitcast_fusion
  495.3 1.6 fusion
  496.9 0.0 copy-done.2
  496.9 0.0 copy-start.4
  496.9 0.8 copy.43
  497.7 0.0 copy-start.3
  497.7 1.9 copy.44
  499.6 0.0 copy-done.6
  499.6 0.0 copy-start.1
  499.6 0.8 copy.45
  500.4 0.0 copy-done.5
  500.4 0.8 copy.46
  501.2 0.0 copy-done.4
  501.2 0.8 copy.47
  502.0 0.0 copy-done.3
  502.0 0.8 copy.48
  502.8 0.0 copy-done.1
  502.8 0.0 copy-start
  502.8 1.3 copy.49
  504.2 1.0 copy-done
  505.2 1.3 copy.50
Async XLA Ops:
  382.4 114.5 %copy-start.2 = (bf16[128,2048]{1,0:T(8,128)(2,1)S(1)}, bf16[128,2048]{1,0:T(8,128)(2,1)}, u32[]{:S(2)}) copy-start(bf16[128,2048]{1,0:T(8,128)(2,1)} %get-tuple-element.82) | copy-start | bytes 1572868
  494.0 5.7 %copy-start.6 = (f32[64,2048]{1,0:T(8,128)S(1)}, f32[64,2048]{1,0:T(8,128)}, u32[]{:S(2)}) copy-start(f32[64,2048]{1,0:T(8,128)} %get-tuple-element.84) | copy-start | bytes 1572868
  494.0 6.5 %copy-start.5 = (f32[64,2048]{1,0:T(8,128)S(1)}, f32[64,2048]{1,0:T(8,128)}, u32[]{:S(2)}) copy-start(f32[64,2048]{1,0:T(8,128)} %get-tuple-element.86) | copy-start | bytes 1572868
  496.9 4.3 copy-start.4
  497.7 4.3 copy-start.3
  499.6 3.2 copy-start.1
  502.8 2.3 copy-start
